TPU v7x, 32 devices: a whole 2x2x4 slice. The times are simulated.
32 devices in a mesh: grp: 2 (over y), patch: 4 (over z), lead: 4 (over x, core).
Axes of the slice: x: 2, y: 2, z: 4, core: 2. Of those that a mesh axis runs over, the one named last changes fastest.
Arguments:
- features: bfloat16 [8, 4, 128, 32, 128], P(('grp', 'lead'), 'patch'), parts along dimension 0, may hold values from -6 to 6
- context: bfloat16 [4, 8, 128, 2048], P('patch', ('grp', 'lead')), parts along dimension 1, may hold values from -6 to 6
- owner: int32 [8], P('grp'), parts along dimension 0, may hold values from 0 to 3, as said below
- hours: int32 [8], P('grp'), parts along dimension 0, may hold values from 0 to 18, as said below
- w_first: bfloat16 [9, 192, 128], replicated, may hold values from -0.15625 to 0.15625
- w_second: bfloat16 [9, 128, 128], replicated, may hold values from -0.1875 to 0.1875
- w_lead_in: bfloat16 [128, 32], replicated, may hold values from -0.5 to 0.5
- w_lead_mix: bfloat16 [3, 32, 32], replicated, may hold values from -0.625 to 0.625
- w_lead_out: bfloat16 [32, 128], replicated, may hold values from -1 to 1
Outputs:
- updated: bfloat16 [8, 4, 128, 32, 128], P(('grp', 'lead'), 'patch'), parts along dimension 0
There are 2 independent parts, one for each index of `grp`. A program takes and returns all parts, laid end to end along the dimension named above; an argument that names none is the same for every part. Nothing has to cross between parts.
Inputs may be any that keep to these rules, and one draw needn't show every extreme that they name: `owner`: values are patch indices; some lead hour is owned by patch 0 and some by patch 4 - 1. `hours`: strictly increasing along the lead hours; consecutive differences run from 1 to 6, both reached; the last lead hour is the largest value.
All inputs are finite; a program needn't handle non-finite values.
Results may differ from a plain program's by a relative error of at most 0.0037.
Values may be sent and summed in bfloat16 or wider, within the bound.
No kernel may reach another device: no remote copies, remote signals or barrier semaphores. Data moves between devices by JAX's collectives and lax.ppermute only.
A program may use at most 64 MiB of HBM per device.

v0:
```python
import jax
import jax.numpy as jnp
from jax import lax
from jax.sharding import PartitionSpec as P


def passed_along(block, axis, distance):
    devices = range(lax.axis_size(axis))
    route = [(i - distance, i) for i in devices if i - distance in devices]
    return lax.ppermute(block, axis, route)


def broadcast(block, axis, holder):
    block = jnp.where(lax.axis_index(axis) == holder, block, jnp.zeros_like(block))
    return lax.psum(block, axis)


def conv_padded(padded, kernel, height, width):
    depth = padded.shape[2]
    total = jnp.zeros((height * width, kernel.shape[2]), jnp.float32)
    for tap_index in range(9):
        row_off, col_off = divmod(tap_index, 3)
        window = padded[row_off : row_off + height, col_off : col_off + width].reshape(
            height * width, depth
        )
        total = total + jnp.dot(window, kernel[tap_index], preferred_element_type=jnp.float32)
    return total


def conv3x3(field, kernel):
    height, width = (field.shape[0], field.shape[1])
    padded = jnp.pad(field, ((1, 1), (1, 1), (0, 0)))
    return conv_padded(padded, kernel, height, width)


def per_device(
    features, context, owner, hours, w_first, w_second, w_lead_in, w_lead_mix, w_lead_out
):
    row_count, col_count, channels = (features.shape[2], features.shape[3], features.shape[4])
    temporal = w_lead_in.shape[1]
    lead_count = hours.shape[0]
    lead_index = lax.axis_index("lead")
    owner_index = owner[lead_index]
    resident = features[0, 0]
    lead_proj = jnp.dot(
        resident.reshape(-1, channels), w_lead_in, preferred_element_type=jnp.float32
    ).astype(jnp.bfloat16)
    proj_rows = lead_proj.reshape(row_count, col_count * temporal)
    preceding = passed_along(proj_rows, "lead", 1)
    following = passed_along(proj_rows, "lead", -1)
    context_full = broadcast(context[0, 0], "patch", owner_index)
    context_full = context_full.reshape(row_count, col_count, -1)
    joined = jnp.concatenate([resident, context_full], axis=-1)
    first_pre = conv3x3(joined, w_first)
    first_act = jax.nn.silu(first_pre).astype(jnp.bfloat16).reshape(row_count, col_count, -1)
    second_pre = conv3x3(first_act, w_second)
    hour_float = hours.astype(jnp.float32)
    hour_now = hour_float[lead_index]
    hour_prev = hour_float[jnp.maximum(lead_index - 1, 0)]
    hour_next = hour_float[jnp.minimum(lead_index + 1, lead_count - 1)]
    gain_prev = jnp.where(lead_index > 0, jnp.exp(-0.5 * (hour_now - hour_prev - 1.0)), 0.0)
    gain_next = jnp.where(
        lead_index < lead_count - 1, jnp.exp(-0.5 * (hour_next - hour_now - 1.0)), 0.0
    )
    mixed = gain_prev * jnp.dot(
        preceding.reshape(-1, temporal), w_lead_mix[0], preferred_element_type=jnp.float32
    )
    mixed = mixed + jnp.dot(lead_proj, w_lead_mix[1], preferred_element_type=jnp.float32)
    mixed = mixed + gain_next * jnp.dot(
        following.reshape(-1, temporal), w_lead_mix[2], preferred_element_type=jnp.float32
    )
    mixed = mixed.astype(jnp.bfloat16)
    lifted = jnp.dot(mixed, w_lead_out, preferred_element_type=jnp.float32)
    result = resident.reshape(-1, channels).astype(jnp.float32) + jax.nn.silu(second_pre + lifted)
    return result.astype(jnp.bfloat16).reshape(1, 1, row_count, col_count, channels)


def solution(mesh):
    placed = (
        P(("grp", "lead"), "patch", None, None, None),
        P("patch", ("grp", "lead"), None, None),
        P("grp"),
        P("grp"),
        P(),
        P(),
        P(),
        P(),
        P(),
    )
    return jax.shard_map(
        per_device,
        mesh=mesh,
        in_specs=placed,
        out_specs=P(("grp", "lead"), "patch", None, None, None),
        check_vma=False,
    )
```

profile of v0, /device:TPU:0, one launch (start us, length us, event | category | flops | bytes accessed | tf_op | source)
XLA Modules:
  0.0 107.9 jit_solution(15575565231238159172)
XLA Ops:
  6.5 1.7 %convolution_convert_fusion = bf16[4096,32]{0,1:T(8,128)(2,1)S(1)} fusion(bf16[4096,128]{1,0:T(8,128)(2,1)} %bitcast.114, bf16[128,32]{0,1:T(8,128)(2,1)} %param.15), kind=kOutput, calls=%fused_computation.29 | convolution fusion | flops 33685504 | bytes 1318912 | tf_op jit(solution)/shard_map/dot_general | solution.py:45
  8.8 1.1 %reshape.106 = bf16[128,1024]{1,0:T(8,128)(2,1)S(1)} reshape(bf16[4096,32]{1,0:T(8,128)(2,1)S(1)} %copy.17) | data formatting | bytes 524288 | tf_op jit(solution)/shard_map/reshape | solution.py:48
  10.0 2.4 %collective-permute-start = (bf16[128,1024]{1,0:T(8,128)(2,1)S(1)}, bf16[128,1024]{1,0:T(8,128)(2,1)S(1)}, u32[]{:S(2)}, u32[]{:S(2)}) collective-permute-start(bf16[128,1024]{1,0:T(8,128)(2,1)S(1)} %reshape.106), channel_id=1, source_target_pairs={{0,1},{1,2},{2,3},{4,5},{5,6},{6,7},{8,9},{9,10},{10,11},{12,13},{... | collective-permute-start | bytes 786440 | tf_op jit(solution)/shard_map/ppermute | solution.py:10
  12.3 1.3 %collective-permute-start.1 = (bf16[128,1024]{1,0:T(8,128)(2,1)S(1)}, bf16[128,1024]{1,0:T(8,128)(2,1)S(1)}, u32[]{:S(2)}, u32[]{:S(2)}) collective-permute-start(bf16[128,1024]{1,0:T(8,128)(2,1)S(1)} %reshape.106), channel_id=1, source_target_pairs={{1,0},{2,1},{3,2},{5,4},{6,5},{7,6},{9,8},{10,9},{11,10},{13,12},{... | collective-permute-start | bytes 786440 | tf_op jit(solution)/shard_map/ppermute | solution.py:10
  15.2 0.8 select_bitcast_fusion
  19.6 0.8 reshape.107
  20.4 1.8 %reshape.108 = bf16[4096,32]{1,0:T(8,128)(2,1)} reshape(bf16[128,1024]{1,0:T(8,128)(2,1)S(1)} %collective-permute-done.1) | data formatting | bytes 524288 | tf_op jit(solution)/shard_map/reshape | solution.py:70
  22.2 1.3 %fusion.4 = f32[4096,32]{0,1:T(8,128)} fusion(f32[4096,32]{0,1:T(8,128)S(1)} %fusion.55, bf16[4096,32]{1,0:T(8,128)(2,1)S(1)} %reshape.107, f32[]{:T(128)S(6)} %select_n.30, bf16[3,32,32]{2,1,0:T(8,128)(2,1)S(1)} %copy-done.13), kind=kOutput, calls=%fused_computation.27 | convolution fusion | flops 8650752 | bytes 2105348 | tf_op jit(solution)/shard_map/dot_general | solution.py:65
  23.5 35.6 %all-reduce.4.cloned.1.call-done = bf16[128,2048]{0,1:T(8,128)(2,1)} async-done(((bf16[128,2048]{0,1:T(8,128)(2,1)}), bf16[128,2048]{0,1:T(8,128)(2,1)}) %all-reduce.4.cloned.1.call-update) | async-done | bytes 524304 | tf_op jit(solution)/shard_map/psum | solution.py:15
  59.1 2.5 %copy.15 = bf16[128,32,64]{2,1,0:T(8,128)(2,1)S(1)} copy(bf16[128,32,64]{0,2,1:T(8,128)(2,1)} %bitcast.134) | data formatting | bytes 1048576 | tf_op jit(solution)/shard_map/reshape | solution.py:52
  61.5 3.0 %fusion.9 = bf16[130,34,192]{2,1,0:T(8,128)(2,1)S(1)} fusion(bf16[128,32,64]{2,1,0:T(8,128)(2,1)S(1)} %copy.15, bf16[128,32,128]{2,1,0:T(8,128)(2,1)S(1)} %bitcast.115), kind=kLoop, calls=%fused_computation.33 | loop fusion | flops 12729600 | bytes 3270144 | tf_op jit(solution)/shard_map/concatenate | solution.py:53
  64.6 8.0 %fusion.63 = (bf16[128,32,192]{2,1,0:T(8,128)(2,1)}, bf16[128,32,192]{2,1,0:T(8,128)(2,1)}, bf16[128,32,192]{2,1,0:T(8,128)(2,1)}, bf16[128,32,192]{2,1,0:T(8,12...) fusion(bf16[130,34,192]{2,1,0:T(8,128)(2,1)S(1)} %fusion.9), kind=kLoop, calls=%fused_computation.96 | loop fusion | bytes 25165824 | tf_op jit(solution)/shard_map/slice | solution.py:23
  72.6 2.1 %copy.16 = bf16[128,2048]{1,0:T(8,128)(2,1)} copy(bf16[128,2048]{0,1:T(8,128)(2,1)} %all-reduce.4.cloned.1.call-done) | data formatting | bytes 1048576 | tf_op jit(solution)/shard_map/psum | solution.py:15
  74.6 2.8 %concatenate.9 = bf16[4096,64]{1,0:T(8,128)(2,1)} reshape(bf16[128,2048]{1,0:T(8,128)(2,1)} %copy.16) | data formatting | bytes 1048576 | tf_op jit(solution)/shard_map/concatenate | solution.py:53
  77.4 1.6 %fusion.23 = f32[4096,128]{1,0:T(8,128)S(1)} fusion(bf16[4096,192]{1,0:T(8,128)(2,1)S(1)} %bitcast.113, bf16[9,192,128]{2,1,0:T(8,128)(2,1)} %param.13), kind=kOutput, calls=%fused_computation.58 | convolution fusion | flops 201326592 | bytes 3719168 | tf_op jit(solution)/shard_map/dot_general | solution.py:26
  79.8 0.9 copy-done.6
  81.4 0.9 copy-done.5
  84.2 0.9 copy-done.4
  85.8 0.9 copy-done.3
  87.4 0.9 copy-done.2
  88.9 0.9 copy-done.9
  89.8 0.7 multiply_convert_fusion
  90.6 3.2 %pad_slice_fusion = (bf16[128,32,128]{2,1,0:T(8,128)(2,1)S(1)}, bf16[128,32,128]{2,1,0:T(8,128)(2,1)S(1)}, bf16[128,32,128]{2,1,0:T(8,128)(2,1)S(1)}, bf16[128,3...) fusion(bf16[128,32,128]{2,1,0:T(8,128)(2,1)S(1)} %bitcast.125), kind=kLoop, calls=%fused_computation.40 | loop fusion | bytes 9437184 | tf_op jit(solution)/shard_map/slice | solution.py:23
  97.5 3.5 %add_convert_fusion = bf16[4096,128]{1,0:T(8,128)(2,1)} fusion(f32[4096,128]{1,0:T(8,128)S(1)} %convolution_add_fusion.1, bf16[32,128]{1,0:T(8,128)(2,1)S(1)} %copy-done, bf16[4096,128]{1,0:T(8,128)(2,1)S(1)} %bitcast.117, f32[4096,32]{0,1:T(8,128)} %fusion.4, bf16[4096,32]{1,0:T(8,128)(2,1)} %reshape.108, f32[]{:T(128)S(6)} %select_n.32, ...), kind=kOutput, calls=%fused_computation.38 | convolution fusion | flops 46530560 | bytes 4997124 | tf_op jit(solution)/shard_map/dot_general | solution.py:73
  (52 shorter events, 11.4 us)
Async XLA Ops:
  6.5 91.0 %copy-start = (bf16[32,128]{1,0:T(8,128)(2,1)S(1)}, bf16[32,128]{1,0:T(8,128)(2,1)}, u32[]{:S(2)}) copy-start(bf16[32,128]{1,0:T(8,128)(2,1)} %param.17) | copy-start | bytes 24580
  6.5 7.1 %copy-start.10 = (bf16[1,1,128,2048]{3,2,1,0:T(8,128)(2,1)S(1)}, bf16[1,1,128,2048]{3,2,1,0:T(8,128)(2,1)}, u32[]{:S(2)}) copy-start(bf16[1,1,128,2048]{3,2,1,0:T(8,128)(2,1)} %param.10) | copy-start | bytes 1572868
  6.5 52.5 %all-reduce.4.cloned.1.call-start = ((), (), s32[]{:S(2)}) async-start(), calls=%async_computation | async-start | bytes 1048576 | tf_op jit(solution)/shard_map/psum | solution.py:15
  8.3 5.7 %copy-start.14 = (s32[4]{0:T(128)S(1)}, s32[4]{0:T(128)}, u32[]{:S(2)}) copy-start(s32[4]{0:T(128)} %param.11) | copy-start | bytes 52
  8.8 7.3 %copy-start.15 = (s32[4]{0:T(128)S(1)}, s32[4]{0:T(128)}, u32[]{:S(2)}) copy-start(s32[4]{0:T(128)} %param.12) | copy-start | bytes 52
  8.8 10.6 %copy-start.13 = (bf16[3,32,32]{2,1,0:T(8,128)(2,1)S(1)}, bf16[3,32,32]{2,1,0:T(8,128)(2,1)}, u32[]{:S(2)}) copy-start(bf16[3,32,32]{2,1,0:T(8,128)(2,1)} %param.16) | copy-start | bytes 18436
  10.0 9.7 %collective-permute-start = (bf16[128,1024]{1,0:T(8,128)(2,1)S(1)}, bf16[128,1024]{1,0:T(8,128)(2,1)S(1)}, u32[]{:S(2)}, u32[]{:S(2)}) collective-permute-start(bf16[128,1024]{1,0:T(8,128)(2,1)S(1)} %reshape.106), channel_id=1, source_target_pairs={{0,1},{1,2},{2,3},{4,5},{5,6},{6,7},{8,9},{9,10},{10,11},{12,13},{... | collective-permute-start | bytes 786440 | tf_op jit(solution)/shard_map/ppermute | solution.py:10
  12.3 8.1 %collective-permute-start.1 = (bf16[128,1024]{1,0:T(8,128)(2,1)S(1)}, bf16[128,1024]{1,0:T(8,128)(2,1)S(1)}, u32[]{:S(2)}, u32[]{:S(2)}) collective-permute-start(bf16[128,1024]{1,0:T(8,128)(2,1)S(1)} %reshape.106), channel_id=1, source_target_pairs={{1,0},{2,1},{3,2},{5,4},{6,5},{7,6},{9,8},{10,9},{11,10},{13,12},{... | collective-permute-start | bytes 786440 | tf_op jit(solution)/shard_map/ppermute | solution.py:10
  22.2 39.4 %copy-start.1 = (bf16[1,1,128,32,128]{4,3,2,1,0:T(8,128)(2,1)S(1)}, bf16[1,1,128,32,128]{4,3,2,1,0:T(8,128)(2,1)}, u32[]{:S(2)}) copy-start(bf16[1,1,128,32,128]{4,3,2,1,0:T(8,128)(2,1)} %param.9) | copy-start | bytes 3145732
  77.4 1.7 %copy-start.7 = (bf16[128,32,192]{2,1,0:T(8,128)(2,1)S(1)}, bf16[128,32,192]{2,1,0:T(8,128)(2,1)}, u32[]{:S(2)}) copy-start(bf16[128,32,192]{2,1,0:T(8,128)(2,1)} %get-tuple-element.11) | copy-start | bytes 4718596
  77.4 1.7 %copy-start.11 = (bf16[9,192,128]{2,1,0:T(8,128)(2,1)S(1)}, bf16[9,192,128]{2,1,0:T(8,128)(2,1)}, u32[]{:S(2)}) copy-start(bf16[9,192,128]{2,1,0:T(8,128)(2,1)} %param.13) | copy-start | bytes 1327108
  79.1 1.6 %copy-start.6 = (bf16[128,32,192]{2,1,0:T(8,128)(2,1)S(1)}, bf16[128,32,192]{2,1,0:T(8,128)(2,1)}, u32[]{:S(2)}) copy-start(bf16[128,32,192]{2,1,0:T(8,128)(2,1)} %get-tuple-element.10) | copy-start | bytes 4718596
  80.7 1.6 %copy-start.5 = (bf16[128,32,192]{2,1,0:T(8,128)(2,1)S(1)}, bf16[128,32,192]{2,1,0:T(8,128)(2,1)}, u32[]{:S(2)}) copy-start(bf16[128,32,192]{2,1,0:T(8,128)(2,1)} %get-tuple-element.9) | copy-start | bytes 4718596
  82.2 1.2 %copy-start.8 = (bf16[4096,64]{1,0:T(8,128)(2,1)S(1)}, bf16[4096,64]{1,0:T(8,128)(2,1)}, u32[]{:S(2)}) copy-start(bf16[4096,64]{1,0:T(8,128)(2,1)} %concatenate.9) | copy-start | bytes 1572868
  83.5 1.6 %copy-start.4 = (bf16[128,32,192]{2,1,0:T(8,128)(2,1)S(1)}, bf16[128,32,192]{2,1,0:T(8,128)(2,1)}, u32[]{:S(2)}) copy-start(bf16[128,32,192]{2,1,0:T(8,128)(2,1)} %get-tuple-element.8) | copy-start | bytes 4718596
  85.1 1.6 %copy-start.3 = (bf16[128,32,192]{2,1,0:T(8,128)(2,1)S(1)}, bf16[128,32,192]{2,1,0:T(8,128)(2,1)}, u32[]{:S(2)}) copy-start(bf16[128,32,192]{2,1,0:T(8,128)(2,1)} %get-tuple-element.7) | copy-start | bytes 4718596
  86.7 1.6 %copy-start.2 = (bf16[128,32,192]{2,1,0:T(8,128)(2,1)S(1)}, bf16[128,32,192]{2,1,0:T(8,128)(2,1)}, u32[]{:S(2)}) copy-start(bf16[128,32,192]{2,1,0:T(8,128)(2,1)} %get-tuple-element.6) | copy-start | bytes 4718596
  88.2 1.6 %copy-start.9 = (bf16[128,32,192]{2,1,0:T(8,128)(2,1)S(1)}, bf16[128,32,192]{2,1,0:T(8,128)(2,1)}, u32[]{:S(2)}) copy-start(bf16[128,32,192]{2,1,0:T(8,128)(2,1)} %get-tuple-element.5) | copy-start | bytes 4718596
  90.6 3.2 %copy-start.12 = (bf16[9,128,128]{2,1,0:T(8,128)(2,1)S(1)}, bf16[9,128,128]{2,1,0:T(8,128)(2,1)}, u32[]{:S(2)}) copy-start(bf16[9,128,128]{2,1,0:T(8,128)(2,1)} %param.14) | copy-start | bytes 884740
Sparse Core Ops, SparseCore 0:
  16.2 42.8 all-reduce.3
where the time goes:
time: 109 us; the launch traced here: 108 us
  waiting for transfers between devices  35.6 us (33%)
  local copies, waits for them, and re-layouts  30.1 us (28%)
  matrix products  17.7 us (16%)
  between operations  17 us (16%)
  other arithmetic  3.88 us (4%)
  starting transfers between devices  3.67 us (3%)
    psum x1, waiting for transfers between devices, broadcast(): return lax.psum(block, axis)  35.6 us
    slice x2, local copies, waits for them, and re-layouts, conv_padded(): padded[row_off:row_off + height, col_off:col_off + width]  11.1 us
    dot_general x18, matrix products, conv_padded(): jnp.dot(window, kernel[tap_index], preferred_element_type=jnp.float32)  10.9 us
    unnamed x33, local copies, waits for them, and re-layouts  6.23 us
    ppermute x2, starting transfers between devices, passed_along(): return lax.ppermute(block, axis, route)  3.67 us
    dot_general x1, matrix products, per_device(): lifted = jnp.dot(mixed, w_lead_out, preferred_element_type=jnp.float32)  3.53 us
    concatenate x1, other arithmetic, per_device(): joined = jnp.concatenate([resident, context_full], axis=-1)  3.04 us
    concatenate x1, local copies, waits for them, and re-layouts, per_device(): joined = jnp.concatenate([resident, context_full], axis=-1)  2.78 us
  transfers between devices with their start and end apart: 3, of which 1 were waited for; matrix products, arithmetic and copies ran while one was open for 6% of the time, Pallas kernels for 0%

commit v1 on v0

v1 whole, which is shorter than its diff:
```python
import jax
import jax.numpy as jnp
from jax import lax
from jax.experimental import pallas as pl
from jax.experimental.pallas import tpu as pltpu
from jax.sharding import PartitionSpec as P

BF16 = jnp.bfloat16
F32 = jnp.float32
EDGE = 8
CHUNK = 256
VMEM_BYTES = 40 * 1024 * 1024


def silu(v):
    return 0.5 * v * (1.0 + jnp.tanh(0.5 * v))


def dot(a, b):
    return jnp.dot(a, b, preferred_element_type=F32)


def in_vmem(count):
    return [pl.BlockSpec(memory_space=pltpu.VMEM)] * count


def put_pair_weights(target, weights, first, depth, offsets):
    out = weights.shape[2]
    span = depth * len(offsets)
    for a in range(3):
        for place, d in enumerate(offsets):
            rows = pl.ds(a * span + place * depth, depth)
            for q in range(2):
                b = d - q + 1
                lanes = pl.ds(q * out, out)
                if 0 <= b <= 2:
                    target[rows, lanes] = weights[3 * a + b, pl.ds(first, depth), :]
                else:
                    target[rows, lanes] = jnp.zeros((depth, out), target.dtype)


def clear_edges(ref, pairs):
    zero = jnp.zeros((pairs, ref.shape[1]), ref.dtype)
    ref[pl.ds(0, pairs), :] = zero
    ref[pl.ds(ref.shape[0] - pairs, pairs), :] = zero


def pair_taps(taps, weights, start, size, pairs):
    depth = taps.shape[1]
    total = dot(taps[pl.ds(start, size), :], weights[pl.ds(0, depth), :])
    for a in range(1, 3):
        total += dot(
            taps[pl.ds(start + a * pairs, size), :], weights[pl.ds(a * depth, depth), :]
        )
    return total


def column_masks(size, lanes, pairs):
    m = lax.broadcasted_iota(jnp.int32, (size, lanes), 0) & (pairs - 1)
    return m == 0, m == pairs - 1


def resident_kernel(
    x_ref, first_ref, second_ref, in_ref, acc_ref, proj_ref, w_second_ref, w_glob_ref,
    cells, taps, w_first, w_in,
):
    height, width, channels = x_ref.shape
    pairs = width // 2
    rows = height * pairs
    temporal = in_ref.shape[1]
    glob = first_ref.shape[1] - channels
    put_pair_weights(w_first, first_ref, 0, channels, (-1, 0, 1, 2))
    put_pair_weights(w_second_ref, second_ref, 0, channels, (-1, 0, 1, 2))
    put_pair_weights(w_glob_ref, first_ref, channels, glob, (0, 1, 2, -1))
    w_in[...] = jnp.zeros_like(w_in)
    for s in range(4):
        w_in[pl.ds(s * channels, channels), pl.ds(s * temporal, temporal)] = in_ref[...]
    clear_edges(taps, pairs)
    left, right = column_masks(CHUNK, channels, pairs)
    for start in range(0, rows, CHUNK):
        part = x_ref[pl.ds(start // pairs, CHUNK // pairs), :, :].astype(F32)
        cells[pl.ds(EDGE + 2 * start, 2 * CHUNK), :] = part.reshape(2 * CHUNK, channels)
    for start in range(0, rows, CHUNK):
        for place, d in enumerate((-1, 0, 1, 2)):
            value = cells[pl.ds(EDGE + 2 * start + d, CHUNK, stride=2), :]
            if d == -1:
                value = jnp.where(left, 0.0, value)
            if d == 2:
                value = jnp.where(right, 0.0, value)
            taps[pl.ds(pairs + start, CHUNK), pl.ds(place * channels, channels)] = value.astype(BF16)
    half = rows // 2
    for start in range(0, half, CHUNK):
        value = dot(
            taps[pl.ds(pairs + start, CHUNK), pl.ds(channels, 2 * channels)],
            w_in[pl.ds(0, 2 * channels), :],
        ) + dot(
            taps[pl.ds(pairs + half + start, CHUNK), pl.ds(channels, 2 * channels)],
            w_in[pl.ds(2 * channels, 2 * channels), :],
        )
        proj_ref[pl.ds(start, CHUNK), :] = value.astype(BF16)
    for start in range(0, rows, CHUNK):
        acc_ref[pl.ds(start, CHUNK), :] = pair_taps(taps, w_first, start, CHUNK, pairs)


def resident_part(x, w_first, w_second, w_in):
    height, width, channels = x.shape
    out = w_first.shape[2]
    temporal = w_in.shape[1]
    glob = w_first.shape[1] - channels
    pairs = width // 2
    rows = height * pairs
    return pl.pallas_call(
        resident_kernel,
        out_shape=(
            jax.ShapeDtypeStruct((rows, 2 * out), F32),
            jax.ShapeDtypeStruct((rows // 2, 4 * temporal), BF16),
            jax.ShapeDtypeStruct((12 * out, 2 * out), BF16),
            jax.ShapeDtypeStruct((12 * glob, 2 * out), BF16),
        ),
        in_specs=in_vmem(4),
        out_specs=tuple(in_vmem(4)),
        scratch_shapes=[
            pltpu.VMEM((2 * rows + 2 * EDGE, channels), F32),
            pltpu.VMEM((rows + 2 * pairs, 4 * channels), BF16),
            pltpu.VMEM((12 * channels, 2 * out), BF16),
            pltpu.VMEM((4 * channels, 4 * temporal), BF16),
        ],
        compiler_params=pltpu.CompilerParams(vmem_limit_bytes=VMEM_BYTES),
        cost_estimate=pl.CostEstimate(
            flops=2 * rows * 12 * channels * 2 * out,
            bytes_accessed=8 * 1024 * 1024,
            transcendentals=0,
        ),
        name="resident_part",
    )(x, w_first, w_second, w_in)


def mix_kernel(lead_axis, hours_ref, prev_ref, self_ref, next_ref, mix_ref, mixed_ref, w_mix):
    leads = hours_ref.shape[0]
    temporal = mix_ref.shape[1]
    lead = lax.axis_index(lead_axis)
    now = hours_ref[lead]
    before = hours_ref[jnp.maximum(lead - 1, 0)]
    after = hours_ref[jnp.minimum(lead + 1, leads - 1)]

    def gain(gap, used):
        gap = jnp.full((1, 4 * temporal), gap, jnp.int32).astype(F32)
        return jnp.where(used, jnp.exp(-0.5 * (gap - 1.0)), 0.0)

    gain_prev = gain(now - before, lead > 0)
    gain_next = gain(after - now, lead < leads - 1)
    w_mix[...] = jnp.zeros_like(w_mix)
    for k in range(3):
        for s in range(4):
            w_mix[k, pl.ds(s * temporal, temporal), pl.ds(s * temporal, temporal)] = mix_ref[k]
    rows = mixed_ref.shape[0]
    for start in range(0, rows, CHUNK):
        part = pl.ds(start, CHUNK)
        value = gain_prev * dot(prev_ref[part, :], w_mix[0])
        value = value + dot(self_ref[part, :], w_mix[1])
        value = value + gain_next * dot(next_ref[part, :], w_mix[2])
        mixed_ref[part, :] = value.astype(BF16)


def mix_part(hours, before, own, after, w_mix):
    lanes = own.shape[1]
    return pl.pallas_call(
        lambda *refs: mix_kernel("lead", *refs),
        out_shape=jax.ShapeDtypeStruct(own.shape, BF16),
        in_specs=[pl.BlockSpec(memory_space=pltpu.SMEM)] + in_vmem(4),
        out_specs=pl.BlockSpec(memory_space=pltpu.VMEM),
        scratch_shapes=[pltpu.VMEM((3, lanes, lanes), BF16)],
        cost_estimate=pl.CostEstimate(
            flops=6 * own.shape[0] * lanes * lanes, bytes_accessed=1024 * 1024, transcendentals=0
        ),
        name="mix_part",
    )(hours, before, own, after, w_mix)


def rest_kernel(
    place, owner_ref, acc_ref, x_ref, mixed_ref, w_second_ref, w_glob_ref, w_out_ref, *refs
):
    pieces, (out_ref, glob_cells, glob_taps, odd, even, taps, w_lift, cells) = refs[:-8], refs[-8:]
    height, width, channels = x_ref.shape
    pairs = width // 2
    rows = height * pairs
    out = channels
    temporal = w_out_ref.shape[0]
    lanes = glob_cells.shape[1]
    share = height // len(pieces)
    clear_edges(glob_taps, pairs)
    clear_edges(taps, pairs)
    w_lift[...] = jnp.zeros_like(w_lift)
    for s in range(2):
        for q in range(2):
            w_lift[
                s, pl.ds((2 * s + q) * temporal, temporal), pl.ds(q * out, out)
            ] = w_out_ref[...]
    for k, piece in enumerate(pieces):
        base = place(owner_ref, k) * (share * pairs)
        for m in range(pairs):
            value = piece[:, pl.ds(m * lanes, lanes)].astype(F32)
            glob_cells[pl.ds(EDGE + base + m, share, stride=pairs), :] = value
    left, right = column_masks(CHUNK, lanes, pairs)
    low = lax.broadcasted_iota(jnp.int32, (CHUNK, lanes), 1) < lanes // 2
    for start in range(0, rows, CHUNK):
        here = glob_cells[pl.ds(EDGE + start, CHUNK), :]
        before = jnp.where(left, 0.0, glob_cells[pl.ds(EDGE + start - 1, CHUNK), :])
        after = jnp.where(right, 0.0, glob_cells[pl.ds(EDGE + start + 1, CHUNK), :])
        glob_taps[pl.ds(pairs + start, CHUNK), pl.ds(0, lanes)] = here.astype(BF16)
        glob_taps[pl.ds(pairs + start, CHUNK), pl.ds(lanes, lanes)] = jnp.where(
            low, after, before
        ).astype(BF16)
    for start in range(0, rows, CHUNK):
        value = acc_ref[pl.ds(start, CHUNK), :] + pair_taps(
            glob_taps, w_glob_ref, start, CHUNK, pairs
        )
        value = silu(value)
        even[pl.ds(EDGE + start, CHUNK), :] = value[:, :out]
        odd[pl.ds(EDGE + start, CHUNK), :] = value[:, out:]
        taps[pl.ds(pairs + start, CHUNK), pl.ds(out, 2 * out)] = value.astype(BF16)
    left, right = column_masks(CHUNK, out, pairs)
    for start in range(0, rows, CHUNK):
        before = jnp.where(left, 0.0, odd[pl.ds(EDGE + start - 1, CHUNK), :])
        after = jnp.where(right, 0.0, even[pl.ds(EDGE + start + 1, CHUNK), :])
        taps[pl.ds(pairs + start, CHUNK), pl.ds(0, out)] = before.astype(BF16)
        taps[pl.ds(pairs + start, CHUNK), pl.ds(3 * out, out)] = after.astype(BF16)
    half = rows // 2
    for start in range(0, rows, CHUNK):
        s = start // half
        value = pair_taps(taps, w_second_ref, start, CHUNK, pairs)
        value = value + dot(mixed_ref[pl.ds(start - s * half, CHUNK), :], w_lift[s])
        value = silu(value)
        cells[pl.ds(2 * start, CHUNK, stride=2), :] = value[:, :out]
        cells[pl.ds(2 * start + 1, CHUNK, stride=2), :] = value[:, out:]
        part = pl.ds(start // pairs, CHUNK // pairs)
        value = cells[pl.ds(2 * start, 2 * CHUNK), :].reshape(CHUNK // pairs, width, channels)
        out_ref[part, :, :] = (x_ref[part, :, :].astype(F32) + value).astype(BF16)


def rest_part(place, owner, acc, x, mixed, w_second, w_glob, w_out, pieces):
    height, width, channels = x.shape
    pairs = width // 2
    rows = height * pairs
    lanes = pieces[0].shape[1] // pairs
    return pl.pallas_call(
        lambda *refs: rest_kernel(place, *refs),
        out_shape=jax.ShapeDtypeStruct(x.shape, BF16),
        in_specs=[pl.BlockSpec(memory_space=pltpu.SMEM)] + in_vmem(6 + len(pieces)),
        out_specs=pl.BlockSpec(memory_space=pltpu.VMEM),
        scratch_shapes=[
            pltpu.VMEM((rows + 2 * EDGE, lanes), F32),
            pltpu.VMEM((rows + 2 * pairs, 2 * lanes), BF16),
            pltpu.VMEM((rows + 2 * EDGE, channels), F32),
            pltpu.VMEM((rows + 2 * EDGE, channels), F32),
            pltpu.VMEM((rows + 2 * pairs, 4 * channels), BF16),
            pltpu.VMEM((2, mixed.shape[1], 2 * channels), BF16),
            pltpu.VMEM((2 * rows, channels), F32),
        ],
        compiler_params=pltpu.CompilerParams(vmem_limit_bytes=VMEM_BYTES),
        cost_estimate=pl.CostEstimate(
            flops=4 * rows * 12 * channels * 2 * channels,
            bytes_accessed=8 * 1024 * 1024,
            transcendentals=0,
        ),
        name="rest_part",
    )(owner, acc, x, mixed, w_second, w_glob, w_out, *pieces)


def passed_along(block, axis, distance):
    devices = range(lax.axis_size(axis))
    route = [(i - distance, i) for i in devices if i - distance in devices]
    return lax.ppermute(block, axis, route)


def rotated(block, axis, distance):
    count = lax.axis_size(axis)
    return lax.ppermute(block, axis, [(i, (i + distance) % count) for i in range(count)])


def pick_kernel(owner_ref, *refs):
    pieces, out_ref = refs[:-1], refs[-1]
    count = len(pieces)
    want = lax.rem(
        lax.axis_index("patch") - owner_ref[lax.axis_index("lead")] + count, count
    )
    for k, piece in enumerate(pieces):

        @pl.when(want == k)
        def _(piece=piece):
            out_ref[...] = piece[...]


def pick(owner, pieces):
    return pl.pallas_call(
        pick_kernel,
        out_shape=jax.ShapeDtypeStruct(pieces[0].shape, pieces[0].dtype),
        in_specs=[pl.BlockSpec(memory_space=pltpu.SMEM)] + in_vmem(len(pieces)),
        out_specs=pl.BlockSpec(memory_space=pltpu.VMEM),
        name="pick",
    )(owner, *pieces)


def spread(block, owner):
    count = lax.axis_size("patch")
    share = block.shape[0] // count
    pieces = [block[k * share : (k + 1) * share] for k in range(count)]
    got = [pieces[0]] + [rotated(pieces[k], "patch", k) for k in range(1, count)]
    held = pick(owner, got)
    held_by = [held] + [rotated(held, "patch", k) for k in range(1, count)]

    def place(owner_ref, k):
        away = lax.axis_index("patch") - k - owner_ref[lax.axis_index("lead")]
        return lax.rem(away + 2 * count, count)

    return held_by, place


def broadcast(block, owner):
    mine = lax.axis_index("patch") == owner[lax.axis_index("lead")]
    block = lax.psum(jnp.where(mine, block, jnp.zeros_like(block)), "patch")
    return [block], lambda owner_ref, k: 0


def per_device(
    features, context, owner, hours, w_first, w_second, w_lead_in, w_lead_mix, w_lead_out
):
    resident = features[0, 0]
    few = lax.axis_size("patch") <= 4
    pieces, place = (spread if few else broadcast)(context[0, 0], owner)
    acc, proj, w_second, w_glob = resident_part(resident, w_first, w_second, w_lead_in)
    preceding = passed_along(proj, "lead", 1)
    following = passed_along(proj, "lead", -1)
    mixed = mix_part(hours, preceding, proj, following, w_lead_mix)
    result = rest_part(place, owner, acc, resident, mixed, w_second, w_glob, w_lead_out, pieces)
    return result[None, None]


def solution(mesh):
    placed = (
        P(("grp", "lead"), "patch", None, None, None),
        P("patch", ("grp", "lead"), None, None),
        P("grp"),
        P("grp"),
        P(),
        P(),
        P(),
        P(),
        P(),
    )
    return jax.shard_map(
        per_device,
        mesh=mesh,
        in_specs=placed,
        out_specs=P(("grp", "lead"), "patch", None, None, None),
        check_vma=False,
    )
```

time: 109 us -> 56.4 us (0.52)
  local copies, waits for them, and re-layouts: 30.1 us -> 11.5 us
  matrix products: 17.7 us -> 0 us
  between operations: 17 us -> 0.1 us
  waiting for transfers between devices: 35.6 us -> 19.2 us
  Pallas kernels: 0 us -> 11.8 us
  starting transfers between devices: 3.67 us -> 13.4 us
  other arithmetic: 3.88 us -> 0 us
    psum x1 -> x0, waiting for transfers between devices: 35.6 us -> none  [broadcast(): return lax.psum(block, axis)]
    ppermute x0 -> x6, waiting for transfers between devices: none -> 19.1 us  [rotated(): lax.ppermute(block, axis, [(i, (i + distance) % count) for i in range(cou...]
    dot_general x22 -> x0, matrix products: 17.7 us -> none  [the longest x18 10.9 us: conv_padded(): jnp.dot(window, kernel[tap_index], preferred_element_type=jnp.float32)]
    pallas_call x0 -> x4, Pallas kernels: none -> 11.8 us  [the longest x1 5.24 us: rest_part(): pl.pallas_call(lambda *refs: rest_kernel(place, *refs), out_shape=jax.Sha...]
    slice x2 -> x1, local copies, waits for them, and re-layouts: 11.1 us -> 0.71 us  [spread(): pieces = [block[k * share:(k + 1) * share] for k in range(count)]]
    ppermute x0 -> x6, starting transfers between devices: none -> 8.92 us  [rotated(): lax.ppermute(block, axis, [(i, (i + distance) % count) for i in range(cou...]
    reshape x4 -> x0, local copies, waits for them, and re-layouts: 6.14 us -> none  [the longest x1 2.46 us: per_device(): context_full = context_full.reshape(row_count, col_count, -1)]
    unnamed x33 -> x35, local copies, waits for them, and re-layouts: 6.23 us -> 10.8 us
  transfers between devices with their start and end apart: 3 -> 8, of which waited for: 1 -> 4; matrix products, arithmetic and copies ran while one was open for 6% -> 1% of each run, Pallas kernels for 0% -> 7%
where the time goes in v1:
time: 56.4 us; the launch traced here: 55.9 us
  waiting for transfers between devices  19.2 us (34%)
  starting transfers between devices  13.4 us (24%)
  Pallas kernels  11.8 us (21%)
  local copies, waits for them, and re-layouts  11.5 us (20%)
    ppermute x6, waiting for transfers between devices, rotated(): lax.ppermute(block, axis, [(i, (i + distance) % count) for i in range(cou...  19.1 us
    unnamed x35, local copies, waits for them, and re-layouts  10.8 us
    ppermute x6, starting transfers between devices, rotated(): lax.ppermute(block, axis, [(i, (i + distance) % count) for i in range(cou...  8.92 us
    pallas_call x1, Pallas kernels, rest_part(): pl.pallas_call(lambda *refs: rest_kernel(place, *refs), out_shape=jax.Sha...  5.24 us
    ppermute x2, starting transfers between devices, passed_along(): return lax.ppermute(block, axis, route)  4.47 us
    pallas_call x1, Pallas kernels, resident_part(): pl.pallas_call(resident_kernel, out_shape=(jax.ShapeDtypeStruct((rows, 2...  2.44 us
    pallas_call x1, Pallas kernels, mix_part(): pl.pallas_call(lambda *refs: mix_kernel('lead', *refs), out_shape=jax.Sha...  2.28 us
    pallas_call x1, Pallas kernels, pick(): pl.pallas_call(pick_kernel, out_shape=jax.ShapeDtypeStruct(pieces[0].shap...  1.8 us
  transfers between devices with their start and end apart: 8, of which 4 were waited for; matrix products, arithmetic and copies ran while one was open for 1% of the time, Pallas kernels for 7%

profile of v1, /device:TPU:0, one launch (start us, length us, event | category | flops | bytes accessed | tf_op | source)
XLA Modules:
  0.0 55.9 jit_solution(859038222062140042)
XLA Ops:
  0.0 0.8 %copy.10.in_ref = bf16[128,32]{1,0:T(8,128)(2,1)S(1)} copy(bf16[128,32]{0,1:T(8,128)(2,1)} %param.15) | data formatting | bytes 16384 | tf_op args[6]
  0.8 1.2 %copy-done.4 = bf16[1,1,128,32,128]{4,3,2,1,0:T(8,128)(2,1)S(1)} copy-done((bf16[1,1,128,32,128]{4,3,2,1,0:T(8,128)(2,1)S(1)}, bf16[1,1,128,32,128]{4,3,2,1,0:T(8,128)(2,1)}, u32[]{:S(2)}) %copy-start.4) | copy-done | bytes 1048600
  2.0 1.0 %copy-done.6 = bf16[9,192,128]{2,1,0:T(8,128)(2,1)S(1)} copy-done((bf16[9,192,128]{2,1,0:T(8,128)(2,1)S(1)}, bf16[9,192,128]{2,1,0:T(8,128)(2,1)}, u32[]{:S(2)}) %copy-start.6) | copy-done | bytes 442392
  3.1 1.0 %copy-done.7 = bf16[9,128,128]{2,1,0:T(8,128)(2,1)S(1)} copy-done((bf16[9,128,128]{2,1,0:T(8,128)(2,1)S(1)}, bf16[9,128,128]{2,1,0:T(8,128)(2,1)}, u32[]{:S(2)}) %copy-start.7) | copy-done | bytes 294936
  4.0 2.4 %resident_part.1 = (f32[2048,256]{1,0:T(8,128)S(1)}, bf16[1024,128]{1,0:T(8,128)(2,1)S(1)}, bf16[1536,256]{1,0:T(8,128)(2,1)S(1)}, bf16[768,256]{1,0:T(8,128)(2,1)S(1)}) custom-call(bf16[128,32,128]{2,1,0:T(8,128)(2,1)S(1)} %bitcast.10, bf16[9,192,128]{2,1,0:T(8,128)(2,1)S(1)} %copy-done.6, bf16[9,128,128]{2,1,0:T(8,128)(2,1)S(1)} %copy-done.7, ...), custom_call_target="tpu_custom_call" | custom-call | flops 1610612736 | bytes 8388608 | tf_op jit(solution)/shard_map/resident_part/pallas_call | solution.py:112
  6.5 1.3 %copy-done.9 = f32[2048,256]{1,0:T(8,128)} copy-done((f32[2048,256]{1,0:T(8,128)}, f32[2048,256]{1,0:T(8,128)S(1)}, u32[]{:S(2)}) %copy-start.9) | copy-done | bytes 2097176
  7.8 1.4 %collective-permute-start.1 = (bf16[1024,128]{1,0:T(8,128)(2,1)S(1)}, bf16[1024,128]{1,0:T(8,128)(2,1)S(1)}, u32[]{:S(2)}, u32[]{:S(2)}) collective-permute-start(bf16[1024,128]{1,0:T(8,128)(2,1)S(1)} %get-tuple-element.10.refs_2_), channel_id=1, source_target_pairs={{1,0},{2,1},{3,2},{5,4},{6,5},{7,6},{9,8},{10,9},{11,10},{13,12},{... | collective-permute-start | bytes 786440 | tf_op jit(solution)/shard_map/ppermute | solution.py:273
  9.2 3.0 %collective-permute-start = (bf16[1024,128]{1,0:T(8,128)(2,1)S(1)}, bf16[1024,128]{1,0:T(8,128)(2,1)S(1)}, u32[]{:S(2)}, u32[]{:S(2)}) collective-permute-start(bf16[1024,128]{1,0:T(8,128)(2,1)S(1)} %get-tuple-element.10.refs_2_), channel_id=1, source_target_pairs={{0,1},{1,2},{2,3},{4,5},{5,6},{6,7},{8,9},{9,10},{10,11},{12,13},{... | collective-permute-start | bytes 786440 | tf_op jit(solution)/shard_map/ppermute | solution.py:273
  12.3 0.7 %slice_bitcast_fusion = (bf16[32,2048]{1,0:T(8,128)(2,1)S(1)}, bf16[32,2048]{1,0:T(8,128)(2,1)S(1)}, bf16[32,2048]{1,0:T(8,128)(2,1)}, bf16[32,2048]{1,0:T(8,128)(2,1)S(1)}) fusion(bf16[1,1,128,2048]{3,2,1,0:T(8,128)(2,1)S(1)} %copy-done.11), kind=kLoop, calls=%fused_computation | loop fusion | bytes 1048576 | tf_op jit(solution)/shard_map/slice | solution.py:307
  13.0 5.0 %collective-permute-start.4 = (bf16[32,2048]{1,0:T(8,128)(2,1)S(1)}, bf16[32,2048]{1,0:T(8,128)(2,1)S(1)}, u32[]{:S(2)}, u32[]{:S(2)}) collective-permute-start(bf16[32,2048]{1,0:T(8,128)(2,1)S(1)} %get-tuple-element.13), channel_id=1, source_target_pairs={{0,12},{4,0},{8,4},{12,8},{1,13},{5,1},{9,5},{13,9},{2,14},{6,2},{... | collective-permute-start | bytes 393224 | tf_op jit(solution)/shard_map/ppermute | solution.py:278
  18.1 1.0 %collective-permute-start.3 = (bf16[32,2048]{1,0:T(8,128)(2,1)S(1)}, bf16[32,2048]{1,0:T(8,128)(2,1)S(1)}, u32[]{:S(2)}, u32[]{:S(2)}) collective-permute-start(bf16[32,2048]{1,0:T(8,128)(2,1)S(1)} %get-tuple-element.16), channel_id=1, source_target_pairs={{0,8},{4,12},{8,0},{12,4},{1,9},{5,13},{9,1},{13,5},{2,10},{6,14},... | collective-permute-start | bytes 393224 | tf_op jit(solution)/shard_map/ppermute | solution.py:278
  19.1 2.8 %collective-permute-done.4.refs_3_ = bf16[32,2048]{1,0:T(8,128)(2,1)S(1)} collective-permute-done((bf16[32,2048]{1,0:T(8,128)(2,1)S(1)}, bf16[32,2048]{1,0:T(8,128)(2,1)S(1)}, u32[]{:S(2)}, u32[]{:S(2)}) %collective-permute-start.4) | collective-permute-done | bytes 131104 | tf_op jit(solution)/shard_map/ppermute | solution.py:278
  21.9 4.5 %collective-permute-done.2.refs_1_ = bf16[32,2048]{1,0:T(8,128)(2,1)S(1)} collective-permute-done((bf16[32,2048]{1,0:T(8,128)(2,1)S(1)}, bf16[32,2048]{1,0:T(8,128)(2,1)S(1)}, u32[]{:S(2)}, u32[]{:S(2)}) %collective-permute-start.2) | collective-permute-done | bytes 131104 | tf_op jit(solution)/shard_map/ppermute | solution.py:278
  26.3 4.5 %collective-permute-done.3.refs_2_ = bf16[32,2048]{1,0:T(8,128)(2,1)S(1)} collective-permute-done((bf16[32,2048]{1,0:T(8,128)(2,1)S(1)}, bf16[32,2048]{1,0:T(8,128)(2,1)S(1)}, u32[]{:S(2)}, u32[]{:S(2)}) %collective-permute-start.3) | collective-permute-done | bytes 131104 | tf_op jit(solution)/shard_map/ppermute | solution.py:278
  31.4 1.8 %pick.1.refs_7_ = bf16[32,2048]{1,0:T(8,128)(2,1)} custom-call(s32[4]{0:T(128)} %refs_0_.3, bf16[32,2048]{1,0:T(8,128)(2,1)} %get-tuple-element.15.refs_0_, bf16[32,2048]{1,0:T(8,128)(2,1)} %copy-done.15, bf16[32,2048]{1,0:T(8,128)(2,1)} %copy-done.16, bf16[32,2048]{1,0:T(8,128)(2,1)} %copy-done.14), custom_call_target="tpu_custom_call" | custom-call | tf_op jit(solution)/shard_map/pick/pallas_call | solution.py:295
  33.2 2.3 %collective-permute-start.7 = (bf16[32,2048]{1,0:T(8,128)(2,1)}, bf16[32,2048]{1,0:T(8,128)(2,1)S(1)}, u32[]{:S(2)}, u32[]{:S(2)}) collective-permute-start(bf16[32,2048]{1,0:T(8,128)(2,1)} %pick.1.refs_7_), channel_id=1, source_target_pairs={{0,12},{4,0},{8,4},{12,8},{1,13},{5,1},{9,5},{13,9},{2,14},{6,2},{... | collective-permute-start | bytes 393224 | tf_op jit(solution)/shard_map/ppermute | solution.py:278
  36.1 0.7 %copy-done.12 = bf16[1024,128]{1,0:T(8,128)(2,1)} copy-done((bf16[1024,128]{1,0:T(8,128)(2,1)}, bf16[1024,128]{1,0:T(8,128)(2,1)S(1)}, u32[]{:S(2)}) %copy-start.12) | copy-done | bytes 262168
  36.8 0.7 %copy-done.13 = bf16[1024,128]{1,0:T(8,128)(2,1)} copy-done((bf16[1024,128]{1,0:T(8,128)(2,1)}, bf16[1024,128]{1,0:T(8,128)(2,1)S(1)}, u32[]{:S(2)}) %copy-start.13) | copy-done | bytes 262168
  37.5 2.3 %mix_part.1.refs_3_ = bf16[1024,128]{1,0:T(8,128)(2,1)} custom-call(s32[4]{0:T(128)} %refs_0_.2, bf16[1024,128]{1,0:T(8,128)(2,1)} %copy-done.13, bf16[1024,128]{1,0:T(8,128)(2,1)} %copy-done, bf16[1024,128]{1,0:T(8,128)(2,1)} %copy-done.12, bf16[3,32,32]{2,1,0:T(8,128)(2,1)} %refs_4_.1), custom_call_target="tpu_custom_call" | custom-call | flops 100663296 | bytes 1048576 | tf_op jit(solution)/shard_map/mix_part/pallas_call | solution.py:167
  39.8 7.4 %collective-permute-done.6.refs_9_ = bf16[32,2048]{1,0:T(8,128)(2,1)S(1)} collective-permute-done((bf16[32,2048]{1,0:T(8,128)(2,1)}, bf16[32,2048]{1,0:T(8,128)(2,1)S(1)}, u32[]{:S(2)}, u32[]{:S(2)}) %collective-permute-start.6) | collective-permute-done | bytes 131104 | tf_op jit(solution)/shard_map/ppermute | solution.py:278
  47.2 0.9 %copy-done.1 = bf16[1024,128]{1,0:T(8,128)(2,1)S(1)} copy-done((bf16[1024,128]{1,0:T(8,128)(2,1)S(1)}, bf16[1024,128]{1,0:T(8,128)(2,1)}, u32[]{:S(2)}) %copy-start.1) | copy-done | bytes 262168
  48.2 0.9 %copy-done.2 = bf16[32,2048]{1,0:T(8,128)(2,1)S(1)} copy-done((bf16[32,2048]{1,0:T(8,128)(2,1)S(1)}, bf16[32,2048]{1,0:T(8,128)(2,1)}, u32[]{:S(2)}) %copy-start.2) | copy-done | bytes 131096
  49.1 1.6 %copy-done.10 = f32[2048,256]{1,0:T(8,128)S(1)} copy-done((f32[2048,256]{1,0:T(8,128)S(1)}, f32[2048,256]{1,0:T(8,128)}, u32[]{:S(2)}) %copy-start.10) | copy-done | bytes 2097176
  50.7 5.2 %rest_part.1 = bf16[128,32,128]{2,1,0:T(8,128)(2,1)} custom-call(s32[4]{0:T(128)S(1)} %copy-done.3, f32[2048,256]{1,0:T(8,128)S(1)} %copy-done.10, bf16[128,32,128]{2,1,0:T(8,128)(2,1)S(1)} %bitcast.11, bf16[1024,128]{1,0:T(8,128)(2,1)S(1)} %copy-done.1, bf16[1536,256]{1,0:T(8,128)(2,1)S(1)} %get-tuple-element.11.refs_4_, ...), custom_call_target="tpu_custom_call" | custom-call | flops 3221225472 | bytes 8388608 | tf_op jit(solution)/shard_map/rest_part/pallas_call | solution.py:246
  (32 shorter events, 1.3 us)
Async XLA Ops:
  0.8 1.2 %copy-start.4 = (bf16[1,1,128,32,128]{4,3,2,1,0:T(8,128)(2,1)S(1)}, bf16[1,1,128,32,128]{4,3,2,1,0:T(8,128)(2,1)}, u32[]{:S(2)}) copy-start(bf16[1,1,128,32,128]{4,3,2,1,0:T(8,128)(2,1)} %param.9) | copy-start | bytes 3145732
  2.0 1.0 %copy-start.6 = (bf16[9,192,128]{2,1,0:T(8,128)(2,1)S(1)}, bf16[9,192,128]{2,1,0:T(8,128)(2,1)}, u32[]{:S(2)}) copy-start(bf16[9,192,128]{2,1,0:T(8,128)(2,1)} %first_ref.1) | copy-start | bytes 1327108
  3.1 1.0 %copy-start.7 = (bf16[9,128,128]{2,1,0:T(8,128)(2,1)S(1)}, bf16[9,128,128]{2,1,0:T(8,128)(2,1)}, u32[]{:S(2)}) copy-start(bf16[9,128,128]{2,1,0:T(8,128)(2,1)} %second_ref.1) | copy-start | bytes 884740
  4.0 8.3 %copy-start.11 = (bf16[1,1,128,2048]{3,2,1,0:T(8,128)(2,1)S(1)}, bf16[1,1,128,2048]{3,2,1,0:T(8,128)(2,1)}, u32[]{:S(2)}) copy-start(bf16[1,1,128,2048]{3,2,1,0:T(8,128)(2,1)} %param.10) | copy-start | bytes 1572868
  6.5 1.3 %copy-start.9 = (f32[2048,256]{1,0:T(8,128)}, f32[2048,256]{1,0:T(8,128)S(1)}, u32[]{:S(2)}) copy-start(f32[2048,256]{1,0:T(8,128)S(1)} %get-tuple-element.9.refs_1_) | copy-start | bytes 6291460
  7.8 28.3 %copy-start = (bf16[1024,128]{1,0:T(8,128)(2,1)}, bf16[1024,128]{1,0:T(8,128)(2,1)S(1)}, u32[]{:S(2)}) copy-start(bf16[1024,128]{1,0:T(8,128)(2,1)S(1)} %get-tuple-element.10.refs_2_) | copy-start | bytes 786436
  7.8 39.4 %copy-start.3 = (s32[4]{0:T(128)S(1)}, s32[4]{0:T(128)}, u32[]{:S(2)}) copy-start(s32[4]{0:T(128)} %refs_0_.3) | copy-start | bytes 52
  7.8 39.4 %copy-start.5 = (bf16[1,1,128,32,128]{4,3,2,1,0:T(8,128)(2,1)S(1)}, bf16[1,1,128,32,128]{4,3,2,1,0:T(8,128)(2,1)}, u32[]{:S(2)}) copy-start(bf16[1,1,128,32,128]{4,3,2,1,0:T(8,128)(2,1)} %param.9) | copy-start | bytes 3145732
  7.8 39.4 %copy-start.8 = (bf16[32,128]{1,0:T(8,128)(2,1)S(1)}, bf16[32,128]{1,0:T(8,128)(2,1)}, u32[]{:S(2)}) copy-start(bf16[32,128]{1,0:T(8,128)(2,1)} %refs_6_.1) | copy-start | bytes 24580
  7.8 28.3 %collective-permute-start.1 = (bf16[1024,128]{1,0:T(8,128)(2,1)S(1)}, bf16[1024,128]{1,0:T(8,128)(2,1)S(1)}, u32[]{:S(2)}, u32[]{:S(2)}) collective-permute-start(bf16[1024,128]{1,0:T(8,128)(2,1)S(1)} %get-tuple-element.10.refs_2_), channel_id=1, source_target_pairs={{1,0},{2,1},{3,2},{5,4},{6,5},{7,6},{9,8},{10,9},{11,10},{13,12},{... | collective-permute-start | bytes 786440 | tf_op jit(solution)/shard_map/ppermute | solution.py:273
  9.2 26.9 %collective-permute-start = (bf16[1024,128]{1,0:T(8,128)(2,1)S(1)}, bf16[1024,128]{1,0:T(8,128)(2,1)S(1)}, u32[]{:S(2)}, u32[]{:S(2)}) collective-permute-start(bf16[1024,128]{1,0:T(8,128)(2,1)S(1)} %get-tuple-element.10.refs_2_), channel_id=1, source_target_pairs={{0,1},{1,2},{2,3},{4,5},{5,6},{6,7},{8,9},{9,10},{10,11},{12,13},{... | collective-permute-start | bytes 786440 | tf_op jit(solution)/shard_map/ppermute | solution.py:273
  13.0 8.9 %collective-permute-start.4 = (bf16[32,2048]{1,0:T(8,128)(2,1)S(1)}, bf16[32,2048]{1,0:T(8,128)(2,1)S(1)}, u32[]{:S(2)}, u32[]{:S(2)}) collective-permute-start(bf16[32,2048]{1,0:T(8,128)(2,1)S(1)} %get-tuple-element.13), channel_id=1, source_target_pairs={{0,12},{4,0},{8,4},{12,8},{1,13},{5,1},{9,5},{13,9},{2,14},{6,2},{... | collective-permute-start | bytes 393224 | tf_op jit(solution)/shard_map/ppermute | solution.py:278
  18.1 8.3 %collective-permute-start.2 = (bf16[32,2048]{1,0:T(8,128)(2,1)S(1)}, bf16[32,2048]{1,0:T(8,128)(2,1)S(1)}, u32[]{:S(2)}, u32[]{:S(2)}) collective-permute-start(bf16[32,2048]{1,0:T(8,128)(2,1)S(1)} %get-tuple-element.14), channel_id=1, source_target_pairs={{0,4},{4,8},{8,12},{12,0},{1,5},{5,9},{9,13},{13,1},{2,6},{6,10},{... | collective-permute-start | bytes 393224 | tf_op jit(solution)/shard_map/ppermute | solution.py:278
  18.1 12.7 %collective-permute-start.3 = (bf16[32,2048]{1,0:T(8,128)(2,1)S(1)}, bf16[32,2048]{1,0:T(8,128)(2,1)S(1)}, u32[]{:S(2)}, u32[]{:S(2)}) collective-permute-start(bf16[32,2048]{1,0:T(8,128)(2,1)S(1)} %get-tuple-element.16), channel_id=1, source_target_pairs={{0,8},{4,12},{8,0},{12,4},{1,9},{5,13},{9,1},{13,5},{2,10},{6,14},... | collective-permute-start | bytes 393224 | tf_op jit(solution)/shard_map/ppermute | solution.py:278
  21.9 8.9 %copy-start.14 = (bf16[32,2048]{1,0:T(8,128)(2,1)}, bf16[32,2048]{1,0:T(8,128)(2,1)S(1)}, u32[]{:S(2)}) copy-start(bf16[32,2048]{1,0:T(8,128)(2,1)S(1)} %collective-permute-done.4.refs_3_) | copy-start | bytes 393220
  26.3 4.5 %copy-start.15 = (bf16[32,2048]{1,0:T(8,128)(2,1)}, bf16[32,2048]{1,0:T(8,128)(2,1)S(1)}, u32[]{:S(2)}) copy-start(bf16[32,2048]{1,0:T(8,128)(2,1)S(1)} %collective-permute-done.2.refs_1_) | copy-start | bytes 393220
  33.2 6.5 %collective-permute-start.7 = (bf16[32,2048]{1,0:T(8,128)(2,1)}, bf16[32,2048]{1,0:T(8,128)(2,1)S(1)}, u32[]{:S(2)}, u32[]{:S(2)}) collective-permute-start(bf16[32,2048]{1,0:T(8,128)(2,1)} %pick.1.refs_7_), channel_id=1, source_target_pairs={{0,12},{4,0},{8,4},{12,8},{1,13},{5,1},{9,5},{13,9},{2,14},{6,2},{... | collective-permute-start | bytes 393224 | tf_op jit(solution)/shard_map/ppermute | solution.py:278
  35.5 11.7 %collective-permute-start.6 = (bf16[32,2048]{1,0:T(8,128)(2,1)}, bf16[32,2048]{1,0:T(8,128)(2,1)S(1)}, u32[]{:S(2)}, u32[]{:S(2)}) collective-permute-start(bf16[32,2048]{1,0:T(8,128)(2,1)} %pick.1.refs_7_), channel_id=1, source_target_pairs={{0,8},{4,12},{8,0},{12,4},{1,9},{5,13},{9,1},{13,5},{2,10},{6,14},... | collective-permute-start | bytes 393224 | tf_op jit(solution)/shard_map/ppermute | solution.py:278
  35.5 11.7 %collective-permute-start.5 = (bf16[32,2048]{1,0:T(8,128)(2,1)}, bf16[32,2048]{1,0:T(8,128)(2,1)S(1)}, u32[]{:S(2)}, u32[]{:S(2)}) collective-permute-start(bf16[32,2048]{1,0:T(8,128)(2,1)} %pick.1.refs_7_), channel_id=1, source_target_pairs={{0,4},{4,8},{8,12},{12,0},{1,5},{5,9},{9,13},{13,1},{2,6},{6,10},{... | collective-permute-start | bytes 393224 | tf_op jit(solution)/shard_map/ppermute | solution.py:278
  36.1 0.7 %copy-start.12 = (bf16[1024,128]{1,0:T(8,128)(2,1)}, bf16[1024,128]{1,0:T(8,128)(2,1)S(1)}, u32[]{:S(2)}) copy-start(bf16[1024,128]{1,0:T(8,128)(2,1)S(1)} %collective-permute-done.1.refs_3_) | copy-start | bytes 786436
  36.8 0.7 %copy-start.13 = (bf16[1024,128]{1,0:T(8,128)(2,1)}, bf16[1024,128]{1,0:T(8,128)(2,1)S(1)}, u32[]{:S(2)}) copy-start(bf16[1024,128]{1,0:T(8,128)(2,1)S(1)} %collective-permute-done.refs_1_) | copy-start | bytes 786436
  47.2 1.0 %copy-start.1 = (bf16[1024,128]{1,0:T(8,128)(2,1)S(1)}, bf16[1024,128]{1,0:T(8,128)(2,1)}, u32[]{:S(2)}) copy-start(bf16[1024,128]{1,0:T(8,128)(2,1)} %mix_part.1.refs_3_) | copy-start | bytes 786436
  48.2 0.9 %copy-start.2 = (bf16[32,2048]{1,0:T(8,128)(2,1)S(1)}, bf16[32,2048]{1,0:T(8,128)(2,1)}, u32[]{:S(2)}) copy-start(bf16[32,2048]{1,0:T(8,128)(2,1)} %pick.1.refs_7_) | copy-start | bytes 393220
  49.1 1.6 %copy-start.10 = (f32[2048,256]{1,0:T(8,128)S(1)}, f32[2048,256]{1,0:T(8,128)}, u32[]{:S(2)}) copy-start(f32[2048,256]{1,0:T(8,128)} %copy-done.9) | copy-start | bytes 6291460
  (1 other events, 0.7 us)

commit v2 on v1

v2 whole, which is shorter than its diff:
```python
import jax
import jax.numpy as jnp
from jax import lax
from jax.experimental import pallas as pl
from jax.experimental.pallas import tpu as pltpu
from jax.sharding import PartitionSpec as P

BF16 = jnp.bfloat16
F32 = jnp.float32
EDGE = 8
CHUNK = 256
WIDE = 1024
GROUPS = 1
VMEM_BYTES = 20 * 1024 * 1024


def silu(v):
    return 0.5 * v * (1.0 + jnp.tanh(0.5 * v))


def dot(a, b):
    return jnp.dot(a, b, preferred_element_type=F32)


def dot_transposed(a, b):
    return lax.dot_general(a, b, (((1,), (1,)), ((), ())), preferred_element_type=F32)


def in_vmem(count):
    return [pl.BlockSpec(memory_space=pltpu.VMEM)] * count


def in_hbm(count):
    return [pl.BlockSpec(memory_space=pltpu.HBM)] * count


def start_copies(pairs, sems):
    copies = [
        pltpu.make_async_copy(source, target, sems.at[k])
        for k, (source, target) in enumerate(pairs)
    ]
    for copy in copies:
        copy.start()
    return copies


def put_pair_weights(target, weights, first, depth, offsets):
    out = weights.shape[2]
    span = depth * len(offsets)
    for a in range(3):
        for place, d in enumerate(offsets):
            rows = pl.ds(a * span + place * depth, depth)
            for q in range(2):
                b = d - q + 1
                lanes = pl.ds(q * out, out)
                if 0 <= b <= 2:
                    target[rows, lanes] = weights[3 * a + b, pl.ds(first, depth), :]
                else:
                    target[rows, lanes] = jnp.zeros((depth, out), target.dtype)


def clear_edges(ref, pairs):
    zero = jnp.zeros((pairs, ref.shape[1]), ref.dtype)
    ref[pl.ds(0, pairs), :] = zero
    ref[pl.ds(ref.shape[0] - pairs, pairs), :] = zero


def pair_taps(taps, weights, start, size, pairs):
    depth = taps.shape[1]
    total = dot(taps[pl.ds(start, size), :], weights[pl.ds(0, depth), :])
    for a in range(1, 3):
        total += dot(
            taps[pl.ds(start + a * pairs, size), :], weights[pl.ds(a * depth, depth), :]
        )
    return total


def column_masks(size, lanes, pairs):
    m = lax.rem(lax.broadcasted_iota(jnp.int32, (size, lanes), 0), pairs)
    return m == 0, m == pairs - 1


def looped(count, body):
    lax.fori_loop(0, count, lambda k, carry: (body(k), carry)[1], 0)


def resident_kernel(
    x_hbm, first_hbm, second_hbm, w_in_hbm, acc_ref, proj_ref, w_second_hbm, w_glob_hbm,
    x_ref, first_ref, second_ref, in_ref, w_second_ref, w_glob_ref, cells, taps, w_first, w_in, sems,
):
    height, width, channels = x_ref.shape
    pairs = width // 2
    rows = height * pairs
    temporal = in_ref.shape[0]
    glob = first_ref.shape[1] - channels
    copies = start_copies(
        [(x_hbm, x_ref), (w_in_hbm, in_ref), (first_hbm, first_ref), (second_hbm, second_ref)],
        sems,
    )
    clear_edges(taps, pairs)
    w_in[...] = jnp.zeros_like(w_in)
    left, right = column_masks(CHUNK, channels, pairs)
    copies[0].wait()
    for start in range(0, rows, CHUNK):
        part = x_ref[pl.ds(start // pairs, CHUNK // pairs), :, :].astype(F32)
        cells[pl.ds(EDGE + 2 * start, 2 * CHUNK), :] = part.reshape(2 * CHUNK, channels)
    for start in range(0, rows, CHUNK):
        for place, d in enumerate((-1, 0, 1, 2)):
            value = cells[pl.ds(EDGE + 2 * start + d, CHUNK, stride=2), :]
            if d == -1:
                value = jnp.where(left, 0.0, value)
            if d == 2:
                value = jnp.where(right, 0.0, value)
            taps[pl.ds(pairs + start, CHUNK), pl.ds(place * channels, channels)] = value.astype(BF16)
    half = rows // 2
    copies[1].wait()
    for s in range(4):
        w_in[pl.ds(s * temporal, temporal), pl.ds(s * channels, channels)] = in_ref[...]
    for start in range(0, half, CHUNK):
        value = dot_transposed(
            taps[pl.ds(pairs + start, CHUNK), pl.ds(channels, 2 * channels)],
            w_in[:, pl.ds(0, 2 * channels)],
        ) + dot_transposed(
            taps[pl.ds(pairs + half + start, CHUNK), pl.ds(channels, 2 * channels)],
            w_in[:, pl.ds(2 * channels, 2 * channels)],
        )
        proj_ref[pl.ds(start, CHUNK), :] = value.astype(BF16)
    copies[2].wait()
    put_pair_weights(w_first, first_ref, 0, channels, (-1, 0, 1, 2))
    put_pair_weights(w_glob_ref, first_ref, channels, glob, (0, 1, 2, -1))
    copies[3].wait()
    put_pair_weights(w_second_ref, second_ref, 0, channels, (-1, 0, 1, 2))
    writes = start_copies(
        [(w_glob_ref, w_glob_hbm), (w_second_ref, w_second_hbm)], sems.at[pl.ds(4, 2)]
    )
    for start in range(0, rows, WIDE):
        acc_ref[pl.ds(start, WIDE), :] = pair_taps(taps, w_first, start, WIDE, pairs)
    for write in writes:
        write.wait()


def resident_part(x, w_first, w_second, w_in):
    height, width, channels = x.shape
    out = w_first.shape[2]
    temporal = w_in.shape[1]
    w_in = w_in.T
    glob = w_first.shape[1] - channels
    pairs = width // 2
    rows = height * pairs
    results = (
        ((rows, 2 * out), F32),
        ((rows // 2, 4 * temporal), BF16),
        ((12 * out, 2 * out), BF16),
        ((12 * glob, 2 * out), BF16),
    )
    return pl.pallas_call(
        resident_kernel,
        out_shape=tuple(
            space(*kind) for space, kind in zip((pltpu.VMEM,) * 2 + (pltpu.HBM,) * 2, results)
        ),
        in_specs=in_hbm(4),
        out_specs=tuple(in_vmem(2) + in_hbm(2)),
        scratch_shapes=[
            pltpu.VMEM(x.shape, BF16),
            pltpu.VMEM(w_first.shape, BF16),
            pltpu.VMEM(w_second.shape, BF16),
            pltpu.VMEM(w_in.shape, BF16),
            pltpu.VMEM(*results[2]),
            pltpu.VMEM(*results[3]),
            pltpu.VMEM((2 * rows + 2 * EDGE, channels), F32),
            pltpu.VMEM((rows + 2 * pairs, 4 * channels), BF16),
            pltpu.VMEM((12 * channels, 2 * out), BF16),
            pltpu.VMEM((4 * temporal, 4 * channels), BF16),
            pltpu.SemaphoreType.DMA((6,)),
        ],
        compiler_params=pltpu.CompilerParams(vmem_limit_bytes=VMEM_BYTES),
        cost_estimate=pl.CostEstimate(flops=1024, bytes_accessed=1024, transcendentals=0),
        name="resident_part",
    )(*(pltpu.with_memory_space_constraint(a, pltpu.HBM) for a in (x, w_first, w_second, w_in)))


def mix_kernel(hours_ref, prev_ref, self_ref, next_ref, mix_ref, mixed_ref, w_mix):
    leads = hours_ref.shape[0]
    temporal = mix_ref.shape[1]
    lead = lax.axis_index("lead")
    now = hours_ref[lead]
    before = hours_ref[jnp.maximum(lead - 1, 0)]
    after = hours_ref[jnp.minimum(lead + 1, leads - 1)]

    def gain(gap, used):
        gap = jnp.full((1, 4 * temporal), gap, jnp.int32).astype(F32)
        return jnp.where(used, jnp.exp(-0.5 * (gap - 1.0)), 0.0)

    gain_prev = gain(now - before, lead > 0)
    gain_next = gain(after - now, lead < leads - 1)
    w_mix[...] = jnp.zeros_like(w_mix)
    for k in range(3):
        for s in range(4):
            w_mix[k, pl.ds(s * temporal, temporal), pl.ds(s * temporal, temporal)] = mix_ref[k]
    rows = mixed_ref.shape[0]
    for start in range(0, rows, CHUNK):
        part = pl.ds(start, CHUNK)
        value = gain_prev * dot(prev_ref[part, :], w_mix[0])
        value = value + dot(self_ref[part, :], w_mix[1])
        value = value + gain_next * dot(next_ref[part, :], w_mix[2])
        mixed_ref[part, :] = value.astype(BF16)


def mix_part(hours, before, own, after, w_mix):
    lanes = own.shape[1]
    return pl.pallas_call(
        mix_kernel,
        out_shape=jax.ShapeDtypeStruct(own.shape, BF16),
        in_specs=[pl.BlockSpec(memory_space=pltpu.SMEM)] + in_vmem(4),
        out_specs=in_vmem(1)[0],
        scratch_shapes=[
            pltpu.VMEM((3, lanes, lanes), BF16),
        ],
        compiler_params=pltpu.CompilerParams(vmem_limit_bytes=VMEM_BYTES),
        cost_estimate=pl.CostEstimate(
            flops=6 * own.shape[0] * lanes * lanes, bytes_accessed=1024 * 1024, transcendentals=0
        ),
        name="mix_part",
    )(hours, before, own, after, w_mix)


def rest_kernel(
    place, owner_ref, acc_ref, mixed_ref, x_hbm, w_second_hbm, w_glob_hbm, w_out_hbm, *refs
):
    pieces, refs = refs[:-14], refs[-14:]
    out_hbm, x_ref, w_second_ref, w_glob_ref, w_out_ref, *refs = refs
    out_ref, glob_cells, glob_taps, odd, even, taps, w_lift, cells, sems = refs
    copies = start_copies(
        [
            (w_glob_hbm, w_glob_ref),
            (w_out_hbm, w_out_ref),
            (w_second_hbm, w_second_ref),
            (x_hbm, x_ref),
        ],
        sems,
    )
    height, width, channels = x_ref.shape
    pairs = width // 2
    rows = height * pairs
    out = channels
    temporal = w_out_ref.shape[0]
    lanes = glob_cells.shape[1]
    share = pieces[0].shape[0]
    chunks = rows // CHUNK
    wide = rows // WIDE

    def out_copy(k):
        part = pl.ds(k * (WIDE // pairs), WIDE // pairs)
        return pltpu.make_async_copy(
            out_ref.at[part, :, :], out_hbm.at[part, :, :], sems.at[4 + k]
        )

    clear_edges(glob_taps, pairs)
    clear_edges(taps, pairs)
    w_lift[...] = jnp.zeros_like(w_lift)
    for k, piece in enumerate(pieces):
        base = EDGE + place(owner_ref, k) * (share * pairs)
        for m in range(pairs):
            value = piece[:, pl.ds(m * lanes, lanes)].astype(F32)
            glob_cells[pl.ds(base + m, share, stride=pairs), :] = value
    left, right = column_masks(CHUNK, lanes, pairs)
    lower = lax.broadcasted_iota(jnp.int32, (CHUNK, lanes), 1) < lanes // 2

    def glob_chunk(k):
        start = pl.multiple_of(k * CHUNK, CHUNK)
        here = glob_cells[pl.ds(EDGE + start, CHUNK), :]
        before = jnp.where(left, 0.0, glob_cells[pl.ds(EDGE - 1 + start, CHUNK), :])
        after = jnp.where(right, 0.0, glob_cells[pl.ds(EDGE + 1 + start, CHUNK), :])
        part = pl.ds(pairs + start, CHUNK)
        glob_taps[part, pl.ds(0, lanes)] = here.astype(BF16)
        glob_taps[part, pl.ds(lanes, lanes)] = jnp.where(lower, after, before).astype(BF16)

    looped(chunks, glob_chunk)
    for copy in copies[:2]:
        copy.wait()
    for s in range(2):
        for q in range(2):
            w_lift[
                s, pl.ds((2 * s + q) * temporal, temporal), pl.ds(q * out, out)
            ] = w_out_ref[...]
    left, right = column_masks(WIDE, out, pairs)

    def act_chunk(k):
        start = pl.multiple_of(k * WIDE, WIDE)
        value = acc_ref[pl.ds(start, WIDE), :] + pair_taps(
            glob_taps, w_glob_ref, start, WIDE, pairs
        )
        value = silu(value)
        even[pl.ds(EDGE + start, WIDE), :] = value[:, :out]
        odd[pl.ds(EDGE + start, WIDE), :] = value[:, out:]
        part = pl.ds(pairs + start, WIDE)
        taps[part, pl.ds(out, 2 * out)] = value.astype(BF16)
        before = jnp.where(left, 0.0, odd[pl.ds(EDGE - 1 + start, WIDE), :])
        after = jnp.where(right, 0.0, even[pl.ds(EDGE + 1 + start, WIDE), :])
        taps[part, pl.ds(0, out)] = before.astype(BF16)
        taps[part, pl.ds(3 * out, out)] = after.astype(BF16)

    looped(wide, act_chunk)
    for copy in copies[2:]:
        copy.wait()

    def out_chunk(k):
        start = pl.multiple_of(k * WIDE, WIDE)
        s = lax.div(2 * k, wide)
        value = pair_taps(taps, w_second_ref, start, WIDE, pairs)
        low = pl.multiple_of(start - s * (rows // 2), WIDE)
        value = value + dot(mixed_ref[pl.ds(low, WIDE), :], w_lift[s])
        value = silu(value)
        cells[pl.ds(2 * start, WIDE, stride=2), :] = value[:, :out]
        cells[pl.ds(2 * start + 1, WIDE, stride=2), :] = value[:, out:]
        part = pl.ds(k * (WIDE // pairs), WIDE // pairs)
        value = cells[pl.ds(2 * start, 2 * WIDE), :].reshape(WIDE // pairs, width, channels)
        out_ref[part, :, :] = (x_ref[part, :, :].astype(F32) + value).astype(BF16)
        out_copy(k).start()

    looped(wide, out_chunk)
    for k in range(wide):
        out_copy(k).wait()


def rest_part(place, owner, acc, x, mixed, w_second, w_glob, w_out, pieces):
    height, width, channels = x.shape
    pairs = width // 2
    rows = height * pairs
    lanes = pieces[0].shape[1] // pairs
    loaded = [x, w_second, w_glob, w_out]
    return pl.pallas_call(
        lambda *refs: rest_kernel(place, *refs),
        out_shape=jax.ShapeDtypeStruct(x.shape, BF16),
        in_specs=[pl.BlockSpec(memory_space=pltpu.SMEM)]
        + in_vmem(2)
        + in_hbm(len(loaded))
        + in_vmem(len(pieces)),
        out_specs=in_hbm(1)[0],
        scratch_shapes=[
            *(pltpu.VMEM(a.shape, a.dtype) for a in loaded),
            pltpu.VMEM(x.shape, BF16),
            pltpu.VMEM((rows + 2 * EDGE, lanes), F32),
            pltpu.VMEM((rows + 2 * pairs, 2 * lanes), BF16),
            pltpu.VMEM((rows + 2 * EDGE, channels), F32),
            pltpu.VMEM((rows + 2 * EDGE, channels), F32),
            pltpu.VMEM((rows + 2 * pairs, 4 * channels), BF16),
            pltpu.VMEM((2, mixed.shape[1], 2 * channels), BF16),
            pltpu.VMEM((2 * rows, channels), F32),
            pltpu.SemaphoreType.DMA((4 + rows // WIDE,)),
        ],
        compiler_params=pltpu.CompilerParams(vmem_limit_bytes=VMEM_BYTES),
        cost_estimate=pl.CostEstimate(
            flops=4 * rows * 12 * channels * 2 * channels,
            bytes_accessed=8 * 1024 * 1024,
            transcendentals=0,
        ),
        name="rest_part",
    )(
        owner,
        pltpu.with_memory_space_constraint(acc, pltpu.VMEM),
        mixed,
        *(pltpu.with_memory_space_constraint(a, pltpu.HBM) for a in loaded),
        *pieces,
    )


def rotated(block, axis, distance):
    count = lax.axis_size(axis)
    return lax.ppermute(block, axis, [(i, (i + distance) % count) for i in range(count)])


def swapped(block, bit):
    count = lax.axis_size("patch")
    return lax.ppermute(block, "patch", [(i, i ^ bit) for i in range(count)])


def spread(block, owner, early):
    away = lax.axis_index("patch") ^ owner[lax.axis_index("lead")]
    near, beside = (away & 1) == 0, (away & 2) == 0
    half = block.shape[0] // 2
    share = half // (2 * GROUPS)
    arrived, early = lax.optimization_barrier((swapped(block[half:], 1), early))
    pieces = []
    for g in range(GROUPS):
        rows = slice(2 * g * share, 2 * (g + 1) * share)
        part = jnp.where(near, block[rows], arrived[rows])
        own = jnp.where(beside, part[:share], swapped(part[share:], 2))
        across = swapped(own, 2)
        pieces += [own, swapped(own, 1), across, swapped(across, 1)]
    return pieces, early


def piece_place(owner_ref, k):
    away = lax.axis_index("patch") ^ owner_ref[lax.axis_index("lead")] ^ (k % 4)
    return (away & 1) * (2 * GROUPS) + 2 * (k // 4) + (away >> 1)


def whole_place(owner_ref, k):
    return 0


def per_device(
    features, context, owner, hours, w_first, w_second, w_lead_in, w_lead_mix, w_lead_out
):
    resident = features[0, 0]
    height = resident.shape[0]
    count = lax.axis_size("patch")
    acc, proj, w_second, w_glob = resident_part(resident, w_first, w_second, w_lead_in)
    constants = (w_second, w_glob, w_lead_out)

    def mixed_with(proj):
        return mix_part(
            hours, rotated(proj, "lead", 1), proj, rotated(proj, "lead", -1), w_lead_mix
        )

    if count == 4:
        pieces, proj = spread(context[0, 0], owner, proj)
        place = piece_place
    else:
        mine = lax.axis_index("patch") == owner[lax.axis_index("lead")]
        block = jnp.where(mine, context[0, 0], jnp.zeros_like(context[0, 0]))
        pieces, place = [lax.psum(block, "patch")], whole_place
    result = rest_part(place, owner, acc, resident, mixed_with(proj), *constants, pieces)
    return result[None, None]


def solution(mesh):
    placed = (
        P(("grp", "lead"), "patch", None, None, None),
        P("patch", ("grp", "lead"), None, None),
        P("grp"),
        P("grp"),
        P(),
        P(),
        P(),
        P(),
        P(),
    )
    return jax.shard_map(
        per_device,
        mesh=mesh,
        in_specs=placed,
        out_specs=P(("grp", "lead"), "patch", None, None, None),
        check_vma=False,
    )
```

time: 56.4 us -> 39.6 us (0.70)
  local copies, waits for them, and re-layouts: 11.5 us -> 1.65 us
  waiting for transfers between devices: 19.2 us -> 14.5 us
  starting transfers between devices: 13.4 us -> 10 us
  Pallas kernels: 11.8 us -> 12.5 us
  between operations: 0.1 us -> 0.77 us
    ppermute x6 -> x2, waiting for transfers between devices: 19.1 us -> 0.01 us  [rotated(): lax.ppermute(block, axis, [(i, (i + distance) % count) for i in range(cou...]
    ppermute x2 -> x5, waiting for transfers between devices: 0.01 us -> 14.5 us  [swapped(): return lax.ppermute(block, 'patch', [(i, i ^ bit) for i in range(count)])]
    unnamed x35 -> x8, local copies, waits for them, and re-layouts: 10.8 us -> 0.01 us
    ppermute x6 -> x2, starting transfers between devices: 8.92 us -> 0.51 us  [rotated(): lax.ppermute(block, axis, [(i, (i + distance) % count) for i in range(cou...]
    ppermute x2 -> x5, starting transfers between devices: 4.47 us -> 9.5 us  [swapped(): return lax.ppermute(block, 'patch', [(i, i ^ bit) for i in range(count)])]
    pallas_call x1, Pallas kernels: 5.24 us -> 6.4 us  [rest_part(): pl.pallas_call(lambda *refs: rest_kernel(place, *refs), out_shape=jax.Sha...]
    dynamic_slice x0 -> x1, local copies, waits for them, and re-layouts: none -> 0.59 us  [spread(): away = lax.axis_index('patch') ^ owner[lax.axis_index('lead')]]
    pallas_call x3 -> x2, Pallas kernels: 6.51 us -> 6.12 us  [the longest x1 5.13 us: resident_part(): pl.pallas_call(resident_kernel, out_shape=tuple((space(*kind) for space,...]
  transfers between devices with their start and end apart: 8 -> 7, of which waited for: 4 -> 3; matrix products, arithmetic and copies ran while one was open for 1% -> 2% of each run, Pallas kernels for 7% -> 15%
where the time goes in v2:
time: 39.6 us; the launch traced here: 39.5 us
  waiting for transfers between devices  14.5 us (37%)
  Pallas kernels  12.5 us (32%)
  starting transfers between devices  10 us (25%)
  local copies, waits for them, and re-layouts  1.65 us (4%)
  between operations  0.77 us (2%)
    ppermute x5, waiting for transfers between devices, swapped(): return lax.ppermute(block, 'patch', [(i, i ^ bit) for i in range(count)])  14.5 us
    ppermute x5, starting transfers between devices, swapped(): return lax.ppermute(block, 'patch', [(i, i ^ bit) for i in range(count)])  9.5 us
    pallas_call x1, Pallas kernels, rest_part(): pl.pallas_call(lambda *refs: rest_kernel(place, *refs), out_shape=jax.Sha...  6.4 us
    pallas_call x1, Pallas kernels, resident_part(): pl.pallas_call(resident_kernel, out_shape=tuple((space(*kind) for space,...  5.13 us
    slice x1, local copies, waits for them, and re-layouts, spread(): arrived, early = lax.optimization_barrier((swapped(block[half:], 1), early))  1.03 us
    pallas_call x1, Pallas kernels, mix_part(): pl.pallas_call(mix_kernel, out_shape=jax.ShapeDtypeStruct(own.shape, BF16...  0.99 us
  transfers between devices with their start and end apart: 7, of which 3 were waited for; matrix products, arithmetic and copies ran while one was open for 2% of the time, Pallas kernels for 15%

profile of v2, /device:TPU:0, one launch (start us, length us, event | category | flops | bytes accessed | tf_op | source)
XLA Modules:
  0.0 39.5 jit_solution(17484120255183121809)
XLA Ops:
  0.0 0.0 copy-start.3
  0.0 1.0 %slice_bitcast_fusion = bf16[64,2048]{1,0:T(8,128)(2,1)S(1)} fusion(bf16[1,1,128,2048]{3,2,1,0:T(8,128)(2,1)} %param.10), kind=kLoop, calls=%fused_computation.1 | loop fusion | bytes 524288 | tf_op jit(solution)/shard_map/slice | solution.py:383
  1.0 3.1 %collective-permute-start = (bf16[64,2048]{1,0:T(8,128)(2,1)S(1)}, bf16[64,2048]{1,0:T(8,128)(2,1)S(1)}, u32[]{:S(2)}, u32[]{:S(2)}) collective-permute-start(bf16[64,2048]{1,0:T(8,128)(2,1)S(1)} %slice_bitcast_fusion), channel_id=1, source_target_pairs={{0,4},{4,0},{8,12},{12,8},{1,5},{5,1},{9,13},{13,9},{2,6},{6,2},{1... | collective-permute-start | bytes 786440 | tf_op jit(solution)/shard_map/ppermute | solution.py:375
  4.1 5.1 %resident_part.1 = (f32[2048,256]{1,0:T(8,128)S(1)}, bf16[1024,128]{1,0:T(8,128)(2,1)S(1)}, bf16[1536,256]{1,0:T(8,128)(2,1)}, bf16[768,256]{1,0:T(8,128)(2,1)}) custom-call(bf16[128,32,128]{2,1,0:T(8,128)(2,1)} %bitcast.8, bf16[9,192,128]{2,1,0:T(8,128)(2,1)} %first_hbm.1, bf16[9,128,128]{2,1,0:T(8,128)(2,1)} %second_hbm.1, bf16[32,128]{1,0:T(8,128)(2,1)} %bitcast.10), custom_call_target="tpu_custom_call" | custom-call | flops 1024 | bytes 1024 | tf_op jit(solution)/shard_map/resident_part/pallas_call | solution.py:156
  9.3 0.0 copy-done.2
  9.3 0.6 %dynamic_slice.3 = s32[1]{0:T(128)} dynamic-slice(s32[4]{0:T(128)S(1)} %copy-done.2, s32[]{:T(128)S(6)} %select_n.19), dynamic_slice_sizes={1} | dynamic-slice | bytes 12 | tf_op jit(solution)/shard_map/dynamic_slice | solution.py:379
  10.5 0.0 collective-permute-done
  10.5 0.0 copy-done.3
  10.6 2.7 %collective-permute-start.3 = (bf16[32,2048]{1,0:T(8,128)(2,1)S(1)}, bf16[32,2048]{1,0:T(8,128)(2,1)S(1)}, u32[]{:S(2)}, u32[]{:S(2)}) collective-permute-start(bf16[32,2048]{1,0:T(8,128)(2,1)S(1)} %slice.25), channel_id=1, source_target_pairs={{0,8},{4,12},{8,0},{12,4},{1,9},{5,13},{9,1},{13,5},{2,10},{6,14},... | collective-permute-start | bytes 393224 | tf_op jit(solution)/shard_map/ppermute | solution.py:375
  13.3 0.3 collective-permute-start.2
  13.6 0.2 collective-permute-start.1
  13.8 5.5 %collective-permute-done.3 = bf16[32,2048]{1,0:T(8,128)(2,1)S(1)} collective-permute-done((bf16[32,2048]{1,0:T(8,128)(2,1)S(1)}, bf16[32,2048]{1,0:T(8,128)(2,1)S(1)}, u32[]{:S(2)}, u32[]{:S(2)}) %collective-permute-start.3) | collective-permute-done | bytes 131104 | tf_op jit(solution)/shard_map/ppermute | solution.py:375
  19.3 0.1 collective-permute-start.5
  19.4 3.6 %collective-permute-start.4 = (bf16[32,2048]{1,0:T(8,128)(2,1)S(1)}, bf16[32,2048]{1,0:T(8,128)(2,1)S(1)}, u32[]{:S(2)}, u32[]{:S(2)}) collective-permute-start(bf16[32,2048]{1,0:T(8,128)(2,1)S(1)} %slice_select_fusion.refs_7_), channel_id=1, source_target_pairs={{0,4},{4,0},{8,12},{12,8},{1,5},{5,1},{9,13},{13,9},{2,6},{6,2},{1... | collective-permute-start | bytes 393224 | tf_op jit(solution)/shard_map/ppermute | solution.py:375
  23.0 5.0 %collective-permute-done.5.refs_9_ = bf16[32,2048]{1,0:T(8,128)(2,1)S(1)} collective-permute-done((bf16[32,2048]{1,0:T(8,128)(2,1)S(1)}, bf16[32,2048]{1,0:T(8,128)(2,1)S(1)}, u32[]{:S(2)}, u32[]{:S(2)}) %collective-permute-start.5) | collective-permute-done | bytes 131104 | tf_op jit(solution)/shard_map/ppermute | solution.py:375
  28.1 0.0 collective-permute-start.6
  28.1 0.0 collective-permute-done.2.next_ref
  28.1 0.0 collective-permute-done.1.prev_ref
  28.1 0.0 copy-done
  28.1 0.0 copy-done.1
  28.1 1.0 %mix_part.1.refs_2_ = bf16[1024,128]{1,0:T(8,128)(2,1)S(1)} custom-call(s32[4]{0:T(128)S(1)} %copy-done.1, bf16[1024,128]{1,0:T(8,128)(2,1)S(1)} %collective-permute-done.1.prev_ref, bf16[1024,128]{1,0:T(8,128)(2,1)S(1)} %get-tuple-element.13.self_ref, bf16[1024,128]{1,0:T(8,128)(2,1)S(1)} %collective-permute-done.2.next_ref, bf16[3,32,32]{2,1,0:T(8,128)(2,1)S(1)} %copy-done), custom_call_target="tpu_custom_call" | custom-call | flops 100663296 | bytes 1048576 | tf_op jit(solution)/shard_map/mix_part/pallas_call | solution.py:211
  29.1 0.0 collective-permute-done.4.refs_8_
  29.1 3.9 %collective-permute-done.6.refs_10_ = bf16[32,2048]{1,0:T(8,128)(2,1)S(1)} collective-permute-done((bf16[32,2048]{1,0:T(8,128)(2,1)S(1)}, bf16[32,2048]{1,0:T(8,128)(2,1)S(1)}, u32[]{:S(2)}, u32[]{:S(2)}) %collective-permute-start.6) | collective-permute-done | bytes 131104 | tf_op jit(solution)/shard_map/ppermute | solution.py:375
  33.1 6.4 %rest_part.1 = bf16[128,32,128]{2,1,0:T(8,128)(2,1)} custom-call(s32[4]{0:T(128)S(1)} %copy-done.2, f32[2048,256]{1,0:T(8,128)S(1)} %get-tuple-element.11.refs_1_, bf16[1024,128]{1,0:T(8,128)(2,1)S(1)} %mix_part.1.refs_2_, bf16[128,32,128]{2,1,0:T(8,128)(2,1)} %bitcast.9, bf16[1536,256]{1,0:T(8,128)(2,1)} %get-tuple-element.14.refs_4_, ...), custom_call_target="tpu_custom_call" | custom-call | flops 3221225472 | bytes 8388608 | tf_op jit(solution)/shard_map/rest_part/pallas_call | solution.py:332
  (6 shorter events, 0.1 us)
Async XLA Ops:
  0.0 10.5 %copy-start.3 = (bf16[1,1,128,2048]{3,2,1,0:T(8,128)(2,1)S(1)}, bf16[1,1,128,2048]{3,2,1,0:T(8,128)(2,1)}, u32[]{:S(2)}) copy-start(bf16[1,1,128,2048]{3,2,1,0:T(8,128)(2,1)} %param.10) | copy-start | bytes 1572868
  0.0 9.3 %copy-start.2 = (s32[4]{0:T(128)S(1)}, s32[4]{0:T(128)}, u32[]{:S(2)}) copy-start(s32[4]{0:T(128)} %refs_0_.1) | copy-start | bytes 52
  0.0 28.1 %copy-start = (bf16[3,32,32]{2,1,0:T(8,128)(2,1)S(1)}, bf16[3,32,32]{2,1,0:T(8,128)(2,1)}, u32[]{:S(2)}) copy-start(bf16[3,32,32]{2,1,0:T(8,128)(2,1)} %mix_ref.1) | copy-start | bytes 18436
  0.0 28.1 %copy-start.1 = (s32[4]{0:T(128)S(1)}, s32[4]{0:T(128)}, u32[]{:S(2)}) copy-start(s32[4]{0:T(128)} %hours_ref.1) | copy-start | bytes 52
  1.0 9.5 %collective-permute-start = (bf16[64,2048]{1,0:T(8,128)(2,1)S(1)}, bf16[64,2048]{1,0:T(8,128)(2,1)S(1)}, u32[]{:S(2)}, u32[]{:S(2)}) collective-permute-start(bf16[64,2048]{1,0:T(8,128)(2,1)S(1)} %slice_bitcast_fusion), channel_id=1, source_target_pairs={{0,4},{4,0},{8,12},{12,8},{1,5},{5,1},{9,13},{13,9},{2,6},{6,2},{1... | collective-permute-start | bytes 786440 | tf_op jit(solution)/shard_map/ppermute | solution.py:375
  10.6 8.7 %collective-permute-start.3 = (bf16[32,2048]{1,0:T(8,128)(2,1)S(1)}, bf16[32,2048]{1,0:T(8,128)(2,1)S(1)}, u32[]{:S(2)}, u32[]{:S(2)}) collective-permute-start(bf16[32,2048]{1,0:T(8,128)(2,1)S(1)} %slice.25), channel_id=1, source_target_pairs={{0,8},{4,12},{8,0},{12,4},{1,9},{5,13},{9,1},{13,5},{2,10},{6,14},... | collective-permute-start | bytes 393224 | tf_op jit(solution)/shard_map/ppermute | solution.py:375
  13.3 14.8 %collective-permute-start.2 = (bf16[1024,128]{1,0:T(8,128)(2,1)S(1)}, bf16[1024,128]{1,0:T(8,128)(2,1)S(1)}, u32[]{:S(2)}, u32[]{:S(2)}) collective-permute-start(bf16[1024,128]{1,0:T(8,128)(2,1)S(1)} %get-tuple-element.13.self_ref), channel_id=1, source_target_pairs={{0,3},{1,0},{2,1},{3,2},{4,7},{5,4},{6,5},{7,6},{8,11},{9,8},{10,9... | collective-permute-start | bytes 786440 | tf_op jit(solution)/shard_map/ppermute | solution.py:370
  13.6 14.5 %collective-permute-start.1 = (bf16[1024,128]{1,0:T(8,128)(2,1)S(1)}, bf16[1024,128]{1,0:T(8,128)(2,1)S(1)}, u32[]{:S(2)}, u32[]{:S(2)}) collective-permute-start(bf16[1024,128]{1,0:T(8,128)(2,1)S(1)} %get-tuple-element.13.self_ref), channel_id=1, source_target_pairs={{0,1},{1,2},{2,3},{3,0},{4,5},{5,6},{6,7},{7,4},{8,9},{9,10},{10,1... | collective-permute-start | bytes 786440 | tf_op jit(solution)/shard_map/ppermute | solution.py:370
  19.3 8.8 %collective-permute-start.5 = (bf16[32,2048]{1,0:T(8,128)(2,1)S(1)}, bf16[32,2048]{1,0:T(8,128)(2,1)S(1)}, u32[]{:S(2)}, u32[]{:S(2)}) collective-permute-start(bf16[32,2048]{1,0:T(8,128)(2,1)S(1)} %slice_select_fusion.refs_7_), channel_id=1, source_target_pairs={{0,8},{4,12},{8,0},{12,4},{1,9},{5,13},{9,1},{13,5},{2,10},{6,14},... | collective-permute-start | bytes 393224 | tf_op jit(solution)/shard_map/ppermute | solution.py:375
  19.4 9.7 %collective-permute-start.4 = (bf16[32,2048]{1,0:T(8,128)(2,1)S(1)}, bf16[32,2048]{1,0:T(8,128)(2,1)S(1)}, u32[]{:S(2)}, u32[]{:S(2)}) collective-permute-start(bf16[32,2048]{1,0:T(8,128)(2,1)S(1)} %slice_select_fusion.refs_7_), channel_id=1, source_target_pairs={{0,4},{4,0},{8,12},{12,8},{1,5},{5,1},{9,13},{13,9},{2,6},{6,2},{1... | collective-permute-start | bytes 393224 | tf_op jit(solution)/shard_map/ppermute | solution.py:375
  28.1 5.0 %collective-permute-start.6 = (bf16[32,2048]{1,0:T(8,128)(2,1)S(1)}, bf16[32,2048]{1,0:T(8,128)(2,1)S(1)}, u32[]{:S(2)}, u32[]{:S(2)}) collective-permute-start(bf16[32,2048]{1,0:T(8,128)(2,1)S(1)} %collective-permute-done.5.refs_9_), channel_id=1, source_target_pairs={{0,4},{4,0},{8,12},{12,8},{1,5},{5,1},{9,13},{13,9},{2,6},{6,2},{1... | collective-permute-start | bytes 393224 | tf_op jit(solution)/shard_map/ppermute | solution.py:375

commit v3 on v2

v3 whole, which is shorter than its diff:
```python
import jax
import jax.numpy as jnp
from jax import lax
from jax.experimental import pallas as pl
from jax.experimental.pallas import tpu as pltpu
from jax.sharding import PartitionSpec as P

BF16 = jnp.bfloat16
F32 = jnp.float32
EDGE = 8
CHUNK = 256
WIDE = 1024
GROUPS = 1
VMEM_BYTES = 20 * 1024 * 1024


def silu(v):
    return 0.5 * v * (1.0 + jnp.tanh(0.5 * v))


def dot(a, b):
    return jnp.dot(a, b, preferred_element_type=F32)


def dot_transposed(a, b):
    return lax.dot_general(a, b, (((1,), (1,)), ((), ())), preferred_element_type=F32)


def in_vmem(count):
    return [pl.BlockSpec(memory_space=pltpu.VMEM)] * count


def at_hbm(*arrays):
    return [pltpu.with_memory_space_constraint(a, pltpu.HBM) for a in arrays]


def in_hbm(count):
    return [pl.BlockSpec(memory_space=pltpu.HBM)] * count


def start_copies(pairs, sems):
    copies = [
        pltpu.make_async_copy(source, target, sems.at[k])
        for k, (source, target) in enumerate(pairs)
    ]
    for copy in copies:
        copy.start()
    return copies


def put_pair_weights(target, weights, first, depth, offsets):
    out = weights.shape[2]
    span = depth * len(offsets)
    for a in range(3):
        for place, d in enumerate(offsets):
            rows = pl.ds(a * span + place * depth, depth)
            for q in range(2):
                b = d - q + 1
                lanes = pl.ds(q * out, out)
                if 0 <= b <= 2:
                    target[rows, lanes] = weights[3 * a + b, pl.ds(first, depth), :]
                else:
                    target[rows, lanes] = jnp.zeros((depth, out), target.dtype)


def clear_edges(ref, pairs):
    zero = jnp.zeros((pairs, ref.shape[1]), ref.dtype)
    ref[pl.ds(0, pairs), :] = zero
    ref[pl.ds(ref.shape[0] - pairs, pairs), :] = zero


def pair_taps(taps, weights, start, size, pairs):
    depth = taps.shape[1]
    total = dot(taps[pl.ds(start, size), :], weights[pl.ds(0, depth), :])
    for a in range(1, 3):
        total += dot(
            taps[pl.ds(start + a * pairs, size), :], weights[pl.ds(a * depth, depth), :]
        )
    return total


def column_masks(size, lanes, pairs):
    m = lax.rem(lax.broadcasted_iota(jnp.int32, (size, lanes), 0), pairs)
    return m == 0, m == pairs - 1


def looped(count, body):
    lax.fori_loop(0, count, lambda k, carry: (body(k), carry)[1], 0)


def patches_away(owner_ref):
    return lax.axis_index("patch") ^ owner_ref[lax.axis_index("lead")]


def resident_kernel(
    owner_ref, x_hbm, first_hbm, second_hbm, w_in_hbm, block_hbm,
    acc_ref, proj_ref, flags_ref, block_ref, w_second_hbm, w_glob_hbm,
    x_ref, first_ref, second_ref, in_ref, w_second_ref, w_glob_ref, cells, taps, w_first, w_in, sems,
):
    height, width, channels = x_ref.shape
    pairs = width // 2
    rows = height * pairs
    temporal = in_ref.shape[0]
    glob = first_ref.shape[1] - channels
    parts = 4
    step = height // parts
    slices = [pl.ds(k * step, step) for k in range(parts)]
    copies = start_copies(
        [(x_hbm.at[part, :, :], x_ref.at[part, :, :]) for part in slices]
        + [
            (w_in_hbm, in_ref),
            (first_hbm, first_ref),
            (second_hbm, second_ref),
            (block_hbm.at[pl.ds(0, block_ref.shape[0]), :], block_ref),
        ],
        sems,
    )
    away = patches_away(owner_ref)
    flags_ref[0] = jnp.full(flags_ref.shape[1:], away & 1, jnp.int32)
    flags_ref[1] = jnp.full(flags_ref.shape[1:], away & 2, jnp.int32)
    clear_edges(taps, pairs)
    w_in[...] = jnp.zeros_like(w_in)
    left, right = column_masks(CHUNK, channels, pairs)
    for k in range(parts):
        copies[k].wait()
        for start in range(k * step * pairs, (k + 1) * step * pairs, CHUNK):
            part = x_ref[pl.ds(start // pairs, CHUNK // pairs), :, :].astype(F32)
            cells[pl.ds(EDGE + 2 * start, 2 * CHUNK), :] = part.reshape(2 * CHUNK, channels)
            for place, d in enumerate((-1, 0, 1, 2)):
                value = cells[pl.ds(EDGE + 2 * start + d, CHUNK, stride=2), :]
                if d == -1:
                    value = jnp.where(left, 0.0, value)
                if d == 2:
                    value = jnp.where(right, 0.0, value)
                taps[pl.ds(pairs + start, CHUNK), pl.ds(place * channels, channels)] = value.astype(
                    BF16
                )
    half = rows // 2
    copies[parts].wait()
    for s in range(4):
        w_in[pl.ds(s * temporal, temporal), pl.ds(s * channels, channels)] = in_ref[...]
    for start in range(0, half, CHUNK):
        value = dot_transposed(
            taps[pl.ds(pairs + start, CHUNK), pl.ds(channels, 2 * channels)],
            w_in[:, pl.ds(0, 2 * channels)],
        ) + dot_transposed(
            taps[pl.ds(pairs + half + start, CHUNK), pl.ds(channels, 2 * channels)],
            w_in[:, pl.ds(2 * channels, 2 * channels)],
        )
        proj_ref[pl.ds(start, CHUNK), :] = value.astype(BF16)
    copies[parts + 1].wait()
    put_pair_weights(w_first, first_ref, 0, channels, (-1, 0, 1, 2))
    put_pair_weights(w_glob_ref, first_ref, channels, glob, (0, 1, 2, -1))
    copies[parts + 2].wait()
    put_pair_weights(w_second_ref, second_ref, 0, channels, (-1, 0, 1, 2))
    writes = start_copies(
        [(w_glob_ref, w_glob_hbm), (w_second_ref, w_second_hbm)], sems.at[pl.ds(parts + 4, 2)]
    )
    for start in range(0, rows, WIDE):
        acc_ref[pl.ds(start, WIDE), :] = pair_taps(taps, w_first, start, WIDE, pairs)
    for write in [*writes, copies[parts + 3]]:
        write.wait()


def resident_part(owner, x, w_first, w_second, w_in, block):
    height, width, channels = x.shape
    out = w_first.shape[2]
    temporal = w_in.shape[1]
    w_in = w_in.T
    glob = w_first.shape[1] - channels
    pairs = width // 2
    rows = height * pairs
    results = (
        ((rows, 2 * out), F32),
        ((rows // 2, 4 * temporal), BF16),
        ((2, 1, width * glob), jnp.int32),
        ((height // 2, width * glob), BF16),
        ((12 * out, 2 * out), BF16),
        ((12 * glob, 2 * out), BF16),
    )
    return pl.pallas_call(
        resident_kernel,
        out_shape=tuple(
            space(*kind) for space, kind in zip((pltpu.VMEM,) * 4 + (pltpu.HBM,) * 2, results)
        ),
        in_specs=[pl.BlockSpec(memory_space=pltpu.SMEM)] + in_hbm(5),
        out_specs=tuple(in_vmem(4) + in_hbm(2)),
        scratch_shapes=[
            pltpu.VMEM(x.shape, BF16),
            pltpu.VMEM(w_first.shape, BF16),
            pltpu.VMEM(w_second.shape, BF16),
            pltpu.VMEM(w_in.shape, BF16),
            pltpu.VMEM(*results[4]),
            pltpu.VMEM(*results[5]),
            pltpu.VMEM((2 * rows + 2 * EDGE, channels), F32),
            pltpu.VMEM((rows + 2 * pairs, 4 * channels), BF16),
            pltpu.VMEM((12 * channels, 2 * out), BF16),
            pltpu.VMEM((4 * temporal, 4 * channels), BF16),
            pltpu.SemaphoreType.DMA((10,)),
        ],
        compiler_params=pltpu.CompilerParams(vmem_limit_bytes=VMEM_BYTES),
        cost_estimate=pl.CostEstimate(flops=1024, bytes_accessed=1024, transcendentals=0),
        name="resident_part",
    )(*at_hbm(owner, x, w_first, w_second, w_in, block))


def mix_kernel(
    hours_ref, prev_ref, self_ref, next_ref, mix_ref, out_ref, x_hbm, w_second_hbm, w_glob_hbm,
    lifted_ref, x_ref, w_second_ref, w_glob_ref, w_mix, w_lift, mixed_ref, sems,
):
    copies = start_copies(
        [(w_glob_hbm, w_glob_ref), (w_second_hbm, w_second_ref), (x_hbm, x_ref)], sems
    )
    leads = hours_ref.shape[0]
    temporal = mix_ref.shape[1]
    lead = lax.axis_index("lead")
    now = hours_ref[lead]
    before = hours_ref[jnp.maximum(lead - 1, 0)]
    after = hours_ref[jnp.minimum(lead + 1, leads - 1)]

    def gain(gap, used):
        gap = jnp.full((1, 4 * temporal), gap, jnp.int32).astype(F32)
        return jnp.where(used, jnp.exp(-0.5 * (gap - 1.0)), 0.0)

    gain_prev = gain(now - before, lead > 0)
    gain_next = gain(after - now, lead < leads - 1)
    w_mix[...] = jnp.zeros_like(w_mix)
    for k in range(3):
        for s in range(4):
            w_mix[k, pl.ds(s * temporal, temporal), pl.ds(s * temporal, temporal)] = mix_ref[k]
    rows, out = mixed_ref.shape[0], out_ref.shape[1]
    w_lift[...] = jnp.zeros_like(w_lift)
    for s in range(2):
        for q in range(2):
            w_lift[
                s, pl.ds((2 * s + q) * temporal, temporal), pl.ds(q * out, out)
            ] = out_ref[...]
    for start in range(0, rows, CHUNK):
        part = pl.ds(start, CHUNK)
        value = gain_prev * dot(prev_ref[part, :], w_mix[0])
        value = value + dot(self_ref[part, :], w_mix[1])
        value = value + gain_next * dot(next_ref[part, :], w_mix[2])
        mixed_ref[part, :] = value.astype(BF16)
    for s in range(2):
        lifted_ref[pl.ds(s * rows, rows), :] = dot(mixed_ref[...], w_lift[s])
    for copy in copies:
        copy.wait()


def mix_part(hours, before, own, after, w_mix, w_out, moved):
    lanes, out = own.shape[1], w_out.shape[1]
    return pl.pallas_call(
        mix_kernel,
        out_shape=(
            pltpu.VMEM((2 * own.shape[0], 2 * out), F32),
            *(pltpu.VMEM(a.shape, a.dtype) for a in moved),
        ),
        in_specs=[pl.BlockSpec(memory_space=pltpu.SMEM)] + in_vmem(5) + in_hbm(len(moved)),
        out_specs=tuple(in_vmem(1 + len(moved))),
        scratch_shapes=[
            pltpu.VMEM((3, lanes, lanes), BF16),
            pltpu.VMEM((2, lanes, 2 * out), BF16),
            pltpu.VMEM(own.shape, BF16),
            pltpu.SemaphoreType.DMA((len(moved),)),
        ],
        compiler_params=pltpu.CompilerParams(vmem_limit_bytes=VMEM_BYTES),
        cost_estimate=pl.CostEstimate(
            flops=6 * own.shape[0] * lanes * lanes, bytes_accessed=1024 * 1024, transcendentals=0
        ),
        name="mix_part",
    )(hours, before, own, after, w_mix, w_out, *at_hbm(*moved))


def row_parts(rows, pairs):
    count = max(1, rows * pairs // WIDE)
    bounds = [rows * k // count for k in range(count + 1)]
    return [(low, high - low) for low, high in zip(bounds, bounds[1:])]


def rest_kernel(second, side_of, place, owner_ref, acc_ref, lifted_ref, *refs):
    x_ref, w_second_ref, w_glob_ref, *refs = refs
    middle, refs = refs[:-8], refs[-8:]
    out_ref, glob_cells, glob_taps, odd, even, taps, cells, sems = refs
    if second:
        *pieces, glob_edge, taps_edge, _, out_hbm = middle
    else:
        *pieces, out_hbm, glob_edge, taps_edge = middle
    rows, width, channels = out_ref.shape
    pairs = width // 2
    out = channels
    lanes = glob_cells.shape[1]
    share = pieces[0].shape[0]
    half = share * len(pieces)
    side = side_of(owner_ref)
    first = (1 - side) * (half - 2) if second else side * half
    act_first = (1 - side) * (half - 1) if second else side * half
    act_rows = half + 1 if second else half
    act_place = 2 - side if second else 1
    new_place = 3 - 2 * side if second else 1

    def at(row):
        return pl.multiple_of(row * pairs, pairs)

    clear_edges(glob_taps, pairs)
    clear_edges(taps, pairs)
    for k, piece in enumerate(pieces):
        base = EDGE + at(place(owner_ref, k) * share)
        for m in range(pairs):
            value = piece[:, pl.ds(m * lanes, lanes)].astype(F32)
            glob_cells[pl.ds(base + m, share, stride=pairs), :] = value
    left, right = column_masks(CHUNK, lanes, pairs)
    lower = lax.broadcasted_iota(jnp.int32, (CHUNK, lanes), 1) < lanes // 2
    for start in range(0, half * pairs, CHUNK):
        here = glob_cells[pl.ds(EDGE + start, CHUNK), :]
        before = jnp.where(left, 0.0, glob_cells[pl.ds(EDGE - 1 + start, CHUNK), :])
        after = jnp.where(right, 0.0, glob_cells[pl.ds(EDGE + 1 + start, CHUNK), :])
        part = pl.ds(at(new_place + start // pairs), CHUNK)
        glob_taps[part, pl.ds(0, lanes)] = here.astype(BF16)
        glob_taps[part, pl.ds(lanes, lanes)] = jnp.where(lower, after, before).astype(BF16)
    if second:
        glob_taps[pl.ds(at(1 + half * side), 2 * pairs), :] = glob_edge[...]
        taps[pl.ds(at((half + 2) * side), 2 * pairs), :] = taps_edge[...]
    for low, count in row_parts(act_rows, pairs):
        size = count * pairs
        start = EDGE + low * pairs
        left, right = column_masks(size, out, pairs)
        value = acc_ref[pl.ds(at(act_first + low), size), :] + pair_taps(
            glob_taps, w_glob_ref, at(act_place + low - 1), size, pairs
        )
        value = silu(value)
        even[pl.ds(start, size), :] = value[:, :out]
        odd[pl.ds(start, size), :] = value[:, out:]
        part = pl.ds(at(act_place + low), size)
        taps[part, pl.ds(out, 2 * out)] = value.astype(BF16)
        before = jnp.where(left, 0.0, odd[pl.ds(start - 1, size), :])
        after = jnp.where(right, 0.0, even[pl.ds(start + 1, size), :])
        taps[part, pl.ds(0, out)] = before.astype(BF16)
        taps[part, pl.ds(3 * out, out)] = after.astype(BF16)
    if not second:
        glob_edge[...] = glob_taps[pl.ds(at(1 + (half - 2) * (1 - side)), 2 * pairs), :]
        taps_edge[...] = taps[pl.ds(at(2 + (half - 4) * (1 - side)), 2 * pairs), :]
    writes = []
    for low, count in row_parts(rows, pairs):
        size = count * pairs
        value = pair_taps(taps, w_second_ref, low * pairs, size, pairs)
        value = silu(value + lifted_ref[pl.ds(at(first + low), size), :])
        start = 2 * low * pairs
        cells[pl.ds(start, size, stride=2), :] = value[:, :out]
        cells[pl.ds(start + 1, size, stride=2), :] = value[:, out:]
        for here, count in ((low, count // 2), (low + count // 2, count - count // 2)):
            part = pl.ds(here, count)
            value = cells[pl.ds(here * width, count * width), :].reshape(count, width, channels)
            resident = x_ref[pl.ds(first + here, count), :, :].astype(F32)
            out_ref[part, :, :] = (resident + value).astype(BF16)
            writes += start_copies(
                [(out_ref.at[part, :, :], out_hbm.at[pl.ds(first + here, count), :, :])],
                sems.at[pl.ds(len(writes), 1)],
            )
    for write in writes:
        write.wait()


def rest_part(second, side_of, place, owner, acc, lifted, x, w_second, w_glob, pieces, carried):
    _, width, channels = x.shape
    pairs = width // 2
    lanes = pieces[0].shape[1] // pairs
    half = pieces[0].shape[0] * len(pieces)
    rows = half + 2 if second else half
    space = pltpu.with_memory_space_constraint
    results = (pltpu.HBM(x.shape, BF16),)
    if not second:
        results += (
            pltpu.VMEM((2 * pairs, 2 * lanes), BF16),
            pltpu.VMEM((2 * pairs, 4 * channels), BF16),
        )
    return pl.pallas_call(
        lambda *refs: rest_kernel(second, side_of, place, *refs),
        out_shape=results,
        in_specs=[pl.BlockSpec(memory_space=pltpu.SMEM)]
        + in_vmem(5 + len(pieces))
        + (in_vmem(2) + in_hbm(1) if second else []),
        out_specs=tuple(in_hbm(1) + in_vmem(len(results) - 1)),
        input_output_aliases={8 + len(pieces): 0} if second else {},
        scratch_shapes=[
            pltpu.VMEM((rows, width, channels), BF16),
            pltpu.VMEM((half * pairs + 2 * EDGE, lanes), F32),
            pltpu.VMEM(((rows + 2) * pairs, 2 * lanes), BF16),
            pltpu.VMEM(((half + 1) * pairs + 2 * EDGE, channels), F32),
            pltpu.VMEM(((half + 1) * pairs + 2 * EDGE, channels), F32),
            pltpu.VMEM(((rows + 2) * pairs, 4 * channels), BF16),
            pltpu.VMEM((rows * width, channels), F32),
            pltpu.SemaphoreType.DMA((2 * len(row_parts(rows, pairs)),)),
        ],
        compiler_params=pltpu.CompilerParams(vmem_limit_bytes=VMEM_BYTES),
        cost_estimate=pl.CostEstimate(
            flops=4 * rows * width * 12 * channels * channels,
            bytes_accessed=4 * 1024 * 1024,
            transcendentals=0,
        ),
        name="rest_second" if second else "rest_first",
    )(
        owner,
        *(space(a, pltpu.VMEM) for a in (acc, lifted, x, w_second, w_glob)),
        *pieces,
        *carried,
    )


def rotated(block, axis, distance):
    count = lax.axis_size(axis)
    return lax.ppermute(block, axis, [(i, (i + distance) % count) for i in range(count)])


def swapped(block, bit):
    count = lax.axis_size("patch")
    return lax.ppermute(block, "patch", [(i, i ^ bit) for i in range(count)])


def side_first(owner_ref):
    return patches_away(owner_ref) & 1


def place_first(owner_ref, k):
    return 2 * (k // 2) + (((patches_away(owner_ref) >> 1) ^ k) & 1)


def per_device(
    features, context, owner, hours, w_first, w_second, w_lead_in, w_lead_mix, w_lead_out
):
    resident, block = features[0, 0], context[0, 0]
    acc, proj, flags, kept, w_second, w_glob = resident_part(
        owner, resident, w_first, w_second, w_lead_in, block
    )

    def lifted_with(proj):
        before, after = rotated(proj, "lead", 1), rotated(proj, "lead", -1)
        moved = (resident, w_second, w_glob)
        return mix_part(hours, before, proj, after, w_lead_mix, w_lead_out, moved)

    def rest(second, side_of, place, lifted, pieces, carried):
        return rest_part(second, side_of, place, owner, acc, *lifted, pieces, carried)

    if lax.axis_size("patch") != 4:
        mine = lax.axis_index("patch") == owner[lax.axis_index("lead")]
        whole = lax.psum(jnp.where(mine, block, jnp.zeros_like(block)), "patch")
        result, _, _ = rest(
            False, lambda ref: 0, lambda ref, k: k, lifted_with(proj), [whole], []
        )
        return result[None, None]

    near, beside = flags[0] == 0, flags[1] == 0
    half = block.shape[0] // 2
    share = half // (2 * GROUPS)
    arrived, proj = lax.optimization_barrier((swapped(block[half:], 1), proj))
    owns, acrosses = [], []
    for g in range(GROUPS):
        rows = slice(2 * g * share, 2 * (g + 1) * share)
        part = jnp.where(near, kept[rows], arrived[rows])
        owns += [jnp.where(beside, part[:share], swapped(part[share:], 2))]
        acrosses += [swapped(owns[g], 2)]
    lifted = lifted_with(proj)
    acrosses, lifted = lax.optimization_barrier((acrosses, lifted))
    upper = [piece for pair in zip(owns, acrosses) for piece in pair]
    lower = [swapped(piece, 1) for piece in upper]
    result, *edges = rest(False, side_first, place_first, lifted, upper, [])
    (result,) = rest(True, side_first, place_first, lifted, lower, [*edges, result])
    return result[None, None]


def solution(mesh):
    placed = (
        P(("grp", "lead"), "patch", None, None, None),
        P("patch", ("grp", "lead"), None, None),
        P("grp"),
        P("grp"),
        P(),
        P(),
        P(),
        P(),
        P(),
    )
    return jax.shard_map(
        per_device,
        mesh=mesh,
        in_specs=placed,
        out_specs=P(("grp", "lead"), "patch", None, None, None),
        check_vma=False,
    )
```

time: 39.6 us -> 36.8 us (0.929)
  waiting for transfers between devices: 14.5 us -> 8.74 us
  Pallas kernels: 12.5 us -> 16.3 us
  between operations: 0.77 us -> 0.08 us
  local copies, waits for them, and re-layouts: 1.65 us -> 1.02 us
  starting transfers between devices: 10 us -> 10.4 us
    ppermute x5, waiting for transfers between devices: 14.5 us -> 8.74 us  [swapped(): return lax.ppermute(block, 'patch', [(i, i ^ bit) for i in range(count)])]
    pallas_call x2 -> x3, Pallas kernels: 7.39 us -> 10.7 us  [the longest x2 8.25 us: rest_part(): pl.pallas_call(lambda *refs: rest_kernel(second, side_of, place, *refs),...]
    dynamic_slice x1 -> x0, local copies, waits for them, and re-layouts: 0.59 us -> none  [spread(): away = lax.axis_index('patch') ^ owner[lax.axis_index('lead')]]
    pallas_call x1, Pallas kernels: 5.13 us -> 5.54 us  [resident_part(): pl.pallas_call(resident_kernel, out_shape=tuple((space(*kind) for space,...]
  transfers between devices with their start and end apart: 7 -> 7, of which waited for: 3 -> 4; matrix products, arithmetic and copies ran while one was open for 2% -> 0% of each run, Pallas kernels for 15% -> 33%
where the time goes in v3:
time: 36.8 us; the launch traced here: 36.6 us
  Pallas kernels  16.3 us (44%)
  starting transfers between devices  10.4 us (28%)
  waiting for transfers between devices  8.74 us (24%)
  local copies, waits for them, and re-layouts  1.02 us (3%)
    ppermute x5, starting transfers between devices, swapped(): return lax.ppermute(block, 'patch', [(i, i ^ bit) for i in range(count)])  9.89 us
    ppermute x5, waiting for transfers between devices, swapped(): return lax.ppermute(block, 'patch', [(i, i ^ bit) for i in range(count)])  8.74 us
    pallas_call x2, Pallas kernels, rest_part(): pl.pallas_call(lambda *refs: rest_kernel(second, side_of, place, *refs),...  8.25 us
    pallas_call x1, Pallas kernels, resident_part(): pl.pallas_call(resident_kernel, out_shape=tuple((space(*kind) for space,...  5.54 us
    pallas_call x1, Pallas kernels, mix_part(): pl.pallas_call(mix_kernel, out_shape=(pltpu.VMEM((2 * own.shape[0], 2 * o...  2.48 us
    slice x1, local copies, waits for them, and re-layouts, per_device(): arrived, proj = lax.optimization_barrier((swapped(block[half:], 1), proj))  0.99 us
  transfers between devices with their start and end apart: 7, of which 4 were waited for; matrix products, arithmetic and copies ran while one was open for 0% of the time, Pallas kernels for 33%

profile of v3, /device:TPU:0, one launch (start us, length us, event | category | flops | bytes accessed | tf_op | source)
XLA Modules:
  0.0 36.6 jit_solution(12327409074585396696)
XLA Ops:
  0.0 1.0 %slice_bitcast_fusion = bf16[64,2048]{1,0:T(8,128)(2,1)S(1)} fusion(bf16[1,1,128,2048]{3,2,1,0:T(8,128)(2,1)} %param.10), kind=kLoop, calls=%fused_computation | loop fusion | bytes 524288 | tf_op jit(solution)/shard_map/slice | solution.py:454
  1.0 3.1 %collective-permute-start = (bf16[64,2048]{1,0:T(8,128)(2,1)S(1)}, bf16[64,2048]{1,0:T(8,128)(2,1)S(1)}, u32[]{:S(2)}, u32[]{:S(2)}) collective-permute-start(bf16[64,2048]{1,0:T(8,128)(2,1)S(1)} %slice_bitcast_fusion), channel_id=1, source_target_pairs={{0,4},{4,0},{8,12},{12,8},{1,5},{5,1},{9,13},{13,9},{2,6},{6,2},{1... | collective-permute-start | bytes 786440 | tf_op jit(solution)/shard_map/ppermute | solution.py:416
  4.1 5.5 %resident_part.1 = (f32[2048,256]{1,0:T(8,128)S(1)}, bf16[1024,128]{1,0:T(8,128)(2,1)S(1)}, s32[2,1,2048]{2,1,0:T(1,128)S(1)}, bf16[64,2048]{1,0:T(8,128)(2,1)S(...) custom-call(s32[4]{0:T(128)} %refs_0_.3, bf16[128,32,128]{2,1,0:T(8,128)(2,1)} %bitcast.6, ...), custom_call_target="tpu_custom_call" | custom-call | flops 1024 | bytes 1024 | tf_op jit(solution)/shard_map/resident_part/pallas_call | solution.py:181
  9.7 0.1 compare_reduce_fusion.1
  9.7 0.7 %collective-permute-done = bf16[64,2048]{1,0:T(8,128)(2,1)S(1)} collective-permute-done((bf16[64,2048]{1,0:T(8,128)(2,1)S(1)}, bf16[64,2048]{1,0:T(8,128)(2,1)S(1)}, u32[]{:S(2)}, u32[]{:S(2)}) %collective-permute-start) | collective-permute-done | bytes 262176 | tf_op jit(solution)/shard_map/ppermute | solution.py:416
  10.5 2.8 %collective-permute-start.1 = (bf16[32,2048]{1,0:T(8,128)(2,1)S(1)}, bf16[32,2048]{1,0:T(8,128)(2,1)S(1)}, u32[]{:S(2)}, u32[]{:S(2)}) collective-permute-start(bf16[32,2048]{1,0:T(8,128)(2,1)S(1)} %slice.25), channel_id=1, source_target_pairs={{0,8},{4,12},{8,0},{12,4},{1,9},{5,13},{9,1},{13,5},{2,10},{6,14},... | collective-permute-start | bytes 393224 | tf_op jit(solution)/shard_map/ppermute | solution.py:416
  13.3 0.0 collective-permute-start.4
  13.3 0.5 %collective-permute-start.3 = (bf16[1024,128]{1,0:T(8,128)(2,1)S(1)}, bf16[1024,128]{1,0:T(8,128)(2,1)S(1)}, u32[]{:S(2)}, u32[]{:S(2)}) collective-permute-start(bf16[1024,128]{1,0:T(8,128)(2,1)S(1)} %get-tuple-element.30.self_ref), channel_id=1, source_target_pairs={{0,1},{1,2},{2,3},{3,0},{4,5},{5,6},{6,7},{7,4},{8,9},{9,10},{10,1... | collective-permute-start | bytes 786440 | tf_op jit(solution)/shard_map/ppermute | solution.py:411
  13.8 5.1 %collective-permute-done.1 = bf16[32,2048]{1,0:T(8,128)(2,1)S(1)} collective-permute-done((bf16[32,2048]{1,0:T(8,128)(2,1)S(1)}, bf16[32,2048]{1,0:T(8,128)(2,1)S(1)}, u32[]{:S(2)}, u32[]{:S(2)}) %collective-permute-start.1) | collective-permute-done | bytes 131104 | tf_op jit(solution)/shard_map/ppermute | solution.py:416
  18.9 0.4 %collective-permute-start.2 = (bf16[32,2048]{1,0:T(8,128)(2,1)S(1)}, bf16[32,2048]{1,0:T(8,128)(2,1)S(1)}, u32[]{:S(2)}, u32[]{:S(2)}) collective-permute-start(bf16[32,2048]{1,0:T(8,128)(2,1)S(1)} %slice_select_fusion.refs_6_), channel_id=1, source_target_pairs={{0,8},{4,12},{8,0},{12,4},{1,9},{5,13},{9,1},{13,5},{2,10},{6,14},... | collective-permute-start | bytes 393224 | tf_op jit(solution)/shard_map/ppermute | solution.py:416
  19.3 3.6 %collective-permute-start.5 = (bf16[32,2048]{1,0:T(8,128)(2,1)S(1)}, bf16[32,2048]{1,0:T(8,128)(2,1)S(1)}, u32[]{:S(2)}, u32[]{:S(2)}) collective-permute-start(bf16[32,2048]{1,0:T(8,128)(2,1)S(1)} %slice_select_fusion.refs_6_), channel_id=1, source_target_pairs={{0,4},{4,0},{8,12},{12,8},{1,5},{5,1},{9,13},{13,9},{2,6},{6,2},{1... | collective-permute-start | bytes 393224 | tf_op jit(solution)/shard_map/ppermute | solution.py:416
  22.9 0.0 collective-permute-done.4.next_ref
  22.9 0.0 collective-permute-done.3.prev_ref
  22.9 0.0 copy-done.1
  22.9 0.0 copy-done
  22.9 0.0 copy-done.3
  22.9 2.5 %mix_part.1 = (f32[2048,256]{1,0:T(8,128)S(1)}, bf16[128,32,128]{2,1,0:T(8,128)(2,1)S(1)}, bf16[1536,256]{1,0:T(8,128)(2,1)S(1)}, bf16[768,256]{1,0:T(8,128)(2,1)S(1)}) custom-call(s32[4]{0:T(128)S(1)} %copy-done.3, bf16[1024,128]{1,0:T(8,128)(2,1)S(1)} %collective-permute-done.3.prev_ref, bf16[1024,128]{1,0:T(8,128)(2,1)S(1)} %get-tuple-element.30.self_ref, ...), custom_call_target="tpu_custom_call" | custom-call | flops 100663296 | bytes 1048576 | tf_op jit(solution)/shard_map/mix_part/pallas_call | solution.py:252
  25.4 1.9 %collective-permute-done.2.refs_7_ = bf16[32,2048]{1,0:T(8,128)(2,1)S(1)} collective-permute-done((bf16[32,2048]{1,0:T(8,128)(2,1)S(1)}, bf16[32,2048]{1,0:T(8,128)(2,1)S(1)}, u32[]{:S(2)}, u32[]{:S(2)}) %collective-permute-start.2) | collective-permute-done | bytes 131104 | tf_op jit(solution)/shard_map/ppermute | solution.py:416
  27.3 0.0 collective-permute-start.6
  27.3 0.0 copy-done.2
  27.3 3.9 %rest_first.1 = (bf16[128,32,128]{2,1,0:T(8,128)(2,1)}, bf16[32,256]{1,0:T(8,128)(2,1)S(1)}, bf16[32,512]{1,0:T(8,128)(2,1)S(1)}) custom-call(s32[4]{0:T(128)S(1)} %copy-done.2, f32[2048,256]{1,0:T(8,128)S(1)} %get-tuple-element.25.refs_1_, f32[2048,256]{1,0:T(8,128)S(1)} %get-tuple-element.37.refs_2_, bf16[128,32,128]{2,1,0:T(8,128)(2,1)S(1)} %get-tuple-element.38.refs_3_, ...), custom_call_target="tpu_custom_call" | custom-call | flops 1610612736 | bytes 4194304 | tf_op jit(solution)/shard_map/rest_first/pallas_call | solution.py:376
  31.3 0.0 collective-permute-done.5.refs_6_
  31.3 1.0 %collective-permute-done.6.refs_7_ = bf16[32,2048]{1,0:T(8,128)(2,1)S(1)} collective-permute-done((bf16[32,2048]{1,0:T(8,128)(2,1)S(1)}, bf16[32,2048]{1,0:T(8,128)(2,1)S(1)}, u32[]{:S(2)}, u32[]{:S(2)}) %collective-permute-start.6) | collective-permute-done | bytes 131104 | tf_op jit(solution)/shard_map/ppermute | solution.py:416
  32.3 4.3 %rest_second.1 = bf16[128,32,128]{2,1,0:T(8,128)(2,1)} custom-call(s32[4]{0:T(128)S(1)} %copy-done.2, f32[2048,256]{1,0:T(8,128)S(1)} %get-tuple-element.25.refs_1_, f32[2048,256]{1,0:T(8,128)S(1)} %get-tuple-element.37.refs_2_, bf16[128,32,128]{2,1,0:T(8,128)(2,1)S(1)} %get-tuple-element.38.refs_3_, ...), custom_call_target="tpu_custom_call", output_to_operand_aliasing={{}: (10, {})} | custom-call | flops 1660944384 | bytes 4194304 | tf_op jit(solution)/shard_map/rest_second/pallas_call | solution.py:376
  (7 shorter events, 0.1 us)
Async XLA Ops:
  0.0 22.9 %copy-start.1 = (bf16[32,128]{1,0:T(8,128)(2,1)S(1)}, bf16[32,128]{1,0:T(8,128)(2,1)}, u32[]{:S(2)}) copy-start(bf16[32,128]{1,0:T(8,128)(2,1)} %out_ref.1) | copy-start | bytes 24580
  0.0 22.9 %copy-start = (bf16[3,32,32]{2,1,0:T(8,128)(2,1)S(1)}, bf16[3,32,32]{2,1,0:T(8,128)(2,1)}, u32[]{:S(2)}) copy-start(bf16[3,32,32]{2,1,0:T(8,128)(2,1)} %mix_ref.1) | copy-start | bytes 18436
  0.0 22.9 %copy-start.3 = (s32[4]{0:T(128)S(1)}, s32[4]{0:T(128)}, u32[]{:S(2)}) copy-start(s32[4]{0:T(128)} %hours_ref.1) | copy-start | bytes 52
  1.0 9.4 %collective-permute-start = (bf16[64,2048]{1,0:T(8,128)(2,1)S(1)}, bf16[64,2048]{1,0:T(8,128)(2,1)S(1)}, u32[]{:S(2)}, u32[]{:S(2)}) collective-permute-start(bf16[64,2048]{1,0:T(8,128)(2,1)S(1)} %slice_bitcast_fusion), channel_id=1, source_target_pairs={{0,4},{4,0},{8,12},{12,8},{1,5},{5,1},{9,13},{13,9},{2,6},{6,2},{1... | collective-permute-start | bytes 786440 | tf_op jit(solution)/shard_map/ppermute | solution.py:416
  10.4 16.9 %copy-start.2 = (s32[4]{0:T(128)S(1)}, s32[4]{0:T(128)}, u32[]{:S(2)}) copy-start(s32[4]{0:T(128)} %refs_0_.3) | copy-start | bytes 52
  10.5 8.5 %collective-permute-start.1 = (bf16[32,2048]{1,0:T(8,128)(2,1)S(1)}, bf16[32,2048]{1,0:T(8,128)(2,1)S(1)}, u32[]{:S(2)}, u32[]{:S(2)}) collective-permute-start(bf16[32,2048]{1,0:T(8,128)(2,1)S(1)} %slice.25), channel_id=1, source_target_pairs={{0,8},{4,12},{8,0},{12,4},{1,9},{5,13},{9,1},{13,5},{2,10},{6,14},... | collective-permute-start | bytes 393224 | tf_op jit(solution)/shard_map/ppermute | solution.py:416
  13.3 9.6 %collective-permute-start.4 = (bf16[1024,128]{1,0:T(8,128)(2,1)S(1)}, bf16[1024,128]{1,0:T(8,128)(2,1)S(1)}, u32[]{:S(2)}, u32[]{:S(2)}) collective-permute-start(bf16[1024,128]{1,0:T(8,128)(2,1)S(1)} %get-tuple-element.30.self_ref), channel_id=1, source_target_pairs={{0,3},{1,0},{2,1},{3,2},{4,7},{5,4},{6,5},{7,6},{8,11},{9,8},{10,9... | collective-permute-start | bytes 786440 | tf_op jit(solution)/shard_map/ppermute | solution.py:411
  13.3 9.6 %collective-permute-start.3 = (bf16[1024,128]{1,0:T(8,128)(2,1)S(1)}, bf16[1024,128]{1,0:T(8,128)(2,1)S(1)}, u32[]{:S(2)}, u32[]{:S(2)}) collective-permute-start(bf16[1024,128]{1,0:T(8,128)(2,1)S(1)} %get-tuple-element.30.self_ref), channel_id=1, source_target_pairs={{0,1},{1,2},{2,3},{3,0},{4,5},{5,6},{6,7},{7,4},{8,9},{9,10},{10,1... | collective-permute-start | bytes 786440 | tf_op jit(solution)/shard_map/ppermute | solution.py:411
  18.9 8.4 %collective-permute-start.2 = (bf16[32,2048]{1,0:T(8,128)(2,1)S(1)}, bf16[32,2048]{1,0:T(8,128)(2,1)S(1)}, u32[]{:S(2)}, u32[]{:S(2)}) collective-permute-start(bf16[32,2048]{1,0:T(8,128)(2,1)S(1)} %slice_select_fusion.refs_6_), channel_id=1, source_target_pairs={{0,8},{4,12},{8,0},{12,4},{1,9},{5,13},{9,1},{13,5},{2,10},{6,14},... | collective-permute-start | bytes 393224 | tf_op jit(solution)/shard_map/ppermute | solution.py:416
  19.3 11.9 %collective-permute-start.5 = (bf16[32,2048]{1,0:T(8,128)(2,1)S(1)}, bf16[32,2048]{1,0:T(8,128)(2,1)S(1)}, u32[]{:S(2)}, u32[]{:S(2)}) collective-permute-start(bf16[32,2048]{1,0:T(8,128)(2,1)S(1)} %slice_select_fusion.refs_6_), channel_id=1, source_target_pairs={{0,4},{4,0},{8,12},{12,8},{1,5},{5,1},{9,13},{13,9},{2,6},{6,2},{1... | collective-permute-start | bytes 393224 | tf_op jit(solution)/shard_map/ppermute | solution.py:416
  27.3 5.0 %collective-permute-start.6 = (bf16[32,2048]{1,0:T(8,128)(2,1)S(1)}, bf16[32,2048]{1,0:T(8,128)(2,1)S(1)}, u32[]{:S(2)}, u32[]{:S(2)}) collective-permute-start(bf16[32,2048]{1,0:T(8,128)(2,1)S(1)} %collective-permute-done.2.refs_7_), channel_id=1, source_target_pairs={{0,4},{4,0},{8,12},{12,8},{1,5},{5,1},{9,13},{13,9},{2,6},{6,2},{1... | collective-permute-start | bytes 393224 | tf_op jit(solution)/shard_map/ppermute | solution.py:416

commit v4 on v3

--- a/solution.py
+++ b/solution.py
@@ -94,8 +94,8 @@
 
 def resident_kernel(
     owner_ref, x_hbm, first_hbm, second_hbm, w_in_hbm, block_hbm,
-    acc_ref, proj_ref, flags_ref, block_ref, w_second_hbm, w_glob_hbm,
-    x_ref, first_ref, second_ref, in_ref, w_second_ref, w_glob_ref, cells, taps, w_first, w_in, sems,
+    acc_ref, proj_ref, flags_ref, block_ref, w_second_ref, w_glob_ref, x_ref,
+    first_ref, second_ref, in_ref, cells, taps, w_first, w_in, sems,
 ):
     height, width, channels = x_ref.shape
     pairs = width // 2
@@ -153,13 +153,9 @@
     put_pair_weights(w_glob_ref, first_ref, channels, glob, (0, 1, 2, -1))
     copies[parts + 2].wait()
     put_pair_weights(w_second_ref, second_ref, 0, channels, (-1, 0, 1, 2))
-    writes = start_copies(
-        [(w_glob_ref, w_glob_hbm), (w_second_ref, w_second_hbm)], sems.at[pl.ds(parts + 4, 2)]
-    )
     for start in range(0, rows, WIDE):
         acc_ref[pl.ds(start, WIDE), :] = pair_taps(taps, w_first, start, WIDE, pairs)
-    for write in [*writes, copies[parts + 3]]:
-        write.wait()
+    copies[parts + 3].wait()
 
 
 def resident_part(owner, x, w_first, w_second, w_in, block):
@@ -177,21 +173,19 @@
         ((height // 2, width * glob), BF16),
         ((12 * out, 2 * out), BF16),
         ((12 * glob, 2 * out), BF16),
+        (x.shape, BF16),
     )
     return pl.pallas_call(
         resident_kernel,
         out_shape=tuple(
-            space(*kind) for space, kind in zip((pltpu.VMEM,) * 4 + (pltpu.HBM,) * 2, results)
+            space(*kind) for space, kind in zip((pltpu.VMEM,) * 7, results)
         ),
         in_specs=[pl.BlockSpec(memory_space=pltpu.SMEM)] + in_hbm(5),
-        out_specs=tuple(in_vmem(4) + in_hbm(2)),
+        out_specs=tuple(in_vmem(7)),
         scratch_shapes=[
-            pltpu.VMEM(x.shape, BF16),
             pltpu.VMEM(w_first.shape, BF16),
             pltpu.VMEM(w_second.shape, BF16),
             pltpu.VMEM(w_in.shape, BF16),
-            pltpu.VMEM(*results[4]),
-            pltpu.VMEM(*results[5]),
             pltpu.VMEM((2 * rows + 2 * EDGE, channels), F32),
             pltpu.VMEM((rows + 2 * pairs, 4 * channels), BF16),
             pltpu.VMEM((12 * channels, 2 * out), BF16),
@@ -205,12 +199,8 @@
 
 
 def mix_kernel(
-    hours_ref, prev_ref, self_ref, next_ref, mix_ref, out_ref, x_hbm, w_second_hbm, w_glob_hbm,
-    lifted_ref, x_ref, w_second_ref, w_glob_ref, w_mix, w_lift, mixed_ref, sems,
+    hours_ref, prev_ref, self_ref, next_ref, mix_ref, out_ref, lifted_ref, w_mix, w_lift, mixed_ref
 ):
-    copies = start_copies(
-        [(w_glob_hbm, w_glob_ref), (w_second_hbm, w_second_ref), (x_hbm, x_ref)], sems
-    )
     leads = hours_ref.shape[0]
     temporal = mix_ref.shape[1]
     lead = lax.axis_index("lead")
@@ -243,36 +233,30 @@
         mixed_ref[part, :] = value.astype(BF16)
     for s in range(2):
         lifted_ref[pl.ds(s * rows, rows), :] = dot(mixed_ref[...], w_lift[s])
-    for copy in copies:
-        copy.wait()
-
-
-def mix_part(hours, before, own, after, w_mix, w_out, moved):
+
+
+def mix_part(hours, before, own, after, w_mix, w_out):
     lanes, out = own.shape[1], w_out.shape[1]
     return pl.pallas_call(
         mix_kernel,
-        out_shape=(
-            pltpu.VMEM((2 * own.shape[0], 2 * out), F32),
-            *(pltpu.VMEM(a.shape, a.dtype) for a in moved),
-        ),
-        in_specs=[pl.BlockSpec(memory_space=pltpu.SMEM)] + in_vmem(5) + in_hbm(len(moved)),
-        out_specs=tuple(in_vmem(1 + len(moved))),
+        out_shape=pltpu.VMEM((2 * own.shape[0], 2 * out), F32),
+        in_specs=[pl.BlockSpec(memory_space=pltpu.SMEM)] + in_vmem(5),
+        out_specs=in_vmem(1)[0],
         scratch_shapes=[
             pltpu.VMEM((3, lanes, lanes), BF16),
             pltpu.VMEM((2, lanes, 2 * out), BF16),
             pltpu.VMEM(own.shape, BF16),
-            pltpu.SemaphoreType.DMA((len(moved),)),
         ],
         compiler_params=pltpu.CompilerParams(vmem_limit_bytes=VMEM_BYTES),
         cost_estimate=pl.CostEstimate(
             flops=6 * own.shape[0] * lanes * lanes, bytes_accessed=1024 * 1024, transcendentals=0
         ),
         name="mix_part",
-    )(hours, before, own, after, w_mix, w_out, *at_hbm(*moved))
+    )(hours, before, own, after, w_mix, w_out)
 
 
 def row_parts(rows, pairs):
-    count = max(1, rows * pairs // WIDE)
+    count = max(1, rows * pairs // CHUNK)
     bounds = [rows * k // count for k in range(count + 1)]
     return [(low, high - low) for low, high in zip(bounds, bounds[1:])]
 
@@ -417,7 +401,8 @@
 
 
 def side_first(owner_ref):
-    return patches_away(owner_ref) & 1
+    away = patches_away(owner_ref)
+    return (away ^ (away >> 1)) & 1
 
 
 def place_first(owner_ref, k):
@@ -428,17 +413,16 @@
     features, context, owner, hours, w_first, w_second, w_lead_in, w_lead_mix, w_lead_out
 ):
     resident, block = features[0, 0], context[0, 0]
-    acc, proj, flags, kept, w_second, w_glob = resident_part(
+    acc, proj, flags, kept, w_second, w_glob, resident = resident_part(
         owner, resident, w_first, w_second, w_lead_in, block
     )
 
     def lifted_with(proj):
         before, after = rotated(proj, "lead", 1), rotated(proj, "lead", -1)
-        moved = (resident, w_second, w_glob)
-        return mix_part(hours, before, proj, after, w_lead_mix, w_lead_out, moved)
+        return mix_part(hours, before, proj, after, w_lead_mix, w_lead_out)
 
     def rest(second, side_of, place, lifted, pieces, carried):
-        return rest_part(second, side_of, place, owner, acc, *lifted, pieces, carried)
+        return rest_part(second, side_of, place, owner, acc, lifted, resident, w_second, w_glob, pieces, carried)
 
     if lax.axis_size("patch") != 4:
         mine = lax.axis_index("patch") == owner[lax.axis_index("lead")]
@@ -456,8 +440,8 @@
     for g in range(GROUPS):
         rows = slice(2 * g * share, 2 * (g + 1) * share)
         part = jnp.where(near, kept[rows], arrived[rows])
-        owns += [jnp.where(beside, part[:share], swapped(part[share:], 2))]
-        acrosses += [swapped(owns[g], 2)]
+        owns += [jnp.where(beside, part[:share], swapped(part[share:], 3))]
+        acrosses += [swapped(owns[g], 3)]
     lifted = lifted_with(proj)
     acrosses, lifted = lax.optimization_barrier((acrosses, lifted))
     upper = [piece for pair in zip(owns, acrosses) for piece in pair]

time: 36.8 us -> 33.5 us (0.910)
  Pallas kernels: 16.3 us -> 12.7 us
  starting transfers between devices: 10.4 us -> 13.6 us
  waiting for transfers between devices: 8.74 us -> 5.83 us
    ppermute x5, waiting for transfers between devices: 8.74 us -> 4.63 us  [swapped(): return lax.ppermute(block, 'patch', [(i, i ^ bit) for i in range(count)])]
    ppermute x5, starting transfers between devices: 9.89 us -> 13.1 us  [swapped(): return lax.ppermute(block, 'patch', [(i, i ^ bit) for i in range(count)])]
    pallas_call x2, Pallas kernels: 8.25 us -> 6.74 us  [rest_part(): pl.pallas_call(lambda *refs: rest_kernel(second, side_of, place, *refs),...]
    pallas_call x1, Pallas kernels: 2.48 us -> 1.26 us  [mix_part(): pl.pallas_call(mix_kernel, out_shape=pltpu.VMEM((2 * own.shape[0], 2 * ou...]
    ppermute x2, waiting for transfers between devices: 0.01 us -> 1.2 us  [rotated(): lax.ppermute(block, axis, [(i, (i + distance) % count) for i in range(cou...]
    pallas_call x1, Pallas kernels: 5.54 us -> 4.72 us  [resident_part(): pl.pallas_call(resident_kernel, out_shape=tuple((space(*kind) for space,...]
  transfers between devices with their start and end apart: 7 -> 7, of which waited for: 4 -> 4; matrix products, arithmetic and copies ran while one was open for 0% -> 0% of each run, Pallas kernels for 33% -> 28%
where the time goes in v4:
time: 33.5 us; the launch traced here: 33.4 us
  starting transfers between devices  13.6 us (41%)
  Pallas kernels  12.7 us (38%)
  waiting for transfers between devices  5.83 us (17%)
  local copies, waits for them, and re-layouts  1.02 us (3%)
    ppermute x5, starting transfers between devices, swapped(): return lax.ppermute(block, 'patch', [(i, i ^ bit) for i in range(count)])  13.1 us
    pallas_call x2, Pallas kernels, rest_part(): pl.pallas_call(lambda *refs: rest_kernel(second, side_of, place, *refs),...  6.74 us
    pallas_call x1, Pallas kernels, resident_part(): pl.pallas_call(resident_kernel, out_shape=tuple((space(*kind) for space,...  4.72 us
    ppermute x5, waiting for transfers between devices, swapped(): return lax.ppermute(block, 'patch', [(i, i ^ bit) for i in range(count)])  4.63 us
    pallas_call x1, Pallas kernels, mix_part(): pl.pallas_call(mix_kernel, out_shape=pltpu.VMEM((2 * own.shape[0], 2 * ou...  1.26 us
    ppermute x2, waiting for transfers between devices, rotated(): lax.ppermute(block, axis, [(i, (i + distance) % count) for i in range(cou...  1.2 us
    slice x1, local copies, waits for them, and re-layouts, per_device(): arrived, proj = lax.optimization_barrier((swapped(block[half:], 1), proj))  0.99 us
  transfers between devices with their start and end apart: 7, of which 4 were waited for; matrix products, arithmetic and copies ran while one was open for 0% of the time, Pallas kernels for 28%

profile of v4, /device:TPU:0, one launch (start us, length us, event | category | flops | bytes accessed | tf_op | source)
XLA Modules:
  0.0 33.4 jit_solution(15762294153616397595)
XLA Ops:
  0.0 1.0 %slice_bitcast_fusion = bf16[64,2048]{1,0:T(8,128)(2,1)S(1)} fusion(bf16[1,1,128,2048]{3,2,1,0:T(8,128)(2,1)} %param.10), kind=kLoop, calls=%fused_computation | loop fusion | bytes 524288 | tf_op jit(solution)/shard_map/slice | solution.py:438
  1.0 3.1 %collective-permute-start = (bf16[64,2048]{1,0:T(8,128)(2,1)S(1)}, bf16[64,2048]{1,0:T(8,128)(2,1)S(1)}, u32[]{:S(2)}, u32[]{:S(2)}) collective-permute-start(bf16[64,2048]{1,0:T(8,128)(2,1)S(1)} %slice_bitcast_fusion), channel_id=1, source_target_pairs={{0,4},{4,0},{8,12},{12,8},{1,5},{5,1},{9,13},{13,9},{2,6},{6,2},{1... | collective-permute-start | bytes 786440 | tf_op jit(solution)/shard_map/ppermute | solution.py:400
  4.1 4.7 %resident_part.1 = (f32[2048,256]{1,0:T(8,128)S(1)}, bf16[1024,128]{1,0:T(8,128)(2,1)S(1)}, s32[2,1,2048]{2,1,0:T(1,128)S(1)}, bf16[64,2048]{1,0:T(8,128)(2,1)S(...) custom-call(s32[4]{0:T(128)} %refs_0_.3, ...), custom_call_target="tpu_custom_call" | custom-call | flops 1024 | bytes 1024 | tf_op jit(solution)/shard_map/resident_part/pallas_call | solution.py:178
  8.8 0.1 compare_reduce_fusion.1
  8.9 1.5 %collective-permute-done = bf16[64,2048]{1,0:T(8,128)(2,1)S(1)} collective-permute-done((bf16[64,2048]{1,0:T(8,128)(2,1)S(1)}, bf16[64,2048]{1,0:T(8,128)(2,1)S(1)}, u32[]{:S(2)}, u32[]{:S(2)}) %collective-permute-start) | collective-permute-done | bytes 262176 | tf_op jit(solution)/shard_map/ppermute | solution.py:400
  10.5 3.8 %collective-permute-start.1 = (bf16[32,2048]{1,0:T(8,128)(2,1)S(1)}, bf16[32,2048]{1,0:T(8,128)(2,1)S(1)}, u32[]{:S(2)}, u32[]{:S(2)}) collective-permute-start(bf16[32,2048]{1,0:T(8,128)(2,1)S(1)} %slice.25), channel_id=1, source_target_pairs={{0,12},{4,8},{8,4},{12,0},{1,13},{5,9},{9,5},{13,1},{2,14},{6,10},... | collective-permute-start | bytes 393224 | tf_op jit(solution)/shard_map/ppermute | solution.py:400
  14.3 0.0 collective-permute-start.4
  14.3 0.5 %collective-permute-start.3 = (bf16[1024,128]{1,0:T(8,128)(2,1)S(1)}, bf16[1024,128]{1,0:T(8,128)(2,1)S(1)}, u32[]{:S(2)}, u32[]{:S(2)}) collective-permute-start(bf16[1024,128]{1,0:T(8,128)(2,1)S(1)} %get-tuple-element.24.self_ref), channel_id=1, source_target_pairs={{0,1},{1,2},{2,3},{3,0},{4,5},{5,6},{6,7},{7,4},{8,9},{9,10},{10,1... | collective-permute-start | bytes 786440 | tf_op jit(solution)/shard_map/ppermute | solution.py:395
  14.8 2.5 %collective-permute-done.1 = bf16[32,2048]{1,0:T(8,128)(2,1)S(1)} collective-permute-done((bf16[32,2048]{1,0:T(8,128)(2,1)S(1)}, bf16[32,2048]{1,0:T(8,128)(2,1)S(1)}, u32[]{:S(2)}, u32[]{:S(2)}) %collective-permute-start.1) | collective-permute-done | bytes 131104 | tf_op jit(solution)/shard_map/ppermute | solution.py:400
  17.4 3.9 %collective-permute-start.2 = (bf16[32,2048]{1,0:T(8,128)(2,1)S(1)}, bf16[32,2048]{1,0:T(8,128)(2,1)S(1)}, u32[]{:S(2)}, u32[]{:S(2)}) collective-permute-start(bf16[32,2048]{1,0:T(8,128)(2,1)S(1)} %slice_select_fusion.refs_6_), channel_id=1, source_target_pairs={{0,12},{4,8},{8,4},{12,0},{1,13},{5,9},{9,5},{13,1},{2,14},{6,10},... | collective-permute-start | bytes 393224 | tf_op jit(solution)/shard_map/ppermute | solution.py:400
  21.3 0.4 %collective-permute-start.5 = (bf16[32,2048]{1,0:T(8,128)(2,1)S(1)}, bf16[32,2048]{1,0:T(8,128)(2,1)S(1)}, u32[]{:S(2)}, u32[]{:S(2)}) collective-permute-start(bf16[32,2048]{1,0:T(8,128)(2,1)S(1)} %slice_select_fusion.refs_6_), channel_id=1, source_target_pairs={{0,4},{4,0},{8,12},{12,8},{1,5},{5,1},{9,13},{13,9},{2,6},{6,2},{1... | collective-permute-start | bytes 393224 | tf_op jit(solution)/shard_map/ppermute | solution.py:400
  21.7 0.0 collective-permute-done.4.next_ref
  21.7 1.2 %collective-permute-done.3.prev_ref = bf16[1024,128]{1,0:T(8,128)(2,1)S(1)} collective-permute-done((bf16[1024,128]{1,0:T(8,128)(2,1)S(1)}, bf16[1024,128]{1,0:T(8,128)(2,1)S(1)}, u32[]{:S(2)}, u32[]{:S(2)}) %collective-permute-start.3) | collective-permute-done | bytes 262176 | tf_op jit(solution)/shard_map/ppermute | solution.py:395
  22.9 0.0 copy-done.1
  22.9 0.0 copy-done
  22.9 0.0 copy-done.3
  22.9 1.3 %mix_part.1.refs_2_ = f32[2048,256]{1,0:T(8,128)S(1)} custom-call(s32[4]{0:T(128)S(1)} %copy-done.3, bf16[1024,128]{1,0:T(8,128)(2,1)S(1)} %collective-permute-done.3.prev_ref, bf16[1024,128]{1,0:T(8,128)(2,1)S(1)} %get-tuple-element.24.self_ref, bf16[1024,128]{1,0:T(8,128)(2,1)S(1)} %collective-permute-done.4.next_ref, bf16[3,32,32]{2,1,0:T(8,128)(2,1)S(1)} %copy-done, ...), custom_call_target="tpu_custom_call" | custom-call | flops 100663296 | bytes 1048576 | tf_op jit(solution)/shard_map/mix_part/pallas_call | solution.py:240
  24.2 0.6 %collective-permute-done.2.refs_7_ = bf16[32,2048]{1,0:T(8,128)(2,1)S(1)} collective-permute-done((bf16[32,2048]{1,0:T(8,128)(2,1)S(1)}, bf16[32,2048]{1,0:T(8,128)(2,1)S(1)}, u32[]{:S(2)}, u32[]{:S(2)}) %collective-permute-start.2) | collective-permute-done | bytes 131104 | tf_op jit(solution)/shard_map/ppermute | solution.py:400
  24.7 1.9 %collective-permute-start.6 = (bf16[32,2048]{1,0:T(8,128)(2,1)S(1)}, bf16[32,2048]{1,0:T(8,128)(2,1)S(1)}, u32[]{:S(2)}, u32[]{:S(2)}) collective-permute-start(bf16[32,2048]{1,0:T(8,128)(2,1)S(1)} %collective-permute-done.2.refs_7_), channel_id=1, source_target_pairs={{0,4},{4,0},{8,12},{12,8},{1,5},{5,1},{9,13},{13,9},{2,6},{6,2},{1... | collective-permute-start | bytes 393224 | tf_op jit(solution)/shard_map/ppermute | solution.py:400
  26.6 0.0 copy-done.2
  26.6 3.2 %rest_first.1 = (bf16[128,32,128]{2,1,0:T(8,128)(2,1)}, bf16[32,256]{1,0:T(8,128)(2,1)S(1)}, bf16[32,512]{1,0:T(8,128)(2,1)S(1)}) custom-call(s32[4]{0:T(128)S(1)} %copy-done.2, f32[2048,256]{1,0:T(8,128)S(1)} %get-tuple-element.19.refs_1_, f32[2048,256]{1,0:T(8,128)S(1)} %mix_part.1.refs_2_, bf16[128,32,128]{2,1,0:T(8,128)(2,1)S(1)} %get-tuple-element.26.refs_3_, ...), custom_call_target="tpu_custom_call" | custom-call | flops 1610612736 | bytes 4194304 | tf_op jit(solution)/shard_map/rest_first/pallas_call | solution.py:360
  29.8 0.0 collective-permute-done.5.refs_6_
  29.8 0.0 collective-permute-done.6.refs_7_
  29.8 3.5 %rest_second.1 = bf16[128,32,128]{2,1,0:T(8,128)(2,1)} custom-call(s32[4]{0:T(128)S(1)} %copy-done.2, f32[2048,256]{1,0:T(8,128)S(1)} %get-tuple-element.19.refs_1_, f32[2048,256]{1,0:T(8,128)S(1)} %mix_part.1.refs_2_, bf16[128,32,128]{2,1,0:T(8,128)(2,1)S(1)} %get-tuple-element.26.refs_3_, ...), custom_call_target="tpu_custom_call", output_to_operand_aliasing={{}: (10, {})} | custom-call | flops 1660944384 | bytes 4194304 | tf_op jit(solution)/shard_map/rest_second/pallas_call | solution.py:360
  (7 shorter events, 0.1 us)
Async XLA Ops:
  0.0 22.9 %copy-start.1 = (bf16[32,128]{1,0:T(8,128)(2,1)S(1)}, bf16[32,128]{1,0:T(8,128)(2,1)}, u32[]{:S(2)}) copy-start(bf16[32,128]{1,0:T(8,128)(2,1)} %out_ref.1) | copy-start | bytes 24580
  0.0 22.9 %copy-start = (bf16[3,32,32]{2,1,0:T(8,128)(2,1)S(1)}, bf16[3,32,32]{2,1,0:T(8,128)(2,1)}, u32[]{:S(2)}) copy-start(bf16[3,32,32]{2,1,0:T(8,128)(2,1)} %mix_ref.1) | copy-start | bytes 18436
  0.0 22.9 %copy-start.3 = (s32[4]{0:T(128)S(1)}, s32[4]{0:T(128)}, u32[]{:S(2)}) copy-start(s32[4]{0:T(128)} %hours_ref.1) | copy-start | bytes 52
  1.0 9.4 %collective-permute-start = (bf16[64,2048]{1,0:T(8,128)(2,1)S(1)}, bf16[64,2048]{1,0:T(8,128)(2,1)S(1)}, u32[]{:S(2)}, u32[]{:S(2)}) collective-permute-start(bf16[64,2048]{1,0:T(8,128)(2,1)S(1)} %slice_bitcast_fusion), channel_id=1, source_target_pairs={{0,4},{4,0},{8,12},{12,8},{1,5},{5,1},{9,13},{13,9},{2,6},{6,2},{1... | collective-permute-start | bytes 786440 | tf_op jit(solution)/shard_map/ppermute | solution.py:400
  10.4 16.2 %copy-start.2 = (s32[4]{0:T(128)S(1)}, s32[4]{0:T(128)}, u32[]{:S(2)}) copy-start(s32[4]{0:T(128)} %refs_0_.3) | copy-start | bytes 52
  10.5 6.9 %collective-permute-start.1 = (bf16[32,2048]{1,0:T(8,128)(2,1)S(1)}, bf16[32,2048]{1,0:T(8,128)(2,1)S(1)}, u32[]{:S(2)}, u32[]{:S(2)}) collective-permute-start(bf16[32,2048]{1,0:T(8,128)(2,1)S(1)} %slice.25), channel_id=1, source_target_pairs={{0,12},{4,8},{8,4},{12,0},{1,13},{5,9},{9,5},{13,1},{2,14},{6,10},... | collective-permute-start | bytes 393224 | tf_op jit(solution)/shard_map/ppermute | solution.py:400
  14.3 7.4 %collective-permute-start.4 = (bf16[1024,128]{1,0:T(8,128)(2,1)S(1)}, bf16[1024,128]{1,0:T(8,128)(2,1)S(1)}, u32[]{:S(2)}, u32[]{:S(2)}) collective-permute-start(bf16[1024,128]{1,0:T(8,128)(2,1)S(1)} %get-tuple-element.24.self_ref), channel_id=1, source_target_pairs={{0,3},{1,0},{2,1},{3,2},{4,7},{5,4},{6,5},{7,6},{8,11},{9,8},{10,9... | collective-permute-start | bytes 786440 | tf_op jit(solution)/shard_map/ppermute | solution.py:395
  14.3 8.6 %collective-permute-start.3 = (bf16[1024,128]{1,0:T(8,128)(2,1)S(1)}, bf16[1024,128]{1,0:T(8,128)(2,1)S(1)}, u32[]{:S(2)}, u32[]{:S(2)}) collective-permute-start(bf16[1024,128]{1,0:T(8,128)(2,1)S(1)} %get-tuple-element.24.self_ref), channel_id=1, source_target_pairs={{0,1},{1,2},{2,3},{3,0},{4,5},{5,6},{6,7},{7,4},{8,9},{9,10},{10,1... | collective-permute-start | bytes 786440 | tf_op jit(solution)/shard_map/ppermute | solution.py:395
  17.4 7.3 %collective-permute-start.2 = (bf16[32,2048]{1,0:T(8,128)(2,1)S(1)}, bf16[32,2048]{1,0:T(8,128)(2,1)S(1)}, u32[]{:S(2)}, u32[]{:S(2)}) collective-permute-start(bf16[32,2048]{1,0:T(8,128)(2,1)S(1)} %slice_select_fusion.refs_6_), channel_id=1, source_target_pairs={{0,12},{4,8},{8,4},{12,0},{1,13},{5,9},{9,5},{13,1},{2,14},{6,10},... | collective-permute-start | bytes 393224 | tf_op jit(solution)/shard_map/ppermute | solution.py:400
  21.3 8.5 %collective-permute-start.5 = (bf16[32,2048]{1,0:T(8,128)(2,1)S(1)}, bf16[32,2048]{1,0:T(8,128)(2,1)S(1)}, u32[]{:S(2)}, u32[]{:S(2)}) collective-permute-start(bf16[32,2048]{1,0:T(8,128)(2,1)S(1)} %slice_select_fusion.refs_6_), channel_id=1, source_target_pairs={{0,4},{4,0},{8,12},{12,8},{1,5},{5,1},{9,13},{13,9},{2,6},{6,2},{1... | collective-permute-start | bytes 393224 | tf_op jit(solution)/shard_map/ppermute | solution.py:400
  24.7 5.1 %collective-permute-start.6 = (bf16[32,2048]{1,0:T(8,128)(2,1)S(1)}, bf16[32,2048]{1,0:T(8,128)(2,1)S(1)}, u32[]{:S(2)}, u32[]{:S(2)}) collective-permute-start(bf16[32,2048]{1,0:T(8,128)(2,1)S(1)} %collective-permute-done.2.refs_7_), channel_id=1, source_target_pairs={{0,4},{4,0},{8,12},{12,8},{1,5},{5,1},{9,13},{13,9},{2,6},{6,2},{1... | collective-permute-start | bytes 393224 | tf_op jit(solution)/shard_map/ppermute | solution.py:400

commit v5 on v4

--- a/solution.py
+++ b/solution.py
@@ -10,7 +10,6 @@
 EDGE = 8
 CHUNK = 256
 WIDE = 1024
-GROUPS = 1
 VMEM_BYTES = 20 * 1024 * 1024
 
 
@@ -406,7 +405,7 @@
 
 
 def place_first(owner_ref, k):
-    return 2 * (k // 2) + (((patches_away(owner_ref) >> 1) ^ k) & 1)
+    return ((patches_away(owner_ref) >> 1) ^ k) & 1
 
 
 def per_device(
@@ -434,18 +433,18 @@
 
     near, beside = flags[0] == 0, flags[1] == 0
     half = block.shape[0] // 2
-    share = half // (2 * GROUPS)
-    arrived, proj = lax.optimization_barrier((swapped(block[half:], 1), proj))
-    owns, acrosses = [], []
-    for g in range(GROUPS):
-        rows = slice(2 * g * share, 2 * (g + 1) * share)
-        part = jnp.where(near, kept[rows], arrived[rows])
-        owns += [jnp.where(beside, part[:share], swapped(part[share:], 3))]
-        acrosses += [swapped(owns[g], 3)]
+    share = half // 2
+    passing = swapped(block[half + share :], 1)
+    staying = swapped(block[half : half + share], 1)
+    passing, proj = lax.optimization_barrier((passing, proj))
+    passing = jnp.where(near, kept[share:], passing)
+    staying = jnp.where(near, kept[:share], staying)
+    own = jnp.where(beside, staying, swapped(passing, 3))
+    across = swapped(own, 3)
     lifted = lifted_with(proj)
-    acrosses, lifted = lax.optimization_barrier((acrosses, lifted))
-    upper = [piece for pair in zip(owns, acrosses) for piece in pair]
-    lower = [swapped(piece, 1) for piece in upper]
+    across, lifted = lax.optimization_barrier((across, lifted))
+    upper = [own, across]
+    lower = [swapped(own, 1), swapped(across, 1)]
     result, *edges = rest(False, side_first, place_first, lifted, upper, [])
     (result,) = rest(True, side_first, place_first, lifted, lower, [*edges, result])
     return result[None, None]

time: 33.5 us -> 32.5 us (0.970)
  waiting for transfers between devices: 5.83 us -> 4.76 us
    ppermute x5 -> x6, waiting for transfers between devices: 4.63 us -> 3.55 us  [swapped(): return lax.ppermute(block, 'patch', [(i, i ^ bit) for i in range(count)])]
    ppermute x5 -> x6, starting transfers between devices: 13.1 us -> 13.1 us  [swapped(): return lax.ppermute(block, 'patch', [(i, i ^ bit) for i in range(count)])]
    slice x2 -> x1, local copies, waits for them, and re-layouts: 1 us -> 1.01 us  [per_device(): staying = swapped(block[half:half + share], 1)]
  transfers between devices with their start and end apart: 7 -> 8, of which waited for: 4 -> 4; matrix products, arithmetic and copies ran while one was open for 0% -> 0% of each run, Pallas kernels for 28% -> 28%
where the time goes in v5:
time: 32.5 us; the launch traced here: 32.3 us
  starting transfers between devices  13.6 us (42%)
  Pallas kernels  12.7 us (39%)
  waiting for transfers between devices  4.76 us (15%)
  local copies, waits for them, and re-layouts  1.03 us (3%)
    ppermute x6, starting transfers between devices, swapped(): return lax.ppermute(block, 'patch', [(i, i ^ bit) for i in range(count)])  13.1 us
    pallas_call x2, Pallas kernels, rest_part(): pl.pallas_call(lambda *refs: rest_kernel(second, side_of, place, *refs),...  6.74 us
    pallas_call x1, Pallas kernels, resident_part(): pl.pallas_call(resident_kernel, out_shape=tuple((space(*kind) for space,...  4.72 us
    ppermute x6, waiting for transfers between devices, swapped(): return lax.ppermute(block, 'patch', [(i, i ^ bit) for i in range(count)])  3.55 us
    pallas_call x1, Pallas kernels, mix_part(): pl.pallas_call(mix_kernel, out_shape=pltpu.VMEM((2 * own.shape[0], 2 * ou...  1.26 us
    ppermute x2, waiting for transfers between devices, rotated(): lax.ppermute(block, axis, [(i, (i + distance) % count) for i in range(cou...  1.21 us
    slice x1, local copies, waits for them, and re-layouts, per_device(): staying = swapped(block[half:half + share], 1)  1.01 us
  transfers between devices with their start and end apart: 8, of which 4 were waited for; matrix products, arithmetic and copies ran while one was open for 0% of the time, Pallas kernels for 28%

profile of v5, /device:TPU:0, one launch (start us, length us, event | category | flops | bytes accessed | tf_op | source)
XLA Modules:
  0.0 32.3 jit_solution(6707520640361132399)
XLA Ops:
  0.0 1.0 %slice_bitcast_fusion.1 = (bf16[32,2048]{1,0:T(8,128)(2,1)S(1)}, bf16[32,2048]{1,0:T(8,128)(2,1)S(1)}) fusion(bf16[1,1,128,2048]{3,2,1,0:T(8,128)(2,1)} %param.10), kind=kLoop, calls=%fused_computation.3 | loop fusion | bytes 524288 | tf_op jit(solution)/shard_map/slice | solution.py:438
  1.0 3.1 %collective-permute-start.1 = (bf16[32,2048]{1,0:T(8,128)(2,1)S(1)}, bf16[32,2048]{1,0:T(8,128)(2,1)S(1)}, u32[]{:S(2)}, u32[]{:S(2)}) collective-permute-start(bf16[32,2048]{1,0:T(8,128)(2,1)S(1)} %get-tuple-element.36), channel_id=1, source_target_pairs={{0,4},{4,0},{8,12},{12,8},{1,5},{5,1},{9,13},{13,9},{2,6},{6,2},{1... | collective-permute-start | bytes 393224 | tf_op jit(solution)/shard_map/ppermute | solution.py:399
  4.1 0.1 collective-permute-start
  4.2 4.7 %resident_part.1 = (f32[2048,256]{1,0:T(8,128)S(1)}, bf16[1024,128]{1,0:T(8,128)(2,1)S(1)}, s32[2,1,2048]{2,1,0:T(1,128)S(1)}, bf16[64,2048]{1,0:T(8,128)(2,1)S(...) custom-call(s32[4]{0:T(128)} %refs_0_.3, ...), custom_call_target="tpu_custom_call" | custom-call | flops 1024 | bytes 1024 | tf_op jit(solution)/shard_map/resident_part/pallas_call | solution.py:177
  8.9 0.0 copy-start.2
  8.9 0.1 compare_reduce_fusion.1
  9.0 0.0 collective-permute-done.1
  9.0 4.0 %collective-permute-start.2 = (bf16[32,2048]{1,0:T(8,128)(2,1)S(1)}, bf16[32,2048]{1,0:T(8,128)(2,1)S(1)}, u32[]{:S(2)}, u32[]{:S(2)}) collective-permute-start(bf16[32,2048]{1,0:T(8,128)(2,1)S(1)} %slice_select_fusion), channel_id=1, source_target_pairs={{0,12},{4,8},{8,4},{12,0},{1,13},{5,9},{9,5},{13,1},{2,14},{6,10},... | collective-permute-start | bytes 393224 | tf_op jit(solution)/shard_map/ppermute | solution.py:399
  13.1 0.1 collective-permute-start.5
  13.2 0.4 %collective-permute-start.4 = (bf16[1024,128]{1,0:T(8,128)(2,1)S(1)}, bf16[1024,128]{1,0:T(8,128)(2,1)S(1)}, u32[]{:S(2)}, u32[]{:S(2)}) collective-permute-start(bf16[1024,128]{1,0:T(8,128)(2,1)S(1)} %get-tuple-element.24.self_ref), channel_id=1, source_target_pairs={{0,1},{1,2},{2,3},{3,0},{4,5},{5,6},{6,7},{7,4},{8,9},{9,10},{10,1... | collective-permute-start | bytes 786440 | tf_op jit(solution)/shard_map/ppermute | solution.py:394
  13.6 0.0 collective-permute-done
  13.6 2.5 %collective-permute-done.2 = bf16[32,2048]{1,0:T(8,128)(2,1)S(1)} collective-permute-done((bf16[32,2048]{1,0:T(8,128)(2,1)S(1)}, bf16[32,2048]{1,0:T(8,128)(2,1)S(1)}, u32[]{:S(2)}, u32[]{:S(2)}) %collective-permute-start.2) | collective-permute-done | bytes 131104 | tf_op jit(solution)/shard_map/ppermute | solution.py:399
  16.2 3.9 %collective-permute-start.3 = (bf16[32,2048]{1,0:T(8,128)(2,1)S(1)}, bf16[32,2048]{1,0:T(8,128)(2,1)S(1)}, u32[]{:S(2)}, u32[]{:S(2)}) collective-permute-start(bf16[32,2048]{1,0:T(8,128)(2,1)S(1)} %select_select_fusion.refs_6_), channel_id=1, source_target_pairs={{0,12},{4,8},{8,4},{12,0},{1,13},{5,9},{9,5},{13,1},{2,14},{6,10},... | collective-permute-start | bytes 393224 | tf_op jit(solution)/shard_map/ppermute | solution.py:399
  20.0 0.5 %collective-permute-start.6 = (bf16[32,2048]{1,0:T(8,128)(2,1)S(1)}, bf16[32,2048]{1,0:T(8,128)(2,1)S(1)}, u32[]{:S(2)}, u32[]{:S(2)}) collective-permute-start(bf16[32,2048]{1,0:T(8,128)(2,1)S(1)} %select_select_fusion.refs_6_), channel_id=1, source_target_pairs={{0,4},{4,0},{8,12},{12,8},{1,5},{5,1},{9,13},{13,9},{2,6},{6,2},{1... | collective-permute-start | bytes 393224 | tf_op jit(solution)/shard_map/ppermute | solution.py:399
  20.5 0.0 collective-permute-done.5.next_ref
  20.5 1.2 %collective-permute-done.4.prev_ref = bf16[1024,128]{1,0:T(8,128)(2,1)S(1)} collective-permute-done((bf16[1024,128]{1,0:T(8,128)(2,1)S(1)}, bf16[1024,128]{1,0:T(8,128)(2,1)S(1)}, u32[]{:S(2)}, u32[]{:S(2)}) %collective-permute-start.4) | collective-permute-done | bytes 262176 | tf_op jit(solution)/shard_map/ppermute | solution.py:394
  21.7 0.0 copy-done.1
  21.7 1.3 %mix_part.1.refs_2_ = f32[2048,256]{1,0:T(8,128)S(1)} custom-call(s32[4]{0:T(128)S(1)} %copy-done.3, bf16[1024,128]{1,0:T(8,128)(2,1)S(1)} %collective-permute-done.4.prev_ref, bf16[1024,128]{1,0:T(8,128)(2,1)S(1)} %get-tuple-element.24.self_ref, bf16[1024,128]{1,0:T(8,128)(2,1)S(1)} %collective-permute-done.5.next_ref, bf16[3,32,32]{2,1,0:T(8,128)(2,1)S(1)} %copy-done, ...), custom_call_target="tpu_custom_call" | custom-call | flops 100663296 | bytes 1048576 | tf_op jit(solution)/shard_map/mix_part/pallas_call | solution.py:239
  23.0 0.8 %collective-permute-done.3.refs_7_ = bf16[32,2048]{1,0:T(8,128)(2,1)S(1)} collective-permute-done((bf16[32,2048]{1,0:T(8,128)(2,1)S(1)}, bf16[32,2048]{1,0:T(8,128)(2,1)S(1)}, u32[]{:S(2)}, u32[]{:S(2)}) %collective-permute-start.3) | collective-permute-done | bytes 131104 | tf_op jit(solution)/shard_map/ppermute | solution.py:399
  23.8 1.5 %collective-permute-start.7 = (bf16[32,2048]{1,0:T(8,128)(2,1)S(1)}, bf16[32,2048]{1,0:T(8,128)(2,1)S(1)}, u32[]{:S(2)}, u32[]{:S(2)}) collective-permute-start(bf16[32,2048]{1,0:T(8,128)(2,1)S(1)} %collective-permute-done.3.refs_7_), channel_id=1, source_target_pairs={{0,4},{4,0},{8,12},{12,8},{1,5},{5,1},{9,13},{13,9},{2,6},{6,2},{1... | collective-permute-start | bytes 393224 | tf_op jit(solution)/shard_map/ppermute | solution.py:399
  25.4 3.2 %rest_first.1 = (bf16[128,32,128]{2,1,0:T(8,128)(2,1)}, bf16[32,256]{1,0:T(8,128)(2,1)S(1)}, bf16[32,512]{1,0:T(8,128)(2,1)S(1)}) custom-call(s32[4]{0:T(128)S(1)} %copy-done.2, f32[2048,256]{1,0:T(8,128)S(1)} %get-tuple-element.19.refs_1_, f32[2048,256]{1,0:T(8,128)S(1)} %mix_part.1.refs_2_, bf16[128,32,128]{2,1,0:T(8,128)(2,1)S(1)} %get-tuple-element.26.refs_3_, ...), custom_call_target="tpu_custom_call" | custom-call | flops 1610612736 | bytes 4194304 | tf_op jit(solution)/shard_map/rest_first/pallas_call | solution.py:359
  28.6 0.0 collective-permute-done.6.refs_6_
  28.6 0.2 collective-permute-done.7.refs_7_
  28.8 3.5 %rest_second.1 = bf16[128,32,128]{2,1,0:T(8,128)(2,1)} custom-call(s32[4]{0:T(128)S(1)} %copy-done.2, f32[2048,256]{1,0:T(8,128)S(1)} %get-tuple-element.19.refs_1_, f32[2048,256]{1,0:T(8,128)S(1)} %mix_part.1.refs_2_, bf16[128,32,128]{2,1,0:T(8,128)(2,1)S(1)} %get-tuple-element.26.refs_3_, ...), custom_call_target="tpu_custom_call", output_to_operand_aliasing={{}: (10, {})} | custom-call | flops 1660944384 | bytes 4194304 | tf_op jit(solution)/shard_map/rest_second/pallas_call | solution.py:359
  (8 shorter events, 0.1 us)
Async XLA Ops:
  0.0 21.7 %copy-start.1 = (bf16[32,128]{1,0:T(8,128)(2,1)S(1)}, bf16[32,128]{1,0:T(8,128)(2,1)}, u32[]{:S(2)}) copy-start(bf16[32,128]{1,0:T(8,128)(2,1)} %out_ref.1) | copy-start | bytes 24580
  0.0 21.7 %copy-start = (bf16[3,32,32]{2,1,0:T(8,128)(2,1)S(1)}, bf16[3,32,32]{2,1,0:T(8,128)(2,1)}, u32[]{:S(2)}) copy-start(bf16[3,32,32]{2,1,0:T(8,128)(2,1)} %mix_ref.1) | copy-start | bytes 18436
  0.0 21.7 %copy-start.3 = (s32[4]{0:T(128)S(1)}, s32[4]{0:T(128)}, u32[]{:S(2)}) copy-start(s32[4]{0:T(128)} %hours_ref.1) | copy-start | bytes 52
  1.0 8.0 %collective-permute-start.1 = (bf16[32,2048]{1,0:T(8,128)(2,1)S(1)}, bf16[32,2048]{1,0:T(8,128)(2,1)S(1)}, u32[]{:S(2)}, u32[]{:S(2)}) collective-permute-start(bf16[32,2048]{1,0:T(8,128)(2,1)S(1)} %get-tuple-element.36), channel_id=1, source_target_pairs={{0,4},{4,0},{8,12},{12,8},{1,5},{5,1},{9,13},{13,9},{2,6},{6,2},{1... | collective-permute-start | bytes 393224 | tf_op jit(solution)/shard_map/ppermute | solution.py:399
  4.1 9.5 %collective-permute-start = (bf16[32,2048]{1,0:T(8,128)(2,1)S(1)}, bf16[32,2048]{1,0:T(8,128)(2,1)S(1)}, u32[]{:S(2)}, u32[]{:S(2)}) collective-permute-start(bf16[32,2048]{1,0:T(8,128)(2,1)S(1)} %get-tuple-element.35), channel_id=1, source_target_pairs={{0,4},{4,0},{8,12},{12,8},{1,5},{5,1},{9,13},{13,9},{2,6},{6,2},{1... | collective-permute-start | bytes 393224 | tf_op jit(solution)/shard_map/ppermute | solution.py:399
  8.9 16.4 %copy-start.2 = (s32[4]{0:T(128)S(1)}, s32[4]{0:T(128)}, u32[]{:S(2)}) copy-start(s32[4]{0:T(128)} %refs_0_.3) | copy-start | bytes 52
  9.0 7.1 %collective-permute-start.2 = (bf16[32,2048]{1,0:T(8,128)(2,1)S(1)}, bf16[32,2048]{1,0:T(8,128)(2,1)S(1)}, u32[]{:S(2)}, u32[]{:S(2)}) collective-permute-start(bf16[32,2048]{1,0:T(8,128)(2,1)S(1)} %slice_select_fusion), channel_id=1, source_target_pairs={{0,12},{4,8},{8,4},{12,0},{1,13},{5,9},{9,5},{13,1},{2,14},{6,10},... | collective-permute-start | bytes 393224 | tf_op jit(solution)/shard_map/ppermute | solution.py:399
  13.1 7.4 %collective-permute-start.5 = (bf16[1024,128]{1,0:T(8,128)(2,1)S(1)}, bf16[1024,128]{1,0:T(8,128)(2,1)S(1)}, u32[]{:S(2)}, u32[]{:S(2)}) collective-permute-start(bf16[1024,128]{1,0:T(8,128)(2,1)S(1)} %get-tuple-element.24.self_ref), channel_id=1, source_target_pairs={{0,3},{1,0},{2,1},{3,2},{4,7},{5,4},{6,5},{7,6},{8,11},{9,8},{10,9... | collective-permute-start | bytes 786440 | tf_op jit(solution)/shard_map/ppermute | solution.py:394
  13.2 8.6 %collective-permute-start.4 = (bf16[1024,128]{1,0:T(8,128)(2,1)S(1)}, bf16[1024,128]{1,0:T(8,128)(2,1)S(1)}, u32[]{:S(2)}, u32[]{:S(2)}) collective-permute-start(bf16[1024,128]{1,0:T(8,128)(2,1)S(1)} %get-tuple-element.24.self_ref), channel_id=1, source_target_pairs={{0,1},{1,2},{2,3},{3,0},{4,5},{5,6},{6,7},{7,4},{8,9},{9,10},{10,1... | collective-permute-start | bytes 786440 | tf_op jit(solution)/shard_map/ppermute | solution.py:394
  16.2 7.7 %collective-permute-start.3 = (bf16[32,2048]{1,0:T(8,128)(2,1)S(1)}, bf16[32,2048]{1,0:T(8,128)(2,1)S(1)}, u32[]{:S(2)}, u32[]{:S(2)}) collective-permute-start(bf16[32,2048]{1,0:T(8,128)(2,1)S(1)} %select_select_fusion.refs_6_), channel_id=1, source_target_pairs={{0,12},{4,8},{8,4},{12,0},{1,13},{5,9},{9,5},{13,1},{2,14},{6,10},... | collective-permute-start | bytes 393224 | tf_op jit(solution)/shard_map/ppermute | solution.py:399
  20.0 8.6 %collective-permute-start.6 = (bf16[32,2048]{1,0:T(8,128)(2,1)S(1)}, bf16[32,2048]{1,0:T(8,128)(2,1)S(1)}, u32[]{:S(2)}, u32[]{:S(2)}) collective-permute-start(bf16[32,2048]{1,0:T(8,128)(2,1)S(1)} %select_select_fusion.refs_6_), channel_id=1, source_target_pairs={{0,4},{4,0},{8,12},{12,8},{1,5},{5,1},{9,13},{13,9},{2,6},{6,2},{1... | collective-permute-start | bytes 393224 | tf_op jit(solution)/shard_map/ppermute | solution.py:399
  23.8 5.0 %collective-permute-start.7 = (bf16[32,2048]{1,0:T(8,128)(2,1)S(1)}, bf16[32,2048]{1,0:T(8,128)(2,1)S(1)}, u32[]{:S(2)}, u32[]{:S(2)}) collective-permute-start(bf16[32,2048]{1,0:T(8,128)(2,1)S(1)} %collective-permute-done.3.refs_7_), channel_id=1, source_target_pairs={{0,4},{4,0},{8,12},{12,8},{1,5},{5,1},{9,13},{13,9},{2,6},{6,2},{1... | collective-permute-start | bytes 393224 | tf_op jit(solution)/shard_map/ppermute | solution.py:399

commit v6 on v5

--- a/solution.py
+++ b/solution.py
@@ -92,9 +92,9 @@
 
 
 def resident_kernel(
-    owner_ref, x_hbm, first_hbm, second_hbm, w_in_hbm, block_hbm,
+    owner_hbm, x_hbm, first_hbm, second_hbm, w_in_hbm, block_hbm,
     acc_ref, proj_ref, flags_ref, block_ref, w_second_ref, w_glob_ref, x_ref,
-    first_ref, second_ref, in_ref, cells, taps, w_first, w_in, sems,
+    first_ref, second_ref, in_ref, owner_ref, cells, taps, w_first, w_in, sems,
 ):
     height, width, channels = x_ref.shape
     pairs = width // 2
@@ -111,12 +111,10 @@
             (first_hbm, first_ref),
             (second_hbm, second_ref),
             (block_hbm.at[pl.ds(0, block_ref.shape[0]), :], block_ref),
+            (owner_hbm, owner_ref),
         ],
         sems,
     )
-    away = patches_away(owner_ref)
-    flags_ref[0] = jnp.full(flags_ref.shape[1:], away & 1, jnp.int32)
-    flags_ref[1] = jnp.full(flags_ref.shape[1:], away & 2, jnp.int32)
     clear_edges(taps, pairs)
     w_in[...] = jnp.zeros_like(w_in)
     left, right = column_masks(CHUNK, channels, pairs)
@@ -155,6 +153,10 @@
     for start in range(0, rows, WIDE):
         acc_ref[pl.ds(start, WIDE), :] = pair_taps(taps, w_first, start, WIDE, pairs)
     copies[parts + 3].wait()
+    copies[parts + 4].wait()
+    away = patches_away(owner_ref)
+    flags_ref[0] = jnp.full(flags_ref.shape[1:], away & 1, jnp.int32)
+    flags_ref[1] = jnp.full(flags_ref.shape[1:], away & 2, jnp.int32)
 
 
 def resident_part(owner, x, w_first, w_second, w_in, block):
@@ -179,17 +181,18 @@
         out_shape=tuple(
             space(*kind) for space, kind in zip((pltpu.VMEM,) * 7, results)
         ),
-        in_specs=[pl.BlockSpec(memory_space=pltpu.SMEM)] + in_hbm(5),
+        in_specs=in_hbm(6),
         out_specs=tuple(in_vmem(7)),
         scratch_shapes=[
             pltpu.VMEM(w_first.shape, BF16),
             pltpu.VMEM(w_second.shape, BF16),
             pltpu.VMEM(w_in.shape, BF16),
+            pltpu.SMEM(owner.shape, jnp.int32),
             pltpu.VMEM((2 * rows + 2 * EDGE, channels), F32),
             pltpu.VMEM((rows + 2 * pairs, 4 * channels), BF16),
             pltpu.VMEM((12 * channels, 2 * out), BF16),
             pltpu.VMEM((4 * temporal, 4 * channels), BF16),
-            pltpu.SemaphoreType.DMA((10,)),
+            pltpu.SemaphoreType.DMA((9,)),
         ],
         compiler_params=pltpu.CompilerParams(vmem_limit_bytes=VMEM_BYTES),
         cost_estimate=pl.CostEstimate(flops=1024, bytes_accessed=1024, transcendentals=0),
@@ -198,21 +201,12 @@
 
 
 def mix_kernel(
-    hours_ref, prev_ref, self_ref, next_ref, mix_ref, out_ref, lifted_ref, w_mix, w_lift, mixed_ref
+    hours_hbm, prev_ref, self_ref, next_ref, mix_ref, out_ref, lifted_ref,
+    w_mix, w_lift, mixed_ref, hours_ref, sem,
 ):
-    leads = hours_ref.shape[0]
+    hours_copy = pltpu.make_async_copy(hours_hbm, hours_ref, sem)
+    hours_copy.start()
     temporal = mix_ref.shape[1]
-    lead = lax.axis_index("lead")
-    now = hours_ref[lead]
-    before = hours_ref[jnp.maximum(lead - 1, 0)]
-    after = hours_ref[jnp.minimum(lead + 1, leads - 1)]
-
-    def gain(gap, used):
-        gap = jnp.full((1, 4 * temporal), gap, jnp.int32).astype(F32)
-        return jnp.where(used, jnp.exp(-0.5 * (gap - 1.0)), 0.0)
-
-    gain_prev = gain(now - before, lead > 0)
-    gain_next = gain(after - now, lead < leads - 1)
     w_mix[...] = jnp.zeros_like(w_mix)
     for k in range(3):
         for s in range(4):
@@ -224,6 +218,19 @@
             w_lift[
                 s, pl.ds((2 * s + q) * temporal, temporal), pl.ds(q * out, out)
             ] = out_ref[...]
+    hours_copy.wait()
+    leads = hours_ref.shape[0]
+    lead = lax.axis_index("lead")
+    now = hours_ref[lead]
+    before = hours_ref[jnp.maximum(lead - 1, 0)]
+    after = hours_ref[jnp.minimum(lead + 1, leads - 1)]
+
+    def gain(gap, used):
+        gap = jnp.full((1, 4 * temporal), gap, jnp.int32).astype(F32)
+        return jnp.where(used, jnp.exp(-0.5 * (gap - 1.0)), 0.0)
+
+    gain_prev = gain(now - before, lead > 0)
+    gain_next = gain(after - now, lead < leads - 1)
     for start in range(0, rows, CHUNK):
         part = pl.ds(start, CHUNK)
         value = gain_prev * dot(prev_ref[part, :], w_mix[0])
@@ -239,19 +246,21 @@
     return pl.pallas_call(
         mix_kernel,
         out_shape=pltpu.VMEM((2 * own.shape[0], 2 * out), F32),
-        in_specs=[pl.BlockSpec(memory_space=pltpu.SMEM)] + in_vmem(5),
+        in_specs=in_hbm(1) + in_vmem(5),
         out_specs=in_vmem(1)[0],
         scratch_shapes=[
             pltpu.VMEM((3, lanes, lanes), BF16),
             pltpu.VMEM((2, lanes, 2 * out), BF16),
             pltpu.VMEM(own.shape, BF16),
+            pltpu.SMEM(hours.shape, jnp.int32),
+            pltpu.SemaphoreType.DMA(()),
         ],
         compiler_params=pltpu.CompilerParams(vmem_limit_bytes=VMEM_BYTES),
         cost_estimate=pl.CostEstimate(
             flops=6 * own.shape[0] * lanes * lanes, bytes_accessed=1024 * 1024, transcendentals=0
         ),
         name="mix_part",
-    )(hours, before, own, after, w_mix, w_out)
+    )(*at_hbm(hours), before, own, after, w_mix, w_out)
 
 
 def row_parts(rows, pairs):
@@ -260,7 +269,7 @@
     return [(low, high - low) for low, high in zip(bounds, bounds[1:])]
 
 
-def rest_kernel(second, side_of, place, owner_ref, acc_ref, lifted_ref, *refs):
+def rest_kernel(second, side_of, place, flags_ref, acc_ref, lifted_ref, *refs):
     x_ref, w_second_ref, w_glob_ref, *refs = refs
     middle, refs = refs[:-8], refs[-8:]
     out_ref, glob_cells, glob_taps, odd, even, taps, cells, sems = refs
@@ -274,7 +283,8 @@
     lanes = glob_cells.shape[1]
     share = pieces[0].shape[0]
     half = share * len(pieces)
-    side = side_of(owner_ref)
+    away = jnp.max(flags_ref[0, :, :128]) + jnp.max(flags_ref[1, :, :128])
+    side = side_of(away)
     first = (1 - side) * (half - 2) if second else side * half
     act_first = (1 - side) * (half - 1) if second else side * half
     act_rows = half + 1 if second else half
@@ -287,7 +297,7 @@
     clear_edges(glob_taps, pairs)
     clear_edges(taps, pairs)
     for k, piece in enumerate(pieces):
-        base = EDGE + at(place(owner_ref, k) * share)
+        base = EDGE + at(place(away, k) * share)
         for m in range(pairs):
             value = piece[:, pl.ds(m * lanes, lanes)].astype(F32)
             glob_cells[pl.ds(base + m, share, stride=pairs), :] = value
@@ -343,7 +353,7 @@
         write.wait()
 
 
-def rest_part(second, side_of, place, owner, acc, lifted, x, w_second, w_glob, pieces, carried):
+def rest_part(second, side_of, place, flags, acc, lifted, x, w_second, w_glob, pieces, carried):
     _, width, channels = x.shape
     pairs = width // 2
     lanes = pieces[0].shape[1] // pairs
@@ -359,8 +369,7 @@
     return pl.pallas_call(
         lambda *refs: rest_kernel(second, side_of, place, *refs),
         out_shape=results,
-        in_specs=[pl.BlockSpec(memory_space=pltpu.SMEM)]
-        + in_vmem(5 + len(pieces))
+        in_specs=in_vmem(6 + len(pieces))
         + (in_vmem(2) + in_hbm(1) if second else []),
         out_specs=tuple(in_hbm(1) + in_vmem(len(results) - 1)),
         input_output_aliases={8 + len(pieces): 0} if second else {},
@@ -382,8 +391,7 @@
         ),
         name="rest_second" if second else "rest_first",
     )(
-        owner,
-        *(space(a, pltpu.VMEM) for a in (acc, lifted, x, w_second, w_glob)),
+        *(space(a, pltpu.VMEM) for a in (flags, acc, lifted, x, w_second, w_glob)),
         *pieces,
         *carried,
     )
@@ -399,13 +407,12 @@
     return lax.ppermute(block, "patch", [(i, i ^ bit) for i in range(count)])
 
 
-def side_first(owner_ref):
-    away = patches_away(owner_ref)
+def side_first(away):
     return (away ^ (away >> 1)) & 1
 
 
-def place_first(owner_ref, k):
-    return ((patches_away(owner_ref) >> 1) ^ k) & 1
+def place_first(away, k):
+    return ((away >> 1) ^ k) & 1
 
 
 def per_device(
@@ -421,13 +428,13 @@
         return mix_part(hours, before, proj, after, w_lead_mix, w_lead_out)
 
     def rest(second, side_of, place, lifted, pieces, carried):
-        return rest_part(second, side_of, place, owner, acc, lifted, resident, w_second, w_glob, pieces, carried)
+        return rest_part(second, side_of, place, flags, acc, lifted, resident, w_second, w_glob, pieces, carried)
 
     if lax.axis_size("patch") != 4:
         mine = lax.axis_index("patch") == owner[lax.axis_index("lead")]
         whole = lax.psum(jnp.where(mine, block, jnp.zeros_like(block)), "patch")
         result, _, _ = rest(
-            False, lambda ref: 0, lambda ref, k: k, lifted_with(proj), [whole], []
+            False, lambda away: 0, lambda away, k: k, lifted_with(proj), [whole], []
         )
         return result[None, None]
 

time: 32.5 us -> 31.4 us (0.966)
  Pallas kernels: 12.7 us -> 11.3 us
  starting transfers between devices: 13.6 us -> 14.1 us
    pallas_call x2, Pallas kernels: 6.74 us -> 5.93 us  [rest_part(): pl.pallas_call(lambda *refs: rest_kernel(second, side_of, place, *refs),...]
    pallas_call x1, Pallas kernels: 4.72 us -> 4.07 us  [resident_part(): pl.pallas_call(resident_kernel, out_shape=tuple((space(*kind) for space,...]
    ppermute x6, starting transfers between devices: 13.1 us -> 13.6 us  [swapped(): return lax.ppermute(block, 'patch', [(i, i ^ bit) for i in range(count)])]
  transfers between devices with their start and end apart: 8 -> 8, of which waited for: 4 -> 5; matrix products, arithmetic and copies ran while one was open for 0% -> 0% of each run, Pallas kernels for 28% -> 26%
where the time goes in v6:
time: 31.4 us; the launch traced here: 31.3 us
  starting transfers between devices  14.1 us (45%)
  Pallas kernels  11.3 us (36%)
  waiting for transfers between devices  4.69 us (15%)
  local copies, waits for them, and re-layouts  1.01 us (3%)
    ppermute x6, starting transfers between devices, swapped(): return lax.ppermute(block, 'patch', [(i, i ^ bit) for i in range(count)])  13.6 us
    pallas_call x2, Pallas kernels, rest_part(): pl.pallas_call(lambda *refs: rest_kernel(second, side_of, place, *refs),...  5.93 us
    pallas_call x1, Pallas kernels, resident_part(): pl.pallas_call(resident_kernel, out_shape=tuple((space(*kind) for space,...  4.07 us
    ppermute x6, waiting for transfers between devices, swapped(): return lax.ppermute(block, 'patch', [(i, i ^ bit) for i in range(count)])  3.57 us
    pallas_call x1, Pallas kernels, mix_part(): pl.pallas_call(mix_kernel, out_shape=pltpu.VMEM((2 * own.shape[0], 2 * ou...  1.33 us
    ppermute x2, waiting for transfers between devices, rotated(): lax.ppermute(block, axis, [(i, (i + distance) % count) for i in range(cou...  1.13 us
    slice x1, local copies, waits for them, and re-layouts, per_device(): staying = swapped(block[half:half + share], 1)  1 us
  transfers between devices with their start and end apart: 8, of which 5 were waited for; matrix products, arithmetic and copies ran while one was open for 0% of the time, Pallas kernels for 26%

profile of v6, /device:TPU:0, one launch (start us, length us, event | category | flops | bytes accessed | tf_op | source)
XLA Modules:
  0.0 31.3 jit_solution(4473401770904401685)
XLA Ops:
  0.0 1.0 %slice_bitcast_fusion.1 = (bf16[32,2048]{1,0:T(8,128)(2,1)S(1)}, bf16[32,2048]{1,0:T(8,128)(2,1)S(1)}) fusion(bf16[1,1,128,2048]{3,2,1,0:T(8,128)(2,1)} %param.10), kind=kLoop, calls=%fused_computation.3 | loop fusion | bytes 524288 | tf_op jit(solution)/shard_map/slice | solution.py:445
  1.0 3.1 %collective-permute-start.1 = (bf16[32,2048]{1,0:T(8,128)(2,1)S(1)}, bf16[32,2048]{1,0:T(8,128)(2,1)S(1)}, u32[]{:S(2)}, u32[]{:S(2)}) collective-permute-start(bf16[32,2048]{1,0:T(8,128)(2,1)S(1)} %get-tuple-element.36), channel_id=1, source_target_pairs={{0,4},{4,0},{8,12},{12,8},{1,5},{5,1},{9,13},{13,9},{2,6},{6,2},{1... | collective-permute-start | bytes 393224 | tf_op jit(solution)/shard_map/ppermute | solution.py:407
  4.1 0.1 collective-permute-start
  4.2 4.1 %resident_part.1 = (f32[2048,256]{1,0:T(8,128)S(1)}, bf16[1024,128]{1,0:T(8,128)(2,1)S(1)}, s32[2,1,2048]{2,1,0:T(1,128)S(1)}, bf16[64,2048]{1,0:T(8,128)(2,1)S(...) custom-call(s32[4]{0:T(128)} %owner_hbm.1, ...), custom_call_target="tpu_custom_call" | custom-call | flops 1024 | bytes 1024 | tf_op jit(solution)/shard_map/resident_part/pallas_call | solution.py:179
  8.3 0.1 compare_reduce_fusion.1
  8.3 0.1 collective-permute-done.1
  8.4 4.1 %collective-permute-start.2 = (bf16[32,2048]{1,0:T(8,128)(2,1)S(1)}, bf16[32,2048]{1,0:T(8,128)(2,1)S(1)}, u32[]{:S(2)}, u32[]{:S(2)}) collective-permute-start(bf16[32,2048]{1,0:T(8,128)(2,1)S(1)} %slice_select_fusion), channel_id=1, source_target_pairs={{0,12},{4,8},{8,4},{12,0},{1,13},{5,9},{9,5},{13,1},{2,14},{6,10},... | collective-permute-start | bytes 393224 | tf_op jit(solution)/shard_map/ppermute | solution.py:407
  12.6 0.0 collective-permute-start.5
  12.6 0.5 %collective-permute-start.4 = (bf16[1024,128]{1,0:T(8,128)(2,1)S(1)}, bf16[1024,128]{1,0:T(8,128)(2,1)S(1)}, u32[]{:S(2)}, u32[]{:S(2)}) collective-permute-start(bf16[1024,128]{1,0:T(8,128)(2,1)S(1)} %get-tuple-element.24.self_ref), channel_id=1, source_target_pairs={{0,1},{1,2},{2,3},{3,0},{4,5},{5,6},{6,7},{7,4},{8,9},{9,10},{10,1... | collective-permute-start | bytes 786440 | tf_op jit(solution)/shard_map/ppermute | solution.py:402
  13.1 0.0 collective-permute-done
  13.1 2.5 %collective-permute-done.2 = bf16[32,2048]{1,0:T(8,128)(2,1)S(1)} collective-permute-done((bf16[32,2048]{1,0:T(8,128)(2,1)S(1)}, bf16[32,2048]{1,0:T(8,128)(2,1)S(1)}, u32[]{:S(2)}, u32[]{:S(2)}) %collective-permute-start.2) | collective-permute-done | bytes 131104 | tf_op jit(solution)/shard_map/ppermute | solution.py:407
  15.6 3.9 %collective-permute-start.3 = (bf16[32,2048]{1,0:T(8,128)(2,1)S(1)}, bf16[32,2048]{1,0:T(8,128)(2,1)S(1)}, u32[]{:S(2)}, u32[]{:S(2)}) collective-permute-start(bf16[32,2048]{1,0:T(8,128)(2,1)S(1)} %select_select_fusion.refs_6_), channel_id=1, source_target_pairs={{0,12},{4,8},{8,4},{12,0},{1,13},{5,9},{9,5},{13,1},{2,14},{6,10},... | collective-permute-start | bytes 393224 | tf_op jit(solution)/shard_map/ppermute | solution.py:407
  19.5 0.5 %collective-permute-start.6 = (bf16[32,2048]{1,0:T(8,128)(2,1)S(1)}, bf16[32,2048]{1,0:T(8,128)(2,1)S(1)}, u32[]{:S(2)}, u32[]{:S(2)}) collective-permute-start(bf16[32,2048]{1,0:T(8,128)(2,1)S(1)} %select_select_fusion.refs_6_), channel_id=1, source_target_pairs={{0,4},{4,0},{8,12},{12,8},{1,5},{5,1},{9,13},{13,9},{2,6},{6,2},{1... | collective-permute-start | bytes 393224 | tf_op jit(solution)/shard_map/ppermute | solution.py:407
  20.0 0.0 collective-permute-done.5.next_ref
  20.0 1.1 %collective-permute-done.4.prev_ref = bf16[1024,128]{1,0:T(8,128)(2,1)S(1)} collective-permute-done((bf16[1024,128]{1,0:T(8,128)(2,1)S(1)}, bf16[1024,128]{1,0:T(8,128)(2,1)S(1)}, u32[]{:S(2)}, u32[]{:S(2)}) %collective-permute-start.4) | collective-permute-done | bytes 262176 | tf_op jit(solution)/shard_map/ppermute | solution.py:402
  21.2 0.0 copy-done.1
  21.2 0.0 copy-done
  21.2 1.3 %mix_part.1.refs_2_ = f32[2048,256]{1,0:T(8,128)S(1)} custom-call(s32[4]{0:T(128)} %hours_hbm.1, bf16[1024,128]{1,0:T(8,128)(2,1)S(1)} %collective-permute-done.4.prev_ref, bf16[1024,128]{1,0:T(8,128)(2,1)S(1)} %get-tuple-element.24.self_ref, bf16[1024,128]{1,0:T(8,128)(2,1)S(1)} %collective-permute-done.5.next_ref, bf16[3,32,32]{2,1,0:T(8,128)(2,1)S(1)} %copy-done, ...), custom_call_target="tpu_custom_call" | custom-call | flops 100663296 | bytes 1048576 | tf_op jit(solution)/shard_map/mix_part/pallas_call | solution.py:246
  22.5 0.5 %collective-permute-done.3.refs_7_ = bf16[32,2048]{1,0:T(8,128)(2,1)S(1)} collective-permute-done((bf16[32,2048]{1,0:T(8,128)(2,1)S(1)}, bf16[32,2048]{1,0:T(8,128)(2,1)S(1)}, u32[]{:S(2)}, u32[]{:S(2)}) %collective-permute-start.3) | collective-permute-done | bytes 131104 | tf_op jit(solution)/shard_map/ppermute | solution.py:407
  23.0 1.8 %collective-permute-start.7 = (bf16[32,2048]{1,0:T(8,128)(2,1)S(1)}, bf16[32,2048]{1,0:T(8,128)(2,1)S(1)}, u32[]{:S(2)}, u32[]{:S(2)}) collective-permute-start(bf16[32,2048]{1,0:T(8,128)(2,1)S(1)} %collective-permute-done.3.refs_7_), channel_id=1, source_target_pairs={{0,4},{4,0},{8,12},{12,8},{1,5},{5,1},{9,13},{13,9},{2,6},{6,2},{1... | collective-permute-start | bytes 393224 | tf_op jit(solution)/shard_map/ppermute | solution.py:407
  24.9 2.8 %rest_first.1 = (bf16[128,32,128]{2,1,0:T(8,128)(2,1)}, bf16[32,256]{1,0:T(8,128)(2,1)S(1)}, bf16[32,512]{1,0:T(8,128)(2,1)S(1)}) custom-call(s32[2,1,2048]{2,1,0:T(1,128)S(1)} %get-tuple-element.19.refs_0_, f32[2048,256]{1,0:T(8,128)S(1)} %get-tuple-element.20.refs_1_, f32[2048,256]{1,0:T(8,128)S(1)} %mix_part.1.refs_2_, ...), custom_call_target="tpu_custom_call" | custom-call | flops 1610612736 | bytes 4194304 | tf_op jit(solution)/shard_map/rest_first/pallas_call | solution.py:369
  27.7 0.0 collective-permute-done.6.refs_6_
  27.7 0.4 %collective-permute-done.7.refs_7_ = bf16[32,2048]{1,0:T(8,128)(2,1)S(1)} collective-permute-done((bf16[32,2048]{1,0:T(8,128)(2,1)S(1)}, bf16[32,2048]{1,0:T(8,128)(2,1)S(1)}, u32[]{:S(2)}, u32[]{:S(2)}) %collective-permute-start.7) | collective-permute-done | bytes 131104 | tf_op jit(solution)/shard_map/ppermute | solution.py:407
  28.1 3.1 %rest_second.1 = bf16[128,32,128]{2,1,0:T(8,128)(2,1)} custom-call(s32[2,1,2048]{2,1,0:T(1,128)S(1)} %get-tuple-element.19.refs_0_, f32[2048,256]{1,0:T(8,128)S(1)} %get-tuple-element.20.refs_1_, f32[2048,256]{1,0:T(8,128)S(1)} %mix_part.1.refs_2_, bf16[128,32,128]{2,1,0:T(8,128)(2,1)S(1)} %get-tuple-element.26.refs_3_, ...), custom_call_target="tpu_custom_call", output_to_operand_aliasing={{}: (10, {})} | custom-call | flops 1660944384 | bytes 4194304 | tf_op jit(solution)/shard_map/rest_second/pallas_call | solution.py:369
  (4 shorter events, 0.0 us)
Async XLA Ops:
  0.0 21.2 %copy-start.1 = (bf16[32,128]{1,0:T(8,128)(2,1)S(1)}, bf16[32,128]{1,0:T(8,128)(2,1)}, u32[]{:S(2)}) copy-start(bf16[32,128]{1,0:T(8,128)(2,1)} %out_ref.1) | copy-start | bytes 24580
  0.0 21.2 %copy-start = (bf16[3,32,32]{2,1,0:T(8,128)(2,1)S(1)}, bf16[3,32,32]{2,1,0:T(8,128)(2,1)}, u32[]{:S(2)}) copy-start(bf16[3,32,32]{2,1,0:T(8,128)(2,1)} %mix_ref.1) | copy-start | bytes 18436
  1.0 7.4 %collective-permute-start.1 = (bf16[32,2048]{1,0:T(8,128)(2,1)S(1)}, bf16[32,2048]{1,0:T(8,128)(2,1)S(1)}, u32[]{:S(2)}, u32[]{:S(2)}) collective-permute-start(bf16[32,2048]{1,0:T(8,128)(2,1)S(1)} %get-tuple-element.36), channel_id=1, source_target_pairs={{0,4},{4,0},{8,12},{12,8},{1,5},{5,1},{9,13},{13,9},{2,6},{6,2},{1... | collective-permute-start | bytes 393224 | tf_op jit(solution)/shard_map/ppermute | solution.py:407
  4.1 9.0 %collective-permute-start = (bf16[32,2048]{1,0:T(8,128)(2,1)S(1)}, bf16[32,2048]{1,0:T(8,128)(2,1)S(1)}, u32[]{:S(2)}, u32[]{:S(2)}) collective-permute-start(bf16[32,2048]{1,0:T(8,128)(2,1)S(1)} %get-tuple-element.35), channel_id=1, source_target_pairs={{0,4},{4,0},{8,12},{12,8},{1,5},{5,1},{9,13},{13,9},{2,6},{6,2},{1... | collective-permute-start | bytes 393224 | tf_op jit(solution)/shard_map/ppermute | solution.py:407
  8.4 7.2 %collective-permute-start.2 = (bf16[32,2048]{1,0:T(8,128)(2,1)S(1)}, bf16[32,2048]{1,0:T(8,128)(2,1)S(1)}, u32[]{:S(2)}, u32[]{:S(2)}) collective-permute-start(bf16[32,2048]{1,0:T(8,128)(2,1)S(1)} %slice_select_fusion), channel_id=1, source_target_pairs={{0,12},{4,8},{8,4},{12,0},{1,13},{5,9},{9,5},{13,1},{2,14},{6,10},... | collective-permute-start | bytes 393224 | tf_op jit(solution)/shard_map/ppermute | solution.py:407
  12.6 7.4 %collective-permute-start.5 = (bf16[1024,128]{1,0:T(8,128)(2,1)S(1)}, bf16[1024,128]{1,0:T(8,128)(2,1)S(1)}, u32[]{:S(2)}, u32[]{:S(2)}) collective-permute-start(bf16[1024,128]{1,0:T(8,128)(2,1)S(1)} %get-tuple-element.24.self_ref), channel_id=1, source_target_pairs={{0,3},{1,0},{2,1},{3,2},{4,7},{5,4},{6,5},{7,6},{8,11},{9,8},{10,9... | collective-permute-start | bytes 786440 | tf_op jit(solution)/shard_map/ppermute | solution.py:402
  12.6 8.6 %collective-permute-start.4 = (bf16[1024,128]{1,0:T(8,128)(2,1)S(1)}, bf16[1024,128]{1,0:T(8,128)(2,1)S(1)}, u32[]{:S(2)}, u32[]{:S(2)}) collective-permute-start(bf16[1024,128]{1,0:T(8,128)(2,1)S(1)} %get-tuple-element.24.self_ref), channel_id=1, source_target_pairs={{0,1},{1,2},{2,3},{3,0},{4,5},{5,6},{6,7},{7,4},{8,9},{9,10},{10,1... | collective-permute-start | bytes 786440 | tf_op jit(solution)/shard_map/ppermute | solution.py:402
  15.6 7.4 %collective-permute-start.3 = (bf16[32,2048]{1,0:T(8,128)(2,1)S(1)}, bf16[32,2048]{1,0:T(8,128)(2,1)S(1)}, u32[]{:S(2)}, u32[]{:S(2)}) collective-permute-start(bf16[32,2048]{1,0:T(8,128)(2,1)S(1)} %select_select_fusion.refs_6_), channel_id=1, source_target_pairs={{0,12},{4,8},{8,4},{12,0},{1,13},{5,9},{9,5},{13,1},{2,14},{6,10},... | collective-permute-start | bytes 393224 | tf_op jit(solution)/shard_map/ppermute | solution.py:407
  19.5 8.2 %collective-permute-start.6 = (bf16[32,2048]{1,0:T(8,128)(2,1)S(1)}, bf16[32,2048]{1,0:T(8,128)(2,1)S(1)}, u32[]{:S(2)}, u32[]{:S(2)}) collective-permute-start(bf16[32,2048]{1,0:T(8,128)(2,1)S(1)} %select_select_fusion.refs_6_), channel_id=1, source_target_pairs={{0,4},{4,0},{8,12},{12,8},{1,5},{5,1},{9,13},{13,9},{2,6},{6,2},{1... | collective-permute-start | bytes 393224 | tf_op jit(solution)/shard_map/ppermute | solution.py:407
  23.0 5.1 %collective-permute-start.7 = (bf16[32,2048]{1,0:T(8,128)(2,1)S(1)}, bf16[32,2048]{1,0:T(8,128)(2,1)S(1)}, u32[]{:S(2)}, u32[]{:S(2)}) collective-permute-start(bf16[32,2048]{1,0:T(8,128)(2,1)S(1)} %collective-permute-done.3.refs_7_), channel_id=1, source_target_pairs={{0,4},{4,0},{8,12},{12,8},{1,5},{5,1},{9,13},{13,9},{2,6},{6,2},{1... | collective-permute-start | bytes 393224 | tf_op jit(solution)/shard_map/ppermute | solution.py:407

commit v7 on v6

--- a/solution.py
+++ b/solution.py
@@ -375,12 +375,12 @@
         input_output_aliases={8 + len(pieces): 0} if second else {},
         scratch_shapes=[
             pltpu.VMEM((rows, width, channels), BF16),
-            pltpu.VMEM((half * pairs + 2 * EDGE, lanes), F32),
+            pltpu.VMEM(((half + 1) * pairs + 2 * EDGE, lanes), F32),
             pltpu.VMEM(((rows + 2) * pairs, 2 * lanes), BF16),
             pltpu.VMEM(((half + 1) * pairs + 2 * EDGE, channels), F32),
             pltpu.VMEM(((half + 1) * pairs + 2 * EDGE, channels), F32),
             pltpu.VMEM(((rows + 2) * pairs, 4 * channels), BF16),
-            pltpu.VMEM((rows * width, channels), F32),
+            pltpu.VMEM((rows * width + EDGE, channels), F32),
             pltpu.SemaphoreType.DMA((2 * len(row_parts(rows, pairs)),)),
         ],
         compiler_params=pltpu.CompilerParams(vmem_limit_bytes=VMEM_BYTES),

time: 31.4 us -> 31.4 us (level)
  no operation moved by 1% of the time
where the time goes in v7:
time: 31.4 us; the launch traced here: 31.3 us
  starting transfers between devices  14.1 us (45%)
  Pallas kernels  11.3 us (36%)
  waiting for transfers between devices  4.69 us (15%)
  local copies, waits for them, and re-layouts  1.01 us (3%)
    ppermute x6, starting transfers between devices, swapped(): return lax.ppermute(block, 'patch', [(i, i ^ bit) for i in range(count)])  13.6 us
    pallas_call x2, Pallas kernels, rest_part(): pl.pallas_call(lambda *refs: rest_kernel(second, side_of, place, *refs),...  5.95 us
    pallas_call x1, Pallas kernels, resident_part(): pl.pallas_call(resident_kernel, out_shape=tuple((space(*kind) for space,...  4.07 us
    ppermute x6, waiting for transfers between devices, swapped(): return lax.ppermute(block, 'patch', [(i, i ^ bit) for i in range(count)])  3.57 us
    pallas_call x1, Pallas kernels, mix_part(): pl.pallas_call(mix_kernel, out_shape=pltpu.VMEM((2 * own.shape[0], 2 * ou...  1.33 us
    ppermute x2, waiting for transfers between devices, rotated(): lax.ppermute(block, axis, [(i, (i + distance) % count) for i in range(cou...  1.13 us
    slice x1, local copies, waits for them, and re-layouts, per_device(): staying = swapped(block[half:half + share], 1)  1 us
  transfers between devices with their start and end apart: 8, of which 5 were waited for; matrix products, arithmetic and copies ran while one was open for 0% of the time, Pallas kernels for 26%

profile of v7, /device:TPU:0, one launch (start us, length us, event | category | flops | bytes accessed | tf_op | source)
XLA Modules:
  0.0 31.3 jit_solution(12512443053669096096)
XLA Ops:
  0.0 1.0 %slice_bitcast_fusion.1 = (bf16[32,2048]{1,0:T(8,128)(2,1)S(1)}, bf16[32,2048]{1,0:T(8,128)(2,1)S(1)}) fusion(bf16[1,1,128,2048]{3,2,1,0:T(8,128)(2,1)} %param.10), kind=kLoop, calls=%fused_computation.3 | loop fusion | bytes 524288 | tf_op jit(solution)/shard_map/slice | solution.py:445
  1.0 3.1 %collective-permute-start.1 = (bf16[32,2048]{1,0:T(8,128)(2,1)S(1)}, bf16[32,2048]{1,0:T(8,128)(2,1)S(1)}, u32[]{:S(2)}, u32[]{:S(2)}) collective-permute-start(bf16[32,2048]{1,0:T(8,128)(2,1)S(1)} %get-tuple-element.36), channel_id=1, source_target_pairs={{0,4},{4,0},{8,12},{12,8},{1,5},{5,1},{9,13},{13,9},{2,6},{6,2},{1... | collective-permute-start | bytes 393224 | tf_op jit(solution)/shard_map/ppermute | solution.py:407
  4.1 0.1 collective-permute-start
  4.2 4.1 %resident_part.1 = (f32[2048,256]{1,0:T(8,128)S(1)}, bf16[1024,128]{1,0:T(8,128)(2,1)S(1)}, s32[2,1,2048]{2,1,0:T(1,128)S(1)}, bf16[64,2048]{1,0:T(8,128)(2,1)S(...) custom-call(s32[4]{0:T(128)} %owner_hbm.1, ...), custom_call_target="tpu_custom_call" | custom-call | flops 1024 | bytes 1024 | tf_op jit(solution)/shard_map/resident_part/pallas_call | solution.py:179
  8.3 0.1 compare_reduce_fusion.1
  8.3 0.1 collective-permute-done.1
  8.4 4.1 %collective-permute-start.2 = (bf16[32,2048]{1,0:T(8,128)(2,1)S(1)}, bf16[32,2048]{1,0:T(8,128)(2,1)S(1)}, u32[]{:S(2)}, u32[]{:S(2)}) collective-permute-start(bf16[32,2048]{1,0:T(8,128)(2,1)S(1)} %slice_select_fusion), channel_id=1, source_target_pairs={{0,12},{4,8},{8,4},{12,0},{1,13},{5,9},{9,5},{13,1},{2,14},{6,10},... | collective-permute-start | bytes 393224 | tf_op jit(solution)/shard_map/ppermute | solution.py:407
  12.6 0.0 collective-permute-start.5
  12.6 0.5 %collective-permute-start.4 = (bf16[1024,128]{1,0:T(8,128)(2,1)S(1)}, bf16[1024,128]{1,0:T(8,128)(2,1)S(1)}, u32[]{:S(2)}, u32[]{:S(2)}) collective-permute-start(bf16[1024,128]{1,0:T(8,128)(2,1)S(1)} %get-tuple-element.24.self_ref), channel_id=1, source_target_pairs={{0,1},{1,2},{2,3},{3,0},{4,5},{5,6},{6,7},{7,4},{8,9},{9,10},{10,1... | collective-permute-start | bytes 786440 | tf_op jit(solution)/shard_map/ppermute | solution.py:402
  13.1 0.0 collective-permute-done
  13.1 2.5 %collective-permute-done.2 = bf16[32,2048]{1,0:T(8,128)(2,1)S(1)} collective-permute-done((bf16[32,2048]{1,0:T(8,128)(2,1)S(1)}, bf16[32,2048]{1,0:T(8,128)(2,1)S(1)}, u32[]{:S(2)}, u32[]{:S(2)}) %collective-permute-start.2) | collective-permute-done | bytes 131104 | tf_op jit(solution)/shard_map/ppermute | solution.py:407
  15.6 3.9 %collective-permute-start.3 = (bf16[32,2048]{1,0:T(8,128)(2,1)S(1)}, bf16[32,2048]{1,0:T(8,128)(2,1)S(1)}, u32[]{:S(2)}, u32[]{:S(2)}) collective-permute-start(bf16[32,2048]{1,0:T(8,128)(2,1)S(1)} %select_select_fusion.refs_6_), channel_id=1, source_target_pairs={{0,12},{4,8},{8,4},{12,0},{1,13},{5,9},{9,5},{13,1},{2,14},{6,10},... | collective-permute-start | bytes 393224 | tf_op jit(solution)/shard_map/ppermute | solution.py:407
  19.5 0.5 %collective-permute-start.6 = (bf16[32,2048]{1,0:T(8,128)(2,1)S(1)}, bf16[32,2048]{1,0:T(8,128)(2,1)S(1)}, u32[]{:S(2)}, u32[]{:S(2)}) collective-permute-start(bf16[32,2048]{1,0:T(8,128)(2,1)S(1)} %select_select_fusion.refs_6_), channel_id=1, source_target_pairs={{0,4},{4,0},{8,12},{12,8},{1,5},{5,1},{9,13},{13,9},{2,6},{6,2},{1... | collective-permute-start | bytes 393224 | tf_op jit(solution)/shard_map/ppermute | solution.py:407
  20.0 0.0 collective-permute-done.5.next_ref
  20.0 1.1 %collective-permute-done.4.prev_ref = bf16[1024,128]{1,0:T(8,128)(2,1)S(1)} collective-permute-done((bf16[1024,128]{1,0:T(8,128)(2,1)S(1)}, bf16[1024,128]{1,0:T(8,128)(2,1)S(1)}, u32[]{:S(2)}, u32[]{:S(2)}) %collective-permute-start.4) | collective-permute-done | bytes 262176 | tf_op jit(solution)/shard_map/ppermute | solution.py:402
  21.2 0.0 copy-done.1
  21.2 0.0 copy-done
  21.2 1.3 %mix_part.1.refs_2_ = f32[2048,256]{1,0:T(8,128)S(1)} custom-call(s32[4]{0:T(128)} %hours_hbm.1, bf16[1024,128]{1,0:T(8,128)(2,1)S(1)} %collective-permute-done.4.prev_ref, bf16[1024,128]{1,0:T(8,128)(2,1)S(1)} %get-tuple-element.24.self_ref, bf16[1024,128]{1,0:T(8,128)(2,1)S(1)} %collective-permute-done.5.next_ref, bf16[3,32,32]{2,1,0:T(8,128)(2,1)S(1)} %copy-done, ...), custom_call_target="tpu_custom_call" | custom-call | flops 100663296 | bytes 1048576 | tf_op jit(solution)/shard_map/mix_part/pallas_call | solution.py:246
  22.5 0.5 %collective-permute-done.3.refs_7_ = bf16[32,2048]{1,0:T(8,128)(2,1)S(1)} collective-permute-done((bf16[32,2048]{1,0:T(8,128)(2,1)S(1)}, bf16[32,2048]{1,0:T(8,128)(2,1)S(1)}, u32[]{:S(2)}, u32[]{:S(2)}) %collective-permute-start.3) | collective-permute-done | bytes 131104 | tf_op jit(solution)/shard_map/ppermute | solution.py:407
  23.0 1.8 %collective-permute-start.7 = (bf16[32,2048]{1,0:T(8,128)(2,1)S(1)}, bf16[32,2048]{1,0:T(8,128)(2,1)S(1)}, u32[]{:S(2)}, u32[]{:S(2)}) collective-permute-start(bf16[32,2048]{1,0:T(8,128)(2,1)S(1)} %collective-permute-done.3.refs_7_), channel_id=1, source_target_pairs={{0,4},{4,0},{8,12},{12,8},{1,5},{5,1},{9,13},{13,9},{2,6},{6,2},{1... | collective-permute-start | bytes 393224 | tf_op jit(solution)/shard_map/ppermute | solution.py:407
  24.9 2.8 %rest_first.1 = (bf16[128,32,128]{2,1,0:T(8,128)(2,1)}, bf16[32,256]{1,0:T(8,128)(2,1)S(1)}, bf16[32,512]{1,0:T(8,128)(2,1)S(1)}) custom-call(s32[2,1,2048]{2,1,0:T(1,128)S(1)} %get-tuple-element.19.refs_0_, f32[2048,256]{1,0:T(8,128)S(1)} %get-tuple-element.20.refs_1_, f32[2048,256]{1,0:T(8,128)S(1)} %mix_part.1.refs_2_, ...), custom_call_target="tpu_custom_call" | custom-call | flops 1610612736 | bytes 4194304 | tf_op jit(solution)/shard_map/rest_first/pallas_call | solution.py:369
  27.7 0.0 collective-permute-done.6.refs_6_
  27.7 0.4 %collective-permute-done.7.refs_7_ = bf16[32,2048]{1,0:T(8,128)(2,1)S(1)} collective-permute-done((bf16[32,2048]{1,0:T(8,128)(2,1)S(1)}, bf16[32,2048]{1,0:T(8,128)(2,1)S(1)}, u32[]{:S(2)}, u32[]{:S(2)}) %collective-permute-start.7) | collective-permute-done | bytes 131104 | tf_op jit(solution)/shard_map/ppermute | solution.py:407
  28.1 3.1 %rest_second.1 = bf16[128,32,128]{2,1,0:T(8,128)(2,1)} custom-call(s32[2,1,2048]{2,1,0:T(1,128)S(1)} %get-tuple-element.19.refs_0_, f32[2048,256]{1,0:T(8,128)S(1)} %get-tuple-element.20.refs_1_, f32[2048,256]{1,0:T(8,128)S(1)} %mix_part.1.refs_2_, bf16[128,32,128]{2,1,0:T(8,128)(2,1)S(1)} %get-tuple-element.26.refs_3_, ...), custom_call_target="tpu_custom_call", output_to_operand_aliasing={{}: (10, {})} | custom-call | flops 1660944384 | bytes 4194304 | tf_op jit(solution)/shard_map/rest_second/pallas_call | solution.py:369
  (4 shorter events, 0.0 us)
Async XLA Ops:
  0.0 21.2 %copy-start.1 = (bf16[32,128]{1,0:T(8,128)(2,1)S(1)}, bf16[32,128]{1,0:T(8,128)(2,1)}, u32[]{:S(2)}) copy-start(bf16[32,128]{1,0:T(8,128)(2,1)} %out_ref.1) | copy-start | bytes 24580
  0.0 21.2 %copy-start = (bf16[3,32,32]{2,1,0:T(8,128)(2,1)S(1)}, bf16[3,32,32]{2,1,0:T(8,128)(2,1)}, u32[]{:S(2)}) copy-start(bf16[3,32,32]{2,1,0:T(8,128)(2,1)} %mix_ref.1) | copy-start | bytes 18436
  1.0 7.4 %collective-permute-start.1 = (bf16[32,2048]{1,0:T(8,128)(2,1)S(1)}, bf16[32,2048]{1,0:T(8,128)(2,1)S(1)}, u32[]{:S(2)}, u32[]{:S(2)}) collective-permute-start(bf16[32,2048]{1,0:T(8,128)(2,1)S(1)} %get-tuple-element.36), channel_id=1, source_target_pairs={{0,4},{4,0},{8,12},{12,8},{1,5},{5,1},{9,13},{13,9},{2,6},{6,2},{1... | collective-permute-start | bytes 393224 | tf_op jit(solution)/shard_map/ppermute | solution.py:407
  4.1 9.0 %collective-permute-start = (bf16[32,2048]{1,0:T(8,128)(2,1)S(1)}, bf16[32,2048]{1,0:T(8,128)(2,1)S(1)}, u32[]{:S(2)}, u32[]{:S(2)}) collective-permute-start(bf16[32,2048]{1,0:T(8,128)(2,1)S(1)} %get-tuple-element.35), channel_id=1, source_target_pairs={{0,4},{4,0},{8,12},{12,8},{1,5},{5,1},{9,13},{13,9},{2,6},{6,2},{1... | collective-permute-start | bytes 393224 | tf_op jit(solution)/shard_map/ppermute | solution.py:407
  8.4 7.2 %collective-permute-start.2 = (bf16[32,2048]{1,0:T(8,128)(2,1)S(1)}, bf16[32,2048]{1,0:T(8,128)(2,1)S(1)}, u32[]{:S(2)}, u32[]{:S(2)}) collective-permute-start(bf16[32,2048]{1,0:T(8,128)(2,1)S(1)} %slice_select_fusion), channel_id=1, source_target_pairs={{0,12},{4,8},{8,4},{12,0},{1,13},{5,9},{9,5},{13,1},{2,14},{6,10},... | collective-permute-start | bytes 393224 | tf_op jit(solution)/shard_map/ppermute | solution.py:407
  12.6 7.4 %collective-permute-start.5 = (bf16[1024,128]{1,0:T(8,128)(2,1)S(1)}, bf16[1024,128]{1,0:T(8,128)(2,1)S(1)}, u32[]{:S(2)}, u32[]{:S(2)}) collective-permute-start(bf16[1024,128]{1,0:T(8,128)(2,1)S(1)} %get-tuple-element.24.self_ref), channel_id=1, source_target_pairs={{0,3},{1,0},{2,1},{3,2},{4,7},{5,4},{6,5},{7,6},{8,11},{9,8},{10,9... | collective-permute-start | bytes 786440 | tf_op jit(solution)/shard_map/ppermute | solution.py:402
  12.6 8.6 %collective-permute-start.4 = (bf16[1024,128]{1,0:T(8,128)(2,1)S(1)}, bf16[1024,128]{1,0:T(8,128)(2,1)S(1)}, u32[]{:S(2)}, u32[]{:S(2)}) collective-permute-start(bf16[1024,128]{1,0:T(8,128)(2,1)S(1)} %get-tuple-element.24.self_ref), channel_id=1, source_target_pairs={{0,1},{1,2},{2,3},{3,0},{4,5},{5,6},{6,7},{7,4},{8,9},{9,10},{10,1... | collective-permute-start | bytes 786440 | tf_op jit(solution)/shard_map/ppermute | solution.py:402
  15.6 7.4 %collective-permute-start.3 = (bf16[32,2048]{1,0:T(8,128)(2,1)S(1)}, bf16[32,2048]{1,0:T(8,128)(2,1)S(1)}, u32[]{:S(2)}, u32[]{:S(2)}) collective-permute-start(bf16[32,2048]{1,0:T(8,128)(2,1)S(1)} %select_select_fusion.refs_6_), channel_id=1, source_target_pairs={{0,12},{4,8},{8,4},{12,0},{1,13},{5,9},{9,5},{13,1},{2,14},{6,10},... | collective-permute-start | bytes 393224 | tf_op jit(solution)/shard_map/ppermute | solution.py:407
  19.5 8.2 %collective-permute-start.6 = (bf16[32,2048]{1,0:T(8,128)(2,1)S(1)}, bf16[32,2048]{1,0:T(8,128)(2,1)S(1)}, u32[]{:S(2)}, u32[]{:S(2)}) collective-permute-start(bf16[32,2048]{1,0:T(8,128)(2,1)S(1)} %select_select_fusion.refs_6_), channel_id=1, source_target_pairs={{0,4},{4,0},{8,12},{12,8},{1,5},{5,1},{9,13},{13,9},{2,6},{6,2},{1... | collective-permute-start | bytes 393224 | tf_op jit(solution)/shard_map/ppermute | solution.py:407
  23.0 5.1 %collective-permute-start.7 = (bf16[32,2048]{1,0:T(8,128)(2,1)S(1)}, bf16[32,2048]{1,0:T(8,128)(2,1)S(1)}, u32[]{:S(2)}, u32[]{:S(2)}) collective-permute-start(bf16[32,2048]{1,0:T(8,128)(2,1)S(1)} %collective-permute-done.3.refs_7_), channel_id=1, source_target_pairs={{0,4},{4,0},{8,12},{12,8},{1,5},{5,1},{9,13},{13,9},{2,6},{6,2},{1... | collective-permute-start | bytes 393224 | tf_op jit(solution)/shard_map/ppermute | solution.py:407

commit v8 on v7

--- a/solution.py
+++ b/solution.py
@@ -271,8 +271,8 @@
 
 def rest_kernel(second, side_of, place, flags_ref, acc_ref, lifted_ref, *refs):
     x_ref, w_second_ref, w_glob_ref, *refs = refs
-    middle, refs = refs[:-8], refs[-8:]
-    out_ref, glob_cells, glob_taps, odd, even, taps, cells, sems = refs
+    middle, refs = refs[:-6], refs[-6:]
+    out_ref, glob_cells, glob_taps, taps, cells, sems = refs
     if second:
         *pieces, glob_edge, taps_edge, _, out_hbm = middle
     else:
@@ -315,18 +315,15 @@
         taps[pl.ds(at((half + 2) * side), 2 * pairs), :] = taps_edge[...]
     for low, count in row_parts(act_rows, pairs):
         size = count * pairs
-        start = EDGE + low * pairs
         left, right = column_masks(size, out, pairs)
         value = acc_ref[pl.ds(at(act_first + low), size), :] + pair_taps(
             glob_taps, w_glob_ref, at(act_place + low - 1), size, pairs
         )
         value = silu(value)
-        even[pl.ds(start, size), :] = value[:, :out]
-        odd[pl.ds(start, size), :] = value[:, out:]
         part = pl.ds(at(act_place + low), size)
         taps[part, pl.ds(out, 2 * out)] = value.astype(BF16)
-        before = jnp.where(left, 0.0, odd[pl.ds(start - 1, size), :])
-        after = jnp.where(right, 0.0, even[pl.ds(start + 1, size), :])
+        before = jnp.where(left, 0.0, pltpu.roll(value[:, out:], 1, 0))
+        after = jnp.where(right, 0.0, pltpu.roll(value[:, :out], size - 1, 0))
         taps[part, pl.ds(0, out)] = before.astype(BF16)
         taps[part, pl.ds(3 * out, out)] = after.astype(BF16)
     if not second:
@@ -377,8 +374,6 @@
             pltpu.VMEM((rows, width, channels), BF16),
             pltpu.VMEM(((half + 1) * pairs + 2 * EDGE, lanes), F32),
             pltpu.VMEM(((rows + 2) * pairs, 2 * lanes), BF16),
-            pltpu.VMEM(((half + 1) * pairs + 2 * EDGE, channels), F32),
-            pltpu.VMEM(((half + 1) * pairs + 2 * EDGE, channels), F32),
             pltpu.VMEM(((rows + 2) * pairs, 4 * channels), BF16),
             pltpu.VMEM((rows * width + EDGE, channels), F32),
             pltpu.SemaphoreType.DMA((2 * len(row_parts(rows, pairs)),)),

time: 31.4 us -> 31.3 us (level)
  no operation moved by 1% of the time
where the time goes in v8:
time: 31.3 us; the launch traced here: 31.2 us
  starting transfers between devices  14.1 us (45%)
  Pallas kernels  11.2 us (36%)
  waiting for transfers between devices  4.72 us (15%)
  local copies, waits for them, and re-layouts  1.01 us (3%)
    ppermute x6, starting transfers between devices, swapped(): return lax.ppermute(block, 'patch', [(i, i ^ bit) for i in range(count)])  13.6 us
    pallas_call x2, Pallas kernels, rest_part(): pl.pallas_call(lambda *refs: rest_kernel(second, side_of, place, *refs),...  5.84 us
    pallas_call x1, Pallas kernels, resident_part(): pl.pallas_call(resident_kernel, out_shape=tuple((space(*kind) for space,...  4.07 us
    ppermute x6, waiting for transfers between devices, swapped(): return lax.ppermute(block, 'patch', [(i, i ^ bit) for i in range(count)])  3.6 us
    pallas_call x1, Pallas kernels, mix_part(): pl.pallas_call(mix_kernel, out_shape=pltpu.VMEM((2 * own.shape[0], 2 * ou...  1.33 us
    ppermute x2, waiting for transfers between devices, rotated(): lax.ppermute(block, axis, [(i, (i + distance) % count) for i in range(cou...  1.13 us
    slice x1, local copies, waits for them, and re-layouts, per_device(): staying = swapped(block[half:half + share], 1)  1 us
  transfers between devices with their start and end apart: 8, of which 5 were waited for; matrix products, arithmetic and copies ran while one was open for 0% of the time, Pallas kernels for 26%

profile of v8, /device:TPU:0, one launch (start us, length us, event | category | flops | bytes accessed | tf_op | source)
XLA Modules:
  0.0 31.2 jit_solution(9329633221509309398)
XLA Ops:
  0.0 1.0 %slice_bitcast_fusion.1 = (bf16[32,2048]{1,0:T(8,128)(2,1)S(1)}, bf16[32,2048]{1,0:T(8,128)(2,1)S(1)}) fusion(bf16[1,1,128,2048]{3,2,1,0:T(8,128)(2,1)} %param.10), kind=kLoop, calls=%fused_computation.3 | loop fusion | bytes 524288 | tf_op jit(solution)/shard_map/slice | solution.py:440
  1.0 3.1 %collective-permute-start.1 = (bf16[32,2048]{1,0:T(8,128)(2,1)S(1)}, bf16[32,2048]{1,0:T(8,128)(2,1)S(1)}, u32[]{:S(2)}, u32[]{:S(2)}) collective-permute-start(bf16[32,2048]{1,0:T(8,128)(2,1)S(1)} %get-tuple-element.36), channel_id=1, source_target_pairs={{0,4},{4,0},{8,12},{12,8},{1,5},{5,1},{9,13},{13,9},{2,6},{6,2},{1... | collective-permute-start | bytes 393224 | tf_op jit(solution)/shard_map/ppermute | solution.py:402
  4.1 0.1 collective-permute-start
  4.2 4.1 %resident_part.1 = (f32[2048,256]{1,0:T(8,128)S(1)}, bf16[1024,128]{1,0:T(8,128)(2,1)S(1)}, s32[2,1,2048]{2,1,0:T(1,128)S(1)}, bf16[64,2048]{1,0:T(8,128)(2,1)S(...) custom-call(s32[4]{0:T(128)} %owner_hbm.1, ...), custom_call_target="tpu_custom_call" | custom-call | flops 1024 | bytes 1024 | tf_op jit(solution)/shard_map/resident_part/pallas_call | solution.py:179
  8.3 0.1 compare_reduce_fusion.1
  8.3 0.1 collective-permute-done.1
  8.4 4.1 %collective-permute-start.2 = (bf16[32,2048]{1,0:T(8,128)(2,1)S(1)}, bf16[32,2048]{1,0:T(8,128)(2,1)S(1)}, u32[]{:S(2)}, u32[]{:S(2)}) collective-permute-start(bf16[32,2048]{1,0:T(8,128)(2,1)S(1)} %slice_select_fusion), channel_id=1, source_target_pairs={{0,12},{4,8},{8,4},{12,0},{1,13},{5,9},{9,5},{13,1},{2,14},{6,10},... | collective-permute-start | bytes 393224 | tf_op jit(solution)/shard_map/ppermute | solution.py:402
  12.6 0.0 collective-permute-start.5
  12.6 0.5 %collective-permute-start.4 = (bf16[1024,128]{1,0:T(8,128)(2,1)S(1)}, bf16[1024,128]{1,0:T(8,128)(2,1)S(1)}, u32[]{:S(2)}, u32[]{:S(2)}) collective-permute-start(bf16[1024,128]{1,0:T(8,128)(2,1)S(1)} %get-tuple-element.24.self_ref), channel_id=1, source_target_pairs={{0,1},{1,2},{2,3},{3,0},{4,5},{5,6},{6,7},{7,4},{8,9},{9,10},{10,1... | collective-permute-start | bytes 786440 | tf_op jit(solution)/shard_map/ppermute | solution.py:397
  13.1 0.0 collective-permute-done
  13.1 2.5 %collective-permute-done.2 = bf16[32,2048]{1,0:T(8,128)(2,1)S(1)} collective-permute-done((bf16[32,2048]{1,0:T(8,128)(2,1)S(1)}, bf16[32,2048]{1,0:T(8,128)(2,1)S(1)}, u32[]{:S(2)}, u32[]{:S(2)}) %collective-permute-start.2) | collective-permute-done | bytes 131104 | tf_op jit(solution)/shard_map/ppermute | solution.py:402
  15.6 3.9 %collective-permute-start.3 = (bf16[32,2048]{1,0:T(8,128)(2,1)S(1)}, bf16[32,2048]{1,0:T(8,128)(2,1)S(1)}, u32[]{:S(2)}, u32[]{:S(2)}) collective-permute-start(bf16[32,2048]{1,0:T(8,128)(2,1)S(1)} %select_select_fusion.refs_6_), channel_id=1, source_target_pairs={{0,12},{4,8},{8,4},{12,0},{1,13},{5,9},{9,5},{13,1},{2,14},{6,10},... | collective-permute-start | bytes 393224 | tf_op jit(solution)/shard_map/ppermute | solution.py:402
  19.5 0.5 %collective-permute-start.6 = (bf16[32,2048]{1,0:T(8,128)(2,1)S(1)}, bf16[32,2048]{1,0:T(8,128)(2,1)S(1)}, u32[]{:S(2)}, u32[]{:S(2)}) collective-permute-start(bf16[32,2048]{1,0:T(8,128)(2,1)S(1)} %select_select_fusion.refs_6_), channel_id=1, source_target_pairs={{0,4},{4,0},{8,12},{12,8},{1,5},{5,1},{9,13},{13,9},{2,6},{6,2},{1... | collective-permute-start | bytes 393224 | tf_op jit(solution)/shard_map/ppermute | solution.py:402
  20.0 0.0 collective-permute-done.5.next_ref
  20.0 1.1 %collective-permute-done.4.prev_ref = bf16[1024,128]{1,0:T(8,128)(2,1)S(1)} collective-permute-done((bf16[1024,128]{1,0:T(8,128)(2,1)S(1)}, bf16[1024,128]{1,0:T(8,128)(2,1)S(1)}, u32[]{:S(2)}, u32[]{:S(2)}) %collective-permute-start.4) | collective-permute-done | bytes 262176 | tf_op jit(solution)/shard_map/ppermute | solution.py:397
  21.2 0.0 copy-done.1
  21.2 0.0 copy-done
  21.2 1.3 %mix_part.1.refs_2_ = f32[2048,256]{1,0:T(8,128)S(1)} custom-call(s32[4]{0:T(128)} %hours_hbm.1, bf16[1024,128]{1,0:T(8,128)(2,1)S(1)} %collective-permute-done.4.prev_ref, bf16[1024,128]{1,0:T(8,128)(2,1)S(1)} %get-tuple-element.24.self_ref, bf16[1024,128]{1,0:T(8,128)(2,1)S(1)} %collective-permute-done.5.next_ref, bf16[3,32,32]{2,1,0:T(8,128)(2,1)S(1)} %copy-done, ...), custom_call_target="tpu_custom_call" | custom-call | flops 100663296 | bytes 1048576 | tf_op jit(solution)/shard_map/mix_part/pallas_call | solution.py:246
  22.5 0.5 %collective-permute-done.3.refs_7_ = bf16[32,2048]{1,0:T(8,128)(2,1)S(1)} collective-permute-done((bf16[32,2048]{1,0:T(8,128)(2,1)S(1)}, bf16[32,2048]{1,0:T(8,128)(2,1)S(1)}, u32[]{:S(2)}, u32[]{:S(2)}) %collective-permute-start.3) | collective-permute-done | bytes 131104 | tf_op jit(solution)/shard_map/ppermute | solution.py:402
  23.0 1.8 %collective-permute-start.7 = (bf16[32,2048]{1,0:T(8,128)(2,1)S(1)}, bf16[32,2048]{1,0:T(8,128)(2,1)S(1)}, u32[]{:S(2)}, u32[]{:S(2)}) collective-permute-start(bf16[32,2048]{1,0:T(8,128)(2,1)S(1)} %collective-permute-done.3.refs_7_), channel_id=1, source_target_pairs={{0,4},{4,0},{8,12},{12,8},{1,5},{5,1},{9,13},{13,9},{2,6},{6,2},{1... | collective-permute-start | bytes 393224 | tf_op jit(solution)/shard_map/ppermute | solution.py:402
  24.9 2.8 %rest_first.1 = (bf16[128,32,128]{2,1,0:T(8,128)(2,1)}, bf16[32,256]{1,0:T(8,128)(2,1)S(1)}, bf16[32,512]{1,0:T(8,128)(2,1)S(1)}) custom-call(s32[2,1,2048]{2,1,0:T(1,128)S(1)} %get-tuple-element.19.refs_0_, f32[2048,256]{1,0:T(8,128)S(1)} %get-tuple-element.20.refs_1_, f32[2048,256]{1,0:T(8,128)S(1)} %mix_part.1.refs_2_, ...), custom_call_target="tpu_custom_call" | custom-call | flops 1610612736 | bytes 4194304 | tf_op jit(solution)/shard_map/rest_first/pallas_call | solution.py:366
  27.7 0.0 collective-permute-done.6.refs_6_
  27.7 0.4 %collective-permute-done.7.refs_7_ = bf16[32,2048]{1,0:T(8,128)(2,1)S(1)} collective-permute-done((bf16[32,2048]{1,0:T(8,128)(2,1)S(1)}, bf16[32,2048]{1,0:T(8,128)(2,1)S(1)}, u32[]{:S(2)}, u32[]{:S(2)}) %collective-permute-start.7) | collective-permute-done | bytes 131104 | tf_op jit(solution)/shard_map/ppermute | solution.py:402
  28.1 3.0 %rest_second.1 = bf16[128,32,128]{2,1,0:T(8,128)(2,1)} custom-call(s32[2,1,2048]{2,1,0:T(1,128)S(1)} %get-tuple-element.19.refs_0_, f32[2048,256]{1,0:T(8,128)S(1)} %get-tuple-element.20.refs_1_, f32[2048,256]{1,0:T(8,128)S(1)} %mix_part.1.refs_2_, bf16[128,32,128]{2,1,0:T(8,128)(2,1)S(1)} %get-tuple-element.26.refs_3_, ...), custom_call_target="tpu_custom_call", output_to_operand_aliasing={{}: (10, {})} | custom-call | flops 1660944384 | bytes 4194304 | tf_op jit(solution)/shard_map/rest_second/pallas_call | solution.py:366
  (4 shorter events, 0.0 us)
Async XLA Ops:
  0.0 21.2 %copy-start.1 = (bf16[32,128]{1,0:T(8,128)(2,1)S(1)}, bf16[32,128]{1,0:T(8,128)(2,1)}, u32[]{:S(2)}) copy-start(bf16[32,128]{1,0:T(8,128)(2,1)} %out_ref.1) | copy-start | bytes 24580
  0.0 21.2 %copy-start = (bf16[3,32,32]{2,1,0:T(8,128)(2,1)S(1)}, bf16[3,32,32]{2,1,0:T(8,128)(2,1)}, u32[]{:S(2)}) copy-start(bf16[3,32,32]{2,1,0:T(8,128)(2,1)} %mix_ref.1) | copy-start | bytes 18436
  1.0 7.4 %collective-permute-start.1 = (bf16[32,2048]{1,0:T(8,128)(2,1)S(1)}, bf16[32,2048]{1,0:T(8,128)(2,1)S(1)}, u32[]{:S(2)}, u32[]{:S(2)}) collective-permute-start(bf16[32,2048]{1,0:T(8,128)(2,1)S(1)} %get-tuple-element.36), channel_id=1, source_target_pairs={{0,4},{4,0},{8,12},{12,8},{1,5},{5,1},{9,13},{13,9},{2,6},{6,2},{1... | collective-permute-start | bytes 393224 | tf_op jit(solution)/shard_map/ppermute | solution.py:402
  4.1 9.0 %collective-permute-start = (bf16[32,2048]{1,0:T(8,128)(2,1)S(1)}, bf16[32,2048]{1,0:T(8,128)(2,1)S(1)}, u32[]{:S(2)}, u32[]{:S(2)}) collective-permute-start(bf16[32,2048]{1,0:T(8,128)(2,1)S(1)} %get-tuple-element.35), channel_id=1, source_target_pairs={{0,4},{4,0},{8,12},{12,8},{1,5},{5,1},{9,13},{13,9},{2,6},{6,2},{1... | collective-permute-start | bytes 393224 | tf_op jit(solution)/shard_map/ppermute | solution.py:402
  8.4 7.2 %collective-permute-start.2 = (bf16[32,2048]{1,0:T(8,128)(2,1)S(1)}, bf16[32,2048]{1,0:T(8,128)(2,1)S(1)}, u32[]{:S(2)}, u32[]{:S(2)}) collective-permute-start(bf16[32,2048]{1,0:T(8,128)(2,1)S(1)} %slice_select_fusion), channel_id=1, source_target_pairs={{0,12},{4,8},{8,4},{12,0},{1,13},{5,9},{9,5},{13,1},{2,14},{6,10},... | collective-permute-start | bytes 393224 | tf_op jit(solution)/shard_map/ppermute | solution.py:402
  12.6 7.4 %collective-permute-start.5 = (bf16[1024,128]{1,0:T(8,128)(2,1)S(1)}, bf16[1024,128]{1,0:T(8,128)(2,1)S(1)}, u32[]{:S(2)}, u32[]{:S(2)}) collective-permute-start(bf16[1024,128]{1,0:T(8,128)(2,1)S(1)} %get-tuple-element.24.self_ref), channel_id=1, source_target_pairs={{0,3},{1,0},{2,1},{3,2},{4,7},{5,4},{6,5},{7,6},{8,11},{9,8},{10,9... | collective-permute-start | bytes 786440 | tf_op jit(solution)/shard_map/ppermute | solution.py:397
  12.6 8.6 %collective-permute-start.4 = (bf16[1024,128]{1,0:T(8,128)(2,1)S(1)}, bf16[1024,128]{1,0:T(8,128)(2,1)S(1)}, u32[]{:S(2)}, u32[]{:S(2)}) collective-permute-start(bf16[1024,128]{1,0:T(8,128)(2,1)S(1)} %get-tuple-element.24.self_ref), channel_id=1, source_target_pairs={{0,1},{1,2},{2,3},{3,0},{4,5},{5,6},{6,7},{7,4},{8,9},{9,10},{10,1... | collective-permute-start | bytes 786440 | tf_op jit(solution)/shard_map/ppermute | solution.py:397
  15.6 7.4 %collective-permute-start.3 = (bf16[32,2048]{1,0:T(8,128)(2,1)S(1)}, bf16[32,2048]{1,0:T(8,128)(2,1)S(1)}, u32[]{:S(2)}, u32[]{:S(2)}) collective-permute-start(bf16[32,2048]{1,0:T(8,128)(2,1)S(1)} %select_select_fusion.refs_6_), channel_id=1, source_target_pairs={{0,12},{4,8},{8,4},{12,0},{1,13},{5,9},{9,5},{13,1},{2,14},{6,10},... | collective-permute-start | bytes 393224 | tf_op jit(solution)/shard_map/ppermute | solution.py:402
  19.5 8.2 %collective-permute-start.6 = (bf16[32,2048]{1,0:T(8,128)(2,1)S(1)}, bf16[32,2048]{1,0:T(8,128)(2,1)S(1)}, u32[]{:S(2)}, u32[]{:S(2)}) collective-permute-start(bf16[32,2048]{1,0:T(8,128)(2,1)S(1)} %select_select_fusion.refs_6_), channel_id=1, source_target_pairs={{0,4},{4,0},{8,12},{12,8},{1,5},{5,1},{9,13},{13,9},{2,6},{6,2},{1... | collective-permute-start | bytes 393224 | tf_op jit(solution)/shard_map/ppermute | solution.py:402
  23.0 5.1 %collective-permute-start.7 = (bf16[32,2048]{1,0:T(8,128)(2,1)S(1)}, bf16[32,2048]{1,0:T(8,128)(2,1)S(1)}, u32[]{:S(2)}, u32[]{:S(2)}) collective-permute-start(bf16[32,2048]{1,0:T(8,128)(2,1)S(1)} %collective-permute-done.3.refs_7_), channel_id=1, source_target_pairs={{0,4},{4,0},{8,12},{12,8},{1,5},{5,1},{9,13},{13,9},{2,6},{6,2},{1... | collective-permute-start | bytes 393224 | tf_op jit(solution)/shard_map/ppermute | solution.py:402

commit v9 on v8

--- a/solution.py
+++ b/solution.py
@@ -444,7 +444,6 @@
     own = jnp.where(beside, staying, swapped(passing, 3))
     across = swapped(own, 3)
     lifted = lifted_with(proj)
-    across, lifted = lax.optimization_barrier((across, lifted))
     upper = [own, across]
     lower = [swapped(own, 1), swapped(across, 1)]
     result, *edges = rest(False, side_first, place_first, lifted, upper, [])

time: 31.3 us -> 32.3 us (1.032)
  waiting for transfers between devices: 4.72 us -> 5.63 us
    ppermute x6, waiting for transfers between devices: 3.6 us -> 5.62 us  [swapped(): return lax.ppermute(block, 'patch', [(i, i ^ bit) for i in range(count)])]
    ppermute x2, waiting for transfers between devices: 1.13 us -> 0.01 us  [rotated(): lax.ppermute(block, axis, [(i, (i + distance) % count) for i in range(cou...]
  transfers between devices with their start and end apart: 8 -> 8, of which waited for: 5 -> 3; matrix products, arithmetic and copies ran while one was open for 0% -> 0% of each run, Pallas kernels for 26% -> 26%
where the time goes in v9:
time: 32.3 us; the launch traced here: 32.1 us
  starting transfers between devices  14.1 us (44%)
  Pallas kernels  11.3 us (35%)
  waiting for transfers between devices  5.63 us (17%)
  local copies, waits for them, and re-layouts  1.01 us (3%)
    ppermute x6, starting transfers between devices, swapped(): return lax.ppermute(block, 'patch', [(i, i ^ bit) for i in range(count)])  13.6 us
    pallas_call x2, Pallas kernels, rest_part(): pl.pallas_call(lambda *refs: rest_kernel(second, side_of, place, *refs),...  5.87 us
    ppermute x6, waiting for transfers between devices, swapped(): return lax.ppermute(block, 'patch', [(i, i ^ bit) for i in range(count)])  5.62 us
    pallas_call x1, Pallas kernels, resident_part(): pl.pallas_call(resident_kernel, out_shape=tuple((space(*kind) for space,...  4.07 us
    pallas_call x1, Pallas kernels, mix_part(): pl.pallas_call(mix_kernel, out_shape=pltpu.VMEM((2 * own.shape[0], 2 * ou...  1.33 us
    slice x1, local copies, waits for them, and re-layouts, per_device(): staying = swapped(block[half:half + share], 1)  1 us
  transfers between devices with their start and end apart: 8, of which 3 were waited for; matrix products, arithmetic and copies ran while one was open for 0% of the time, Pallas kernels for 26%

profile of v9, /device:TPU:0, one launch (start us, length us, event | category | flops | bytes accessed | tf_op | source)
XLA Modules:
  0.0 32.1 jit_solution(17080933344532412035)
XLA Ops:
  0.0 1.0 %slice_bitcast_fusion = (bf16[32,2048]{1,0:T(8,128)(2,1)S(1)}, bf16[32,2048]{1,0:T(8,128)(2,1)S(1)}) fusion(bf16[1,1,128,2048]{3,2,1,0:T(8,128)(2,1)} %param.10), kind=kLoop, calls=%fused_computation.2 | loop fusion | bytes 524288 | tf_op jit(solution)/shard_map/slice | solution.py:440
  1.0 3.1 %collective-permute-start = (bf16[32,2048]{1,0:T(8,128)(2,1)S(1)}, bf16[32,2048]{1,0:T(8,128)(2,1)S(1)}, u32[]{:S(2)}, u32[]{:S(2)}) collective-permute-start(bf16[32,2048]{1,0:T(8,128)(2,1)S(1)} %get-tuple-element.32), channel_id=1, source_target_pairs={{0,4},{4,0},{8,12},{12,8},{1,5},{5,1},{9,13},{13,9},{2,6},{6,2},{1... | collective-permute-start | bytes 393224 | tf_op jit(solution)/shard_map/ppermute | solution.py:402
  4.1 0.1 collective-permute-start.3
  4.2 4.1 %resident_part.1 = (f32[2048,256]{1,0:T(8,128)S(1)}, bf16[1024,128]{1,0:T(8,128)(2,1)S(1)}, s32[2,1,2048]{2,1,0:T(1,128)S(1)}, bf16[64,2048]{1,0:T(8,128)(2,1)S(...) custom-call(s32[4]{0:T(128)} %owner_hbm.1, ...), custom_call_target="tpu_custom_call" | custom-call | flops 1024 | bytes 1024 | tf_op jit(solution)/shard_map/resident_part/pallas_call | solution.py:179
  8.3 0.1 compare_reduce_fusion.1
  8.3 0.1 collective-permute-done
  8.4 4.1 %collective-permute-start.4 = (bf16[32,2048]{1,0:T(8,128)(2,1)S(1)}, bf16[32,2048]{1,0:T(8,128)(2,1)S(1)}, u32[]{:S(2)}, u32[]{:S(2)}) collective-permute-start(bf16[32,2048]{1,0:T(8,128)(2,1)S(1)} %slice_select_fusion), channel_id=1, source_target_pairs={{0,12},{4,8},{8,4},{12,0},{1,13},{5,9},{9,5},{13,1},{2,14},{6,10},... | collective-permute-start | bytes 393224 | tf_op jit(solution)/shard_map/ppermute | solution.py:402
  12.6 0.0 collective-permute-start.2
  12.6 0.5 %collective-permute-start.1 = (bf16[1024,128]{1,0:T(8,128)(2,1)S(1)}, bf16[1024,128]{1,0:T(8,128)(2,1)S(1)}, u32[]{:S(2)}, u32[]{:S(2)}) collective-permute-start(bf16[1024,128]{1,0:T(8,128)(2,1)S(1)} %get-tuple-element.20.self_ref), channel_id=1, source_target_pairs={{0,1},{1,2},{2,3},{3,0},{4,5},{5,6},{6,7},{7,4},{8,9},{9,10},{10,1... | collective-permute-start | bytes 786440 | tf_op jit(solution)/shard_map/ppermute | solution.py:397
  13.1 0.0 collective-permute-done.3
  13.1 2.5 %collective-permute-done.4 = bf16[32,2048]{1,0:T(8,128)(2,1)S(1)} collective-permute-done((bf16[32,2048]{1,0:T(8,128)(2,1)S(1)}, bf16[32,2048]{1,0:T(8,128)(2,1)S(1)}, u32[]{:S(2)}, u32[]{:S(2)}) %collective-permute-start.4) | collective-permute-done | bytes 131104 | tf_op jit(solution)/shard_map/ppermute | solution.py:402
  15.6 3.9 %collective-permute-start.6 = (bf16[32,2048]{1,0:T(8,128)(2,1)S(1)}, bf16[32,2048]{1,0:T(8,128)(2,1)S(1)}, u32[]{:S(2)}, u32[]{:S(2)}) collective-permute-start(bf16[32,2048]{1,0:T(8,128)(2,1)S(1)} %select_select_fusion.refs_6_), channel_id=1, source_target_pairs={{0,12},{4,8},{8,4},{12,0},{1,13},{5,9},{9,5},{13,1},{2,14},{6,10},... | collective-permute-start | bytes 393224 | tf_op jit(solution)/shard_map/ppermute | solution.py:402
  19.5 0.5 %collective-permute-start.5 = (bf16[32,2048]{1,0:T(8,128)(2,1)S(1)}, bf16[32,2048]{1,0:T(8,128)(2,1)S(1)}, u32[]{:S(2)}, u32[]{:S(2)}) collective-permute-start(bf16[32,2048]{1,0:T(8,128)(2,1)S(1)} %select_select_fusion.refs_6_), channel_id=1, source_target_pairs={{0,4},{4,0},{8,12},{12,8},{1,5},{5,1},{9,13},{13,9},{2,6},{6,2},{1... | collective-permute-start | bytes 393224 | tf_op jit(solution)/shard_map/ppermute | solution.py:402
  20.0 3.0 %collective-permute-done.6.refs_7_ = bf16[32,2048]{1,0:T(8,128)(2,1)S(1)} collective-permute-done((bf16[32,2048]{1,0:T(8,128)(2,1)S(1)}, bf16[32,2048]{1,0:T(8,128)(2,1)S(1)}, u32[]{:S(2)}, u32[]{:S(2)}) %collective-permute-start.6) | collective-permute-done | bytes 131104 | tf_op jit(solution)/shard_map/ppermute | solution.py:402
  23.0 1.8 %collective-permute-start.7 = (bf16[32,2048]{1,0:T(8,128)(2,1)S(1)}, bf16[32,2048]{1,0:T(8,128)(2,1)S(1)}, u32[]{:S(2)}, u32[]{:S(2)}) collective-permute-start(bf16[32,2048]{1,0:T(8,128)(2,1)S(1)} %collective-permute-done.6.refs_7_), channel_id=1, source_target_pairs={{0,4},{4,0},{8,12},{12,8},{1,5},{5,1},{9,13},{13,9},{2,6},{6,2},{1... | collective-permute-start | bytes 393224 | tf_op jit(solution)/shard_map/ppermute | solution.py:402
  24.9 0.0 collective-permute-done.2.next_ref
  24.9 0.0 collective-permute-done.1.prev_ref
  24.9 0.0 copy-done.1
  24.9 0.0 copy-done
  24.9 1.3 %mix_part.1.refs_2_ = f32[2048,256]{1,0:T(8,128)S(1)} custom-call(s32[4]{0:T(128)} %hours_hbm.1, bf16[1024,128]{1,0:T(8,128)(2,1)S(1)} %collective-permute-done.1.prev_ref, bf16[1024,128]{1,0:T(8,128)(2,1)S(1)} %get-tuple-element.20.self_ref, bf16[1024,128]{1,0:T(8,128)(2,1)S(1)} %collective-permute-done.2.next_ref, bf16[3,32,32]{2,1,0:T(8,128)(2,1)S(1)} %copy-done, ...), custom_call_target="tpu_custom_call" | custom-call | flops 100663296 | bytes 1048576 | tf_op jit(solution)/shard_map/mix_part/pallas_call | solution.py:246
  26.2 2.8 %rest_first.1 = (bf16[128,32,128]{2,1,0:T(8,128)(2,1)}, bf16[32,256]{1,0:T(8,128)(2,1)S(1)}, bf16[32,512]{1,0:T(8,128)(2,1)S(1)}) custom-call(s32[2,1,2048]{2,1,0:T(1,128)S(1)} %get-tuple-element.17.refs_0_, f32[2048,256]{1,0:T(8,128)S(1)} %get-tuple-element.18.refs_1_, f32[2048,256]{1,0:T(8,128)S(1)} %mix_part.1.refs_2_, ...), custom_call_target="tpu_custom_call" | custom-call | flops 1610612736 | bytes 4194304 | tf_op jit(solution)/shard_map/rest_first/pallas_call | solution.py:366
  29.1 0.0 collective-permute-done.5.refs_6_
  29.1 0.0 collective-permute-done.7.refs_7_
  29.1 3.1 %rest_second.1 = bf16[128,32,128]{2,1,0:T(8,128)(2,1)} custom-call(s32[2,1,2048]{2,1,0:T(1,128)S(1)} %get-tuple-element.17.refs_0_, f32[2048,256]{1,0:T(8,128)S(1)} %get-tuple-element.18.refs_1_, f32[2048,256]{1,0:T(8,128)S(1)} %mix_part.1.refs_2_, bf16[128,32,128]{2,1,0:T(8,128)(2,1)S(1)} %get-tuple-element.21.refs_3_, ...), custom_call_target="tpu_custom_call", output_to_operand_aliasing={{}: (10, {})} | custom-call | flops 1660944384 | bytes 4194304 | tf_op jit(solution)/shard_map/rest_second/pallas_call | solution.py:366
  (4 shorter events, 0.0 us)
Async XLA Ops:
  0.0 24.9 %copy-start.1 = (bf16[32,128]{1,0:T(8,128)(2,1)S(1)}, bf16[32,128]{1,0:T(8,128)(2,1)}, u32[]{:S(2)}) copy-start(bf16[32,128]{1,0:T(8,128)(2,1)} %out_ref.1) | copy-start | bytes 24580
  0.0 24.9 %copy-start = (bf16[3,32,32]{2,1,0:T(8,128)(2,1)S(1)}, bf16[3,32,32]{2,1,0:T(8,128)(2,1)}, u32[]{:S(2)}) copy-start(bf16[3,32,32]{2,1,0:T(8,128)(2,1)} %mix_ref.1) | copy-start | bytes 18436
  1.0 7.4 %collective-permute-start = (bf16[32,2048]{1,0:T(8,128)(2,1)S(1)}, bf16[32,2048]{1,0:T(8,128)(2,1)S(1)}, u32[]{:S(2)}, u32[]{:S(2)}) collective-permute-start(bf16[32,2048]{1,0:T(8,128)(2,1)S(1)} %get-tuple-element.32), channel_id=1, source_target_pairs={{0,4},{4,0},{8,12},{12,8},{1,5},{5,1},{9,13},{13,9},{2,6},{6,2},{1... | collective-permute-start | bytes 393224 | tf_op jit(solution)/shard_map/ppermute | solution.py:402
  4.1 9.0 %collective-permute-start.3 = (bf16[32,2048]{1,0:T(8,128)(2,1)S(1)}, bf16[32,2048]{1,0:T(8,128)(2,1)S(1)}, u32[]{:S(2)}, u32[]{:S(2)}) collective-permute-start(bf16[32,2048]{1,0:T(8,128)(2,1)S(1)} %get-tuple-element.31), channel_id=1, source_target_pairs={{0,4},{4,0},{8,12},{12,8},{1,5},{5,1},{9,13},{13,9},{2,6},{6,2},{1... | collective-permute-start | bytes 393224 | tf_op jit(solution)/shard_map/ppermute | solution.py:402
  8.4 7.2 %collective-permute-start.4 = (bf16[32,2048]{1,0:T(8,128)(2,1)S(1)}, bf16[32,2048]{1,0:T(8,128)(2,1)S(1)}, u32[]{:S(2)}, u32[]{:S(2)}) collective-permute-start(bf16[32,2048]{1,0:T(8,128)(2,1)S(1)} %slice_select_fusion), channel_id=1, source_target_pairs={{0,12},{4,8},{8,4},{12,0},{1,13},{5,9},{9,5},{13,1},{2,14},{6,10},... | collective-permute-start | bytes 393224 | tf_op jit(solution)/shard_map/ppermute | solution.py:402
  12.6 12.3 %collective-permute-start.2 = (bf16[1024,128]{1,0:T(8,128)(2,1)S(1)}, bf16[1024,128]{1,0:T(8,128)(2,1)S(1)}, u32[]{:S(2)}, u32[]{:S(2)}) collective-permute-start(bf16[1024,128]{1,0:T(8,128)(2,1)S(1)} %get-tuple-element.20.self_ref), channel_id=1, source_target_pairs={{0,3},{1,0},{2,1},{3,2},{4,7},{5,4},{6,5},{7,6},{8,11},{9,8},{10,9... | collective-permute-start | bytes 786440 | tf_op jit(solution)/shard_map/ppermute | solution.py:397
  12.6 12.3 %collective-permute-start.1 = (bf16[1024,128]{1,0:T(8,128)(2,1)S(1)}, bf16[1024,128]{1,0:T(8,128)(2,1)S(1)}, u32[]{:S(2)}, u32[]{:S(2)}) collective-permute-start(bf16[1024,128]{1,0:T(8,128)(2,1)S(1)} %get-tuple-element.20.self_ref), channel_id=1, source_target_pairs={{0,1},{1,2},{2,3},{3,0},{4,5},{5,6},{6,7},{7,4},{8,9},{9,10},{10,1... | collective-permute-start | bytes 786440 | tf_op jit(solution)/shard_map/ppermute | solution.py:397
  15.6 7.4 %collective-permute-start.6 = (bf16[32,2048]{1,0:T(8,128)(2,1)S(1)}, bf16[32,2048]{1,0:T(8,128)(2,1)S(1)}, u32[]{:S(2)}, u32[]{:S(2)}) collective-permute-start(bf16[32,2048]{1,0:T(8,128)(2,1)S(1)} %select_select_fusion.refs_6_), channel_id=1, source_target_pairs={{0,12},{4,8},{8,4},{12,0},{1,13},{5,9},{9,5},{13,1},{2,14},{6,10},... | collective-permute-start | bytes 393224 | tf_op jit(solution)/shard_map/ppermute | solution.py:402
  19.5 9.6 %collective-permute-start.5 = (bf16[32,2048]{1,0:T(8,128)(2,1)S(1)}, bf16[32,2048]{1,0:T(8,128)(2,1)S(1)}, u32[]{:S(2)}, u32[]{:S(2)}) collective-permute-start(bf16[32,2048]{1,0:T(8,128)(2,1)S(1)} %select_select_fusion.refs_6_), channel_id=1, source_target_pairs={{0,4},{4,0},{8,12},{12,8},{1,5},{5,1},{9,13},{13,9},{2,6},{6,2},{1... | collective-permute-start | bytes 393224 | tf_op jit(solution)/shard_map/ppermute | solution.py:402
  23.0 6.0 %collective-permute-start.7 = (bf16[32,2048]{1,0:T(8,128)(2,1)S(1)}, bf16[32,2048]{1,0:T(8,128)(2,1)S(1)}, u32[]{:S(2)}, u32[]{:S(2)}) collective-permute-start(bf16[32,2048]{1,0:T(8,128)(2,1)S(1)} %collective-permute-done.6.refs_7_), channel_id=1, source_target_pairs={{0,4},{4,0},{8,12},{12,8},{1,5},{5,1},{9,13},{13,9},{2,6},{6,2},{1... | collective-permute-start | bytes 393224 | tf_op jit(solution)/shard_map/ppermute | solution.py:402
